TPU v7x, 128 devices: a whole 4x4x4 slice. The times are simulated.
128 devices in a mesh: row: 8 (over y_hi, x), col: 16 (over y_lo, z, core).
Axes of the slice: x: 4, y: 4 (y_hi: 2, y_lo: 2; y = y_hi * 2 + y_lo), z: 4, core: 2. Of those that a mesh axis runs over, the one named last changes fastest.
Arguments:
- adj_tiles: bfloat16 [8, 16, 80, 256, 256], P('row', 'col'), may hold values from -0.0625 to 0.0625
- tile_rows: int32 [8, 16, 80], P('row', 'col'), may hold values from 0 to 15, as said below
- tile_cols: int32 [8, 16, 80], P('row', 'col'), may hold values from 0 to 7
- tile_counts: int32 [8, 16], P('row', 'col'), may hold values from 20 to 80, as said below
- features: bfloat16 [32768, 512], P(('col', 'row')), may hold values from -6 to 6
- weight: bfloat16 [512, 512], replicated, may hold values from -0.25 to 0.25
- node_grad: bfloat16 [32768, 512], P(('row', 'col')), may hold values from -6 to 6
Outputs:
- node_out: bfloat16 [32768, 512], P(('row', 'col'))
- weight_grad: float32 [512, 512], replicated
- feature_grad: bfloat16 [32768, 512], P(('col', 'row'))
Inputs may be any that keep to these rules, and one draw needn't show every extreme that they name: Within one cell the first 80 slots name distinct tiles (pairs of tile_rows and tile_cols). `tile_counts`: slots from this number on hold no tile; some cell fills all its slots.
All inputs are finite; a program needn't handle non-finite values.
Results may differ from a plain program's by a relative error of at most 0.027.
Values may be sent and summed in bfloat16 or wider, within the bound.
No kernel may reach another device: no remote copies, remote signals or barrier semaphores. Data moves between devices by JAX's collectives and lax.ppermute only.
A program may use at most 128 MiB of HBM per device.

v0:
```python
import jax
import jax.numpy as jnp
from jax import lax
from jax.sharding import PartitionSpec as P


def spread_tiles(
    cell_tiles,
    order,
    dest_ids,
    source_ids,
    first_live,
    end_live,
    source,
    dest_first,
    dest_tiles,
    transposed,
):
    slot_total = cell_tiles.shape[0]
    slot_block = min(16, slot_total)
    tile_size = cell_tiles.shape[1]
    feat_width = source.shape[2]
    block_total = (end_live - first_live + slot_block - 1) // slot_block
    slot_range = jnp.arange(slot_block, dtype=jnp.int32)
    dest_range = jnp.arange(dest_tiles, dtype=jnp.int32)

    def add_block(block_index, running):
        positions = first_live + block_index * slot_block + slot_range
        live_slots = positions < end_live
        clamped = jnp.minimum(positions, slot_total - 1)
        slot_ids = jnp.take(order, clamped, axis=0)
        tile_block = jnp.take(cell_tiles, slot_ids, axis=0)
        dest_block = jnp.take(dest_ids, slot_ids, axis=0)
        source_block = jnp.take(source_ids, slot_ids, axis=0)
        source_pieces = jnp.take(source, source_block, axis=0)
        if transposed:
            products = jnp.einsum(
                "sba,sbf->saf", tile_block, source_pieces, preferred_element_type=jnp.float32
            )
        else:
            products = jnp.einsum(
                "sab,sbf->saf", tile_block, source_pieces, preferred_element_type=jnp.float32
            )
        placing = (dest_range[:, None] == (dest_block - dest_first)[None, :]) & live_slots[None, :]
        placing = placing.astype(jnp.float32)
        added = jnp.einsum(
            "ds,saf->daf",
            placing,
            products,
            precision=lax.Precision.HIGHEST,
            preferred_element_type=jnp.float32,
        )
        return running + added

    start_value = jnp.zeros((dest_tiles, tile_size, feat_width), jnp.float32)
    return lax.fori_loop(0, block_total, add_block, start_value)


def local(adj_tiles, tile_rows, tile_cols, tile_counts, features, weight, node_grad):
    cell_tiles = adj_tiles[0, 0]
    cell_rows = tile_rows[0, 0]
    cell_cols = tile_cols[0, 0]
    slot_count = tile_counts[0, 0]
    slot_total = cell_tiles.shape[0]
    tile_size = cell_tiles.shape[1]
    feat_width = features.shape[1]
    node_count = features.shape[0]
    row_devices = lax.axis_size("row")
    col_devices = lax.axis_size("col")
    row_tiles = node_count * col_devices // tile_size
    col_tiles = node_count * row_devices // tile_size
    plain_order = jnp.arange(slot_total, dtype=jnp.int32)
    column_feats = lax.all_gather(features, "row", axis=0, tiled=True)
    source = column_feats.reshape(col_tiles, tile_size, feat_width)
    partial_value = spread_tiles(
        cell_tiles, plain_order, cell_rows, cell_cols, 0, slot_count, source, 0, row_tiles, False
    )
    agg = lax.psum_scatter(
        partial_value.reshape(row_tiles * tile_size, feat_width).astype(jnp.bfloat16),
        "col",
        scatter_dimension=0,
        tiled=True,
    )
    pre = jnp.dot(agg, weight, preferred_element_type=jnp.float32)
    node_out = jax.nn.silu(pre).astype(jnp.bfloat16)
    sigma = jax.nn.sigmoid(pre)
    dpre = (node_grad.astype(jnp.float32) * sigma * (1.0 + pre * (1.0 - sigma))).astype(
        jnp.bfloat16
    )
    scale_factor = 1.0 / jnp.sqrt(jnp.float32(node_count * row_devices * col_devices))
    weight_term = jnp.dot(agg.T, dpre, preferred_element_type=jnp.float32) * scale_factor
    dagg = jnp.dot(dpre, weight.T, preferred_element_type=jnp.float32).astype(jnp.bfloat16)
    grad_block = lax.all_gather(dagg, "col", axis=0, tiled=True)
    grad_source = grad_block.reshape(row_tiles, tile_size, feat_width)
    partial_back = spread_tiles(
        cell_tiles,
        plain_order,
        cell_cols,
        cell_rows,
        0,
        slot_count,
        grad_source,
        0,
        col_tiles,
        True,
    )
    summed = lax.psum_scatter(
        partial_back.reshape(col_tiles * tile_size, feat_width).astype(jnp.bfloat16),
        "row",
        scatter_dimension=0,
        tiled=True,
    )
    weight_grad = lax.psum(weight_term, ("row", "col"))
    return (node_out, weight_grad, summed)


def solution(mesh):
    in_specs = (
        P("row", "col", None, None, None),
        P("row", "col", None),
        P("row", "col", None),
        P("row", "col"),
        P(("col", "row"), None),
        P(),
        P(("row", "col"), None),
    )
    out_specs = (P(("row", "col"), None), P(), P(("col", "row"), None))
    return jax.shard_map(local, mesh=mesh, in_specs=in_specs, out_specs=out_specs, check_vma=False)
```

profile of v0, /device:TPU:0, one launch (start us, length us, event | category | flops | bytes accessed | tf_op | source)
XLA Modules:
  0.0 628.5 jit_solution(17216080920683603031)
XLA Ops:
  8.6 59.1 %all-gather.3.cloned.1.call-done = bf16[2048,512]{1,0:T(8,128)(2,1)} async-done(((bf16[256,512]{1,0:T(8,128)(2,1)}), bf16[2048,512]{1,0:T(8,128)(2,1)}) %all-gather.3.cloned.1.call-update) | async-done | bytes 2097168 | tf_op jit(solution)/shard_map/all_gather | solution.py:73
  67.8 4.3 broadcast_in_dim.54
  72.1 147.4 %while.25 = (s32[]{:T(128)}, f32[16,256,512]{2,0,1:T(8,128)}, s32[]{:T(128)}, s32[80]{0:T(128)S(1)}, s32[]{:T(128)}, /*index=5*/bf16[80,256,256]{2,1,0:T(8,128)(...) while((s32[]{:T(128)}, f32[16,256,512]{2,0,1:T(8,128)}, ...), condition=%wide.region_1.0_spmd.clone.clone, body=%wide.region_0.3_spmd.clone.clone.sunk | while | flops 1481641984 | bytes 52443164 | solution.py:56
  74.1 2.8 gather_fusion.7
  76.9 6.0 gather_fusion.8
  82.9 7.4 %fusion.76 = f32[16,256,512]{2,1,0:T(8,128)} fusion(bf16[16,256,512]{2,1,0:T(8,128)(2,1)} %gather_fusion.7, pred[16]{0:T(512)(128)(4,1)S(1)} %get-tuple-element.375, bf16[16,256,256]{2,1,0:T(8,128)(2,1)} %gather_fusion.8, pred[16]{0:T(512)(128)(4,1)S(1)} %get-tuple-element.376), kind=kOutput, calls=%fused_computation.46.clone.1 | convolution fusion | flops 1076887552 | bytes 14680096 | tf_op jit(solution)/shard_map/while/body/sab,sbf->saf/dot_general | solution.py:41
  91.0 17.9 %fusion.77 = f32[16,256,512]{2,0,1:T(8,128)} fusion(f32[16,256,512]{2,0,1:T(8,128)} %get-tuple-element.389, f32[16,256,512]{2,1,0:T(8,128)} %fusion.76, s32[16]{0:T(128)S(1)} %broadcast_select_fusion.5, pred[16]{0:T(512)(128)(4,1)S(1)} %get-tuple-element.377), kind=kOutput, calls=%fused_computation.49.clone.1 | convolution fusion | flops 404750848 | bytes 25165904 | tf_op jit(solution)/shard_map/while/body/ds,saf->daf/dot_general | solution.py:46
  111.0 2.8 gather_fusion.7
  113.7 6.0 gather_fusion.8
  119.7 7.4 %fusion.76 = f32[16,256,512]{2,1,0:T(8,128)} fusion(bf16[16,256,512]{2,1,0:T(8,128)(2,1)} %gather_fusion.7, pred[16]{0:T(512)(128)(4,1)S(1)} %get-tuple-element.375, bf16[16,256,256]{2,1,0:T(8,128)(2,1)} %gather_fusion.8, pred[16]{0:T(512)(128)(4,1)S(1)} %get-tuple-element.376), kind=kOutput, calls=%fused_computation.46.clone.1 | convolution fusion | flops 1076887552 | bytes 14680096 | tf_op jit(solution)/shard_map/while/body/sab,sbf->saf/dot_general | solution.py:41
  127.8 17.9 %fusion.77 = f32[16,256,512]{2,0,1:T(8,128)} fusion(f32[16,256,512]{2,0,1:T(8,128)} %get-tuple-element.389, f32[16,256,512]{2,1,0:T(8,128)} %fusion.76, s32[16]{0:T(128)S(1)} %broadcast_select_fusion.5, pred[16]{0:T(512)(128)(4,1)S(1)} %get-tuple-element.377), kind=kOutput, calls=%fused_computation.49.clone.1 | convolution fusion | flops 404750848 | bytes 25165904 | tf_op jit(solution)/shard_map/while/body/ds,saf->daf/dot_general | solution.py:46
  147.8 2.8 gather_fusion.7
  150.6 6.0 gather_fusion.8
  156.6 7.4 %fusion.76 = f32[16,256,512]{2,1,0:T(8,128)} fusion(bf16[16,256,512]{2,1,0:T(8,128)(2,1)} %gather_fusion.7, pred[16]{0:T(512)(128)(4,1)S(1)} %get-tuple-element.375, bf16[16,256,256]{2,1,0:T(8,128)(2,1)} %gather_fusion.8, pred[16]{0:T(512)(128)(4,1)S(1)} %get-tuple-element.376), kind=kOutput, calls=%fused_computation.46.clone.1 | convolution fusion | flops 1076887552 | bytes 14680096 | tf_op jit(solution)/shard_map/while/body/sab,sbf->saf/dot_general | solution.py:41
  164.6 17.9 %fusion.77 = f32[16,256,512]{2,0,1:T(8,128)} fusion(f32[16,256,512]{2,0,1:T(8,128)} %get-tuple-element.389, f32[16,256,512]{2,1,0:T(8,128)} %fusion.76, s32[16]{0:T(128)S(1)} %broadcast_select_fusion.5, pred[16]{0:T(512)(128)(4,1)S(1)} %get-tuple-element.377), kind=kOutput, calls=%fused_computation.49.clone.1 | convolution fusion | flops 404750848 | bytes 25165904 | tf_op jit(solution)/shard_map/while/body/ds,saf->daf/dot_general | solution.py:46
  184.6 2.8 gather_fusion.7
  187.4 6.0 gather_fusion.8
  193.4 7.4 %fusion.76 = f32[16,256,512]{2,1,0:T(8,128)} fusion(bf16[16,256,512]{2,1,0:T(8,128)(2,1)} %gather_fusion.7, pred[16]{0:T(512)(128)(4,1)S(1)} %get-tuple-element.375, bf16[16,256,256]{2,1,0:T(8,128)(2,1)} %gather_fusion.8, pred[16]{0:T(512)(128)(4,1)S(1)} %get-tuple-element.376), kind=kOutput, calls=%fused_computation.46.clone.1 | convolution fusion | flops 1076887552 | bytes 14680096 | tf_op jit(solution)/shard_map/while/body/sab,sbf->saf/dot_general | solution.py:41
  201.5 17.9 %fusion.77 = f32[16,256,512]{2,0,1:T(8,128)} fusion(f32[16,256,512]{2,0,1:T(8,128)} %get-tuple-element.389, f32[16,256,512]{2,1,0:T(8,128)} %fusion.76, s32[16]{0:T(128)S(1)} %broadcast_select_fusion.5, pred[16]{0:T(512)(128)(4,1)S(1)} %get-tuple-element.377), kind=kOutput, calls=%fused_computation.49.clone.1 | convolution fusion | flops 404750848 | bytes 25165904 | tf_op jit(solution)/shard_map/while/body/ds,saf->daf/dot_general | solution.py:46
  219.4 9.8 %copy.24 = bf16[16,256,512]{2,1,0:T(8,128)(2,1)} copy(f32[16,256,512]{2,0,1:T(8,128)} %get-tuple-element.146) | data formatting | bytes 12582912 | tf_op jit(solution)/shard_map/while | solution.py:56
  229.3 102.0 %reduce-scatter.3.cloned.1.call-done = bf16[256,512]{1,0:T(8,128)(2,1)} async-done(((bf16[4096,512]{1,0:T(8,128)(2,1)}), bf16[256,512]{1,0:T(8,128)(2,1)}) %reduce-scatter.3.cloned.1.call-update) | async-done | bytes 262160 | tf_op jit(solution)/shard_map/reduce_scatter | solution.py:78
  331.3 2.1 multiply_convert_fusion.1
  333.4 1.1 convolution_convert_fusion
  334.5 1.5 convolution_multiply_fusion
  336.1 34.6 %all-gather.5.cloned.1.call-done = bf16[4096,512]{1,0:T(8,128)(2,1)} async-done(((bf16[256,512]{1,0:T(8,128)(2,1)}), bf16[4096,512]{1,0:T(8,128)(2,1)}) %all-gather.5.cloned.1.call-update) | async-done | bytes 4194320 | tf_op jit(solution)/shard_map/all_gather | solution.py:93
  370.6 2.5 broadcast_in_dim.55
  373.1 133.5 %while.24 = (s32[]{:T(128)}, f32[8,256,512]{2,0,1:T(8,128)}, s32[]{:T(128)}, s32[80]{0:T(128)S(1)}, s32[]{:T(128)}, /*index=5*/bf16[80,256,256]{2,1,0:T(8,128)(2...) while((s32[]{:T(128)}, f32[8,256,512]{2,0,1:T(8,128)}, s32[]{:T(128)}, ...), condition=%wide.region_5.8_spmd.clone, body=%wide.region_4.7_spmd.clone.sunk | while | flops 1279266560 | bytes 44054556 | solution.py:56
  375.1 4.9 gather_fusion.2
  380.1 4.7 gather_fusion.3
  384.8 6.8 %fusion.70 = f32[16,256,512]{2,1,0:T(8,128)} fusion(bf16[16,256,512]{2,1,0:T(8,128)(2,1)} %gather_fusion.2, pred[16]{0:T(512)(128)(4,1)S(1)} %get-tuple-element.362, bf16[16,256,256]{2,1,0:T(8,128)(2,1)S(1)} %gather_fusion.3, pred[16]{0:T(512)(128)(4,1)S(1)} %get-tuple-element.363), kind=kOutput, calls=%fused_computation.17.clone.1 | convolution fusion | flops 1076887552 | bytes 14680096 | tf_op jit(solution)/shard_map/while/body/sba,sbf->saf/dot_general | solution.py:37
  392.3 14.2 %fusion.71 = f32[8,256,512]{2,0,1:T(8,128)} fusion(f32[8,256,512]{2,0,1:T(8,128)} %get-tuple-element.419, f32[16,256,512]{2,1,0:T(8,128)} %fusion.70, s32[16]{0:T(128)S(1)} %broadcast_select_fusion.4, pred[16]{0:T(512)(128)(4,1)S(1)} %get-tuple-element.364), kind=kOutput, calls=%fused_computation.20.clone.1 | convolution fusion | flops 202375424 | bytes 16777296 | tf_op jit(solution)/shard_map/while/body/ds,saf->daf/dot_general | solution.py:46
  408.5 5.0 gather_fusion.2
  413.5 4.7 gather_fusion.3
  418.2 6.9 %fusion.70 = f32[16,256,512]{2,1,0:T(8,128)} fusion(bf16[16,256,512]{2,1,0:T(8,128)(2,1)} %gather_fusion.2, pred[16]{0:T(512)(128)(4,1)S(1)} %get-tuple-element.362, bf16[16,256,256]{2,1,0:T(8,128)(2,1)S(1)} %gather_fusion.3, pred[16]{0:T(512)(128)(4,1)S(1)} %get-tuple-element.363), kind=kOutput, calls=%fused_computation.17.clone.1 | convolution fusion | flops 1076887552 | bytes 14680096 | tf_op jit(solution)/shard_map/while/body/sba,sbf->saf/dot_general | solution.py:37
  425.7 14.2 %fusion.71 = f32[8,256,512]{2,0,1:T(8,128)} fusion(f32[8,256,512]{2,0,1:T(8,128)} %get-tuple-element.419, f32[16,256,512]{2,1,0:T(8,128)} %fusion.70, s32[16]{0:T(128)S(1)} %broadcast_select_fusion.4, pred[16]{0:T(512)(128)(4,1)S(1)} %get-tuple-element.364), kind=kOutput, calls=%fused_computation.20.clone.1 | convolution fusion | flops 202375424 | bytes 16777296 | tf_op jit(solution)/shard_map/while/body/ds,saf->daf/dot_general | solution.py:46
  441.9 5.0 gather_fusion.2
  446.9 4.7 gather_fusion.3
  451.6 6.8 %fusion.70 = f32[16,256,512]{2,1,0:T(8,128)} fusion(bf16[16,256,512]{2,1,0:T(8,128)(2,1)} %gather_fusion.2, pred[16]{0:T(512)(128)(4,1)S(1)} %get-tuple-element.362, bf16[16,256,256]{2,1,0:T(8,128)(2,1)S(1)} %gather_fusion.3, pred[16]{0:T(512)(128)(4,1)S(1)} %get-tuple-element.363), kind=kOutput, calls=%fused_computation.17.clone.1 | convolution fusion | flops 1076887552 | bytes 14680096 | tf_op jit(solution)/shard_map/while/body/sba,sbf->saf/dot_general | solution.py:37
  459.1 14.2 %fusion.71 = f32[8,256,512]{2,0,1:T(8,128)} fusion(f32[8,256,512]{2,0,1:T(8,128)} %get-tuple-element.419, f32[16,256,512]{2,1,0:T(8,128)} %fusion.70, s32[16]{0:T(128)S(1)} %broadcast_select_fusion.4, pred[16]{0:T(512)(128)(4,1)S(1)} %get-tuple-element.364), kind=kOutput, calls=%fused_computation.20.clone.1 | convolution fusion | flops 202375424 | bytes 16777296 | tf_op jit(solution)/shard_map/while/body/ds,saf->daf/dot_general | solution.py:46
  475.3 5.0 gather_fusion.2
  480.3 4.7 gather_fusion.3
  484.9 6.9 %fusion.70 = f32[16,256,512]{2,1,0:T(8,128)} fusion(bf16[16,256,512]{2,1,0:T(8,128)(2,1)} %gather_fusion.2, pred[16]{0:T(512)(128)(4,1)S(1)} %get-tuple-element.362, bf16[16,256,256]{2,1,0:T(8,128)(2,1)S(1)} %gather_fusion.3, pred[16]{0:T(512)(128)(4,1)S(1)} %get-tuple-element.363), kind=kOutput, calls=%fused_computation.17.clone.1 | convolution fusion | flops 1076887552 | bytes 14680096 | tf_op jit(solution)/shard_map/while/body/sba,sbf->saf/dot_general | solution.py:37
  492.5 14.2 %fusion.71 = f32[8,256,512]{2,0,1:T(8,128)} fusion(f32[8,256,512]{2,0,1:T(8,128)} %get-tuple-element.419, f32[16,256,512]{2,1,0:T(8,128)} %fusion.70, s32[16]{0:T(128)S(1)} %broadcast_select_fusion.4, pred[16]{0:T(512)(128)(4,1)S(1)} %get-tuple-element.364), kind=kOutput, calls=%fused_computation.20.clone.1 | convolution fusion | flops 202375424 | bytes 16777296 | tf_op jit(solution)/shard_map/while/body/ds,saf->daf/dot_general | solution.py:46
  506.6 2.5 convert_element_type.33
  509.2 2.0 copy.12
  511.2 11.3 %all-reduce.2.cloned.1.call-done = f32[512,512]{1,0:T(8,128)} async-done(((f32[512,512]{1,0:T(8,128)}), f32[512,512]{1,0:T(8,128)}) %all-reduce.2.cloned.1.call-update) | async-done | bytes 1048592 | tf_op jit(solution)/shard_map/psum | solution.py:113
  522.5 97.2 %reduce-scatter.5.cloned.1.call-done = bf16[256,512]{1,0:T(8,128)(2,1)} async-done(((bf16[2048,512]{1,0:T(8,128)(2,1)}), bf16[256,512]{1,0:T(8,128)(2,1)}) %reduce-scatter.5.cloned.1.call-update) | async-done | bytes 262160 | tf_op jit(solution)/shard_map/reduce_scatter | solution.py:107
  619.7 2.3 copy.45
  (112 shorter events, 22.4 us)
Async XLA Ops:
  7.2 324.1 %copy-start = (bf16[512,512]{1,0:T(8,128)(2,1)S(1)}, bf16[512,512]{1,0:T(8,128)(2,1)}, u32[]{:S(2)}) copy-start(bf16[512,512]{1,0:T(8,128)(2,1)} %param.20) | copy-start | bytes 1572868
  7.2 60.6 %all-gather.3.cloned.1.call-start = ((), (), s32[]{:S(2)}) async-start(), calls=%async_computation.2 | async-start | bytes 2359296 | tf_op jit(solution)/shard_map/all_gather | solution.py:73
  7.9 323.3 %reduce-scatter.3.cloned.1.call-start = ((), (), s32[]{:S(2)}) async-start(), calls=%async_computation.3 | async-start | bytes 4456448 | tf_op jit(solution)/shard_map/reduce_scatter | solution.py:78
  67.7 4.3 copy-start.2
  67.7 4.3 copy-start.3
  67.7 4.3 copy-start.4
  229.2 104.2 %copy-start.5 = (bf16[256,512]{1,0:T(8,128)(2,1)S(1)}, bf16[256,512]{1,0:T(8,128)(2,1)}, u32[]{:S(2)}) copy-start(bf16[256,512]{1,0:T(8,128)(2,1)} %param.21) | copy-start | bytes 786436
  229.2 141.4 %all-gather.5.cloned.1.call-start = ((), (), s32[]{:S(2)}) async-start(), calls=%async_computation.5 | async-start | bytes 4456448 | tf_op jit(solution)/shard_map/all_gather | solution.py:93
  331.3 3.3 copy-start.6
  334.5 188.1 %all-reduce.2.cloned.1.call-start = ((), (), s32[]{:S(2)}) async-start(), calls=%async_computation.4 | async-start | bytes 2097152 | tf_op jit(solution)/shard_map/psum | solution.py:113
  336.0 283.7 %reduce-scatter.5.cloned.1.call-start = ((), (), s32[]{:S(2)}) async-start(), calls=%async_computation.6 | async-start | bytes 2359296 | tf_op jit(solution)/shard_map/reduce_scatter | solution.py:107
  506.6 115.3 %copy-start.1 = (bf16[512,512]{1,0:T(8,128)(2,1)S(1)}, bf16[512,512]{1,0:T(8,128)(2,1)}, u32[]{:S(2)}) copy-start(bf16[512,512]{1,0:T(8,128)(2,1)} %param.20) | copy-start | bytes 1572868
Sparse Core Ops, SparseCore 0:
  10.4 57.3 all-gather.2
  229.4 101.8 reduce-scatter.2
  334.6 35.9 all-gather.4
  375.8 146.6 all-reduce.1
  527.2 92.4 reduce-scatter.4
where the time goes:
time: 630 us; the launch traced here: 628 us
  waiting for transfers between devices  305 us (48%)
  matrix products  190 us (30%)
  local copies, waits for them, and re-layouts  110 us (17%)
  between operations  14.5 us (2%)
  other arithmetic  8.2 us (1%)
    dot_general x8, matrix products, add_block(): jnp.einsum('ds,saf->daf', placing, products, precision=lax.Precision.HIGH...  128 us
    reduce_scatter x1, waiting for transfers between devices, local(): lax.psum_scatter(partial_value.reshape(row_tiles * tile_size, feat_width)...  102 us
    reduce_scatter x1, waiting for transfers between devices, local(): lax.psum_scatter(partial_back.reshape(col_tiles * tile_size, feat_width)....  97.2 us
    all_gather x1, waiting for transfers between devices, local(): column_feats = lax.all_gather(features, 'row', axis=0, tiled=True)  59.1 us
    gather x8, local copies, waits for them, and re-layouts, add_block(): tile_block = jnp.take(cell_tiles, slot_ids, axis=0)  42.7 us
    all_gather x1, waiting for transfers between devices, local(): grad_block = lax.all_gather(dagg, 'col', axis=0, tiled=True)  34.6 us
    gather x8, local copies, waits for them, and re-layouts, add_block(): source_pieces = jnp.take(source, source_block, axis=0)  30.9 us
    dot_general x4, matrix products, add_block(): jnp.einsum('sab,sbf->saf', tile_block, source_pieces, preferred_element_t...  29.6 us
  transfers between devices with their start and end apart: 5, of which 5 were waited for; matrix products, arithmetic and copies ran while one was open for 23% of the time, Pallas kernels for 0%

commit v1 on v0

v1 whole, which is shorter than its diff:
```python
import jax
import jax.numpy as jnp
from jax import lax
from jax.experimental import pallas as pl
from jax.experimental.pallas import tpu as pltpu
from jax.sharding import PartitionSpec as P

BF = jnp.bfloat16
F32 = jnp.float32
GROUP = 4
SMEM = pl.BlockSpec(memory_space=pltpu.SMEM)
ANY = pl.BlockSpec(memory_space=pl.ANY)


def list_tiles(dest, source, count, total, dests, first, slots, srcs, fill):
    for d in range(dests):
        fill[d] = 0

    def tally(t, carry):
        fill[dest[t]] = fill[dest[t]] + 1
        return carry

    lax.fori_loop(0, count, tally, 0)

    def place(d, pos):
        first[d] = pos
        groups = jnp.maximum(lax.div(fill[d] + (GROUP - 1), GROUP), 1)
        fill[d] = pos * GROUP
        for k in range(GROUP):
            last = (pos + groups - 1) * GROUP + k
            slots[last] = total
            srcs[last] = 0
        return pos + groups

    first[dests] = lax.fori_loop(0, dests, place, 0)

    def put(t, carry):
        d = dest[t]
        p = fill[d]
        fill[d] = p + 1
        slots[p] = t
        srcs[p] = source[t]
        return carry

    lax.fori_loop(0, count, put, 0)


def schedule(rows, cols, count, row_tiles, col_tiles):
    total = rows.shape[0]

    def body(r, c, n, ff, fs, fc, bf, bs, bc, fill):
        list_tiles(r, c, n[0], total, row_tiles, ff, fs, fc, fill)
        list_tiles(c, r, n[0], total, col_tiles, bf, bs, bc, fill)

    def table(n):
        return jax.ShapeDtypeStruct((n,), jnp.int32)

    fl = total + row_tiles * GROUP
    bl = total + col_tiles * GROUP
    return pl.pallas_call(
        body,
        in_specs=[SMEM] * 3,
        out_specs=[SMEM] * 6,
        out_shape=[table(row_tiles + 1), table(fl), table(fl)]
        + [table(col_tiles + 1), table(bl), table(bl)],
        scratch_shapes=[pltpu.SMEM((max(row_tiles, col_tiles),), jnp.int32)],
        name="schedule",
    )(rows, cols, count)


def spread(first, slots, srcs, tiles, sources, start, dests, transposed):
    total, size = tiles.shape[:2]
    room = slots.shape[0]
    blocks = sum(s.shape[0] for s in sources)
    block = sources[0].shape[1:]

    def body(*refs):
        first, slots, srcs, tiles = refs[:4]
        ins = refs[4 : 4 + len(sources)]
        out, held, src, acc, stage, tile_sem, src_sem, out_sem = refs[4 + len(sources) :]
        base = first[start] * GROUP
        end = first[start + dests] * GROUP
        copies = []
        at = 0
        for k, ref in enumerate(ins):
            n = ref.shape[0]
            copies.append(pltpu.make_async_copy(ref, src.at[pl.ds(at, n)], src_sem.at[k]))
            at += n
        for copy in copies:
            copy.start()

        def fetch(p, carry):
            s = slots[base + p]

            @pl.when(s < total)
            def _():
                pltpu.make_async_copy(tiles.at[s], held.at[p], tile_sem.at[p]).start()

            @pl.when(s >= total)
            def _():
                held[p] = jnp.zeros((size, size), BF)

            return carry

        lax.fori_loop(0, end - base, fetch, 0)
        for copy in copies:
            copy.wait()

        def product(g):
            ps = [g * GROUP + k for k in range(GROUP)]
            for p in ps:

                @pl.when(slots[p] < total)
                def _():
                    pltpu.make_async_copy(
                        tiles.at[0], held.at[p - base], tile_sem.at[p - base]
                    ).wait()

            if transposed:
                left = jnp.concatenate([src[srcs[p]] for p in ps], 1)
                right = held[pl.ds(g * GROUP - base, GROUP)].reshape(GROUP * size, size)
            else:
                left = jnp.concatenate([held[p - base] for p in ps], 1)
                right = jnp.concatenate([src[srcs[p]] for p in ps], 0)
            return jnp.dot(left, right, preferred_element_type=F32)

        def one(d, carry):
            lo = first[start + d]
            acc[...] = product(lo)

            def more(g, inner):
                acc[...] += product(g)
                return inner

            lax.fori_loop(lo + 1, first[start + d + 1], more, 0)
            stage[d] = acc[...].astype(BF)
            pltpu.make_async_copy(stage.at[d], out.at[d], out_sem.at[d]).start()
            return carry

        lax.fori_loop(0, dests, one, 0)

        def finish(d, carry):
            pltpu.make_async_copy(stage.at[d], out.at[d], out_sem.at[d]).wait()
            return carry

        lax.fori_loop(0, dests, finish, 0)

    return pl.pallas_call(
        body,
        in_specs=[SMEM] * 3 + [ANY] * (1 + len(sources)),
        out_specs=ANY,
        out_shape=jax.ShapeDtypeStruct((dests,) + block, BF),
        scratch_shapes=[
            pltpu.VMEM((room, size, size), BF),
            pltpu.VMEM((blocks,) + block, BF),
            pltpu.VMEM(block, F32),
            pltpu.VMEM((dests,) + block, BF),
            pltpu.SemaphoreType.DMA((room,)),
            pltpu.SemaphoreType.DMA((len(sources),)),
            pltpu.SemaphoreType.DMA((dests,)),
        ],
        compiler_params=pltpu.CompilerParams(vmem_limit_bytes=56 * 1024 * 1024),
        name="spread_back" if transposed else "spread",
    )(first, slots, srcs, tiles, *sources)


def local(adj_tiles, tile_rows, tile_cols, tile_counts, features, weight, node_grad):
    tiles = adj_tiles[0, 0]
    size = tiles.shape[1]
    width = features.shape[1]
    row_devices = lax.axis_size("row")
    col_devices = lax.axis_size("col")
    half = col_devices // 2
    core = lax.rem(lax.axis_index("col"), 2)
    same_core = [[2 * k + c for k in range(half)] for c in range(2)]
    swap = [(i, i ^ 1) for i in range(col_devices)]
    rows = tile_rows[0, 0]
    rows = lax.shift_right_logical(rows, 1) + half * ((rows & 1) ^ core)
    ff, fs, fc, bf, bs, bc = schedule(
        rows, tile_cols[0, 0], tile_counts[0], col_devices, row_devices
    )

    spread_feats = jnp.broadcast_to(features[None], (row_devices, size, width))
    column_feats = lax.all_to_all(spread_feats, "row", 0, 0)
    sent = spread(ff, fs, fc, tiles, [column_feats], half, half, False)
    met = lax.ppermute(sent, "col", swap)
    kept = spread(ff, fs, fc, tiles, [column_feats], 0, half, False)
    pair = (kept.astype(F32) + met.astype(F32)).astype(BF)
    parts = lax.all_to_all(pair, "col", 0, 0, axis_index_groups=same_core)
    agg = parts.astype(F32).sum(0).astype(BF)

    pre = jnp.dot(agg, weight, preferred_element_type=F32)
    node_out = jax.nn.silu(pre).astype(BF)
    sigma = jax.nn.sigmoid(pre)
    dpre = (node_grad.astype(F32) * sigma * (1.0 + pre * (1.0 - sigma))).astype(BF)
    dagg = lax.dot_general(
        weight, dpre, (((1,), (1,)), ((), ())), preferred_element_type=F32
    ).astype(BF)
    scale = 1.0 / jnp.sqrt(jnp.float32(size * row_devices * col_devices))
    term = lax.dot_general(agg, dpre, (((0,), (0,)), ((), ())), preferred_element_type=F32)

    own = lax.all_to_all(
        jnp.broadcast_to(dagg[None], (half,) + dagg.shape),
        "col",
        0,
        0,
        axis_index_groups=same_core,
    )
    other = lax.ppermute(own, "col", swap)
    back = spread(bf, bs, bc, tiles, [own, other], 0, row_devices, True)
    back = lax.all_to_all(back, "row", 0, 0)
    feature_grad = back.astype(F32).sum(0).T.astype(BF)

    term = (term * scale).reshape((2,) + (term.shape[0] // 2, term.shape[1]))
    mine = lax.dynamic_index_in_dim(term, core, 0, False)
    yours = lax.dynamic_index_in_dim(term, 1 - core, 0, False)
    mine = mine + lax.ppermute(yours, "col", swap)
    mine = mine.reshape(half, mine.shape[0] // half, mine.shape[1])
    mine = lax.all_to_all(mine, "col", 0, 0, axis_index_groups=same_core).sum(0)
    mine = lax.all_to_all(
        jnp.broadcast_to(mine[None], (row_devices,) + mine.shape), "row", 0, 0
    ).sum(0)
    mine = lax.all_to_all(
        jnp.broadcast_to(mine[None], (half,) + mine.shape),
        "col",
        0,
        0,
        axis_index_groups=same_core,
    ).reshape(weight.shape[0] // 2, weight.shape[1])
    yours = lax.ppermute(mine, "col", swap)
    weight_grad = jnp.where(
        core == 0, jnp.concatenate([mine, yours], 0), jnp.concatenate([yours, mine], 0)
    )
    return node_out, weight_grad, feature_grad


def solution(mesh):
    in_specs = (
        P("row", "col", None, None, None),
        P("row", "col", None),
        P("row", "col", None),
        P("row", "col"),
        P(("col", "row"), None),
        P(),
        P(("row", "col"), None),
    )
    out_specs = (P(("row", "col"), None), P(), P(("col", "row"), None))
    return jax.shard_map(local, mesh=mesh, in_specs=in_specs, out_specs=out_specs, check_vma=False)
```

time: 630 us -> 210 us (0.33)
  waiting for transfers between devices: 305 us -> 70.7 us
  matrix products: 190 us -> 2.97 us
  local copies, waits for them, and re-layouts: 110 us -> 8.38 us
  blocking collectives: 0 us -> 61.5 us
  Pallas kernels: 0 us -> 32.2 us
  starting transfers between devices: 0.2 us -> 22.3 us
  between operations: 14.5 us -> 1.45 us
    reduce_scatter x2 -> x0, waiting for transfers between devices: 199 us -> none  [the longest x1 102 us: local(): lax.psum_scatter(partial_value.reshape(row_tiles * tile_size, feat_width)...]
    dot_general x19 -> x3, matrix products: 190 us -> 2.97 us  [the longest x1 1.52 us: local(): lax.dot_general(agg, dpre, (((0,), (0,)), ((), ())), preferred_element_ty...]
    all_gather x2 -> x0, waiting for transfers between devices: 93.7 us -> none  [the longest x1 59.1 us: local(): column_feats = lax.all_gather(features, 'row', axis=0, tiled=True)]
    gather x40 -> x0, local copies, waits for them, and re-layouts: 89.3 us -> none  [the longest x8 42.7 us: add_block(): tile_block = jnp.take(cell_tiles, slot_ids, axis=0)]
    all_to_all x0 -> x4, waiting for transfers between devices: none -> 68.7 us  [the longest x1 24 us: local(): column_feats = lax.all_to_all(spread_feats, 'row', 0, 0)]
    all_to_all x0 -> x3, blocking collectives: none -> 61.5 us  [the longest x1 33.3 us: local(): parts = lax.all_to_all(pair, 'col', 0, 0, axis_index_groups=same_core)]
    pallas_call x0 -> x4, Pallas kernels: none -> 32.2 us  [the longest x3 28.9 us: spread(): pl.pallas_call(body, in_specs=[SMEM] * 3 + [ANY] * (1 + len(sources)), ou...]
    all_to_all x0 -> x4, starting transfers between devices: none -> 21.2 us  [the longest x1 7.15 us: local(): column_feats = lax.all_to_all(spread_feats, 'row', 0, 0)]
  transfers between devices with their start and end apart: 5 -> 8, of which waited for: 5 -> 4; matrix products, arithmetic and copies ran while one was open for 23% -> 4% of each run, Pallas kernels for 0% -> 12%
where the time goes in v1:
time: 210 us; the launch traced here: 207 us
  waiting for transfers between devices  70.7 us (34%)
  blocking collectives  61.5 us (29%)
  Pallas kernels  32.2 us (15%)
  starting transfers between devices  22.3 us (11%)
  local copies, waits for them, and re-layouts  8.38 us (4%)
  other arithmetic  7.48 us (4%)
  matrix products  2.97 us (1%)
    all_to_all x1, blocking collectives, local(): parts = lax.all_to_all(pair, 'col', 0, 0, axis_index_groups=same_core)  33.3 us
    pallas_call x3, Pallas kernels, spread(): pl.pallas_call(body, in_specs=[SMEM] * 3 + [ANY] * (1 + len(sources)), ou...  28.9 us
    all_to_all x1, waiting for transfers between devices, local(): column_feats = lax.all_to_all(spread_feats, 'row', 0, 0)  24 us
    all_to_all x1, waiting for transfers between devices, local(): lax.all_to_all(jnp.broadcast_to(dagg[None], (half,) + dagg.shape), 'col',...  23.7 us
    all_to_all x1, waiting for transfers between devices, local(): back = lax.all_to_all(back, 'row', 0, 0)  21 us
    all_to_all x1, blocking collectives, local(): lax.all_to_all(jnp.broadcast_to(mine[None], (row_devices,) + mine.shape),...  14.3 us
    all_to_all x1, blocking collectives, local(): mine = lax.all_to_all(mine, 'col', 0, 0, axis_index_groups=same_core).sum(0)  13.9 us
    all_to_all x1, starting transfers between devices, local(): column_feats = lax.all_to_all(spread_feats, 'row', 0, 0)  7.15 us
  transfers between devices with their start and end apart: 8, of which 4 were waited for; matrix products, arithmetic and copies ran while one was open for 4% of the time, Pallas kernels for 12%

profile of v1, /device:TPU:0, one launch (start us, length us, event | category | flops | bytes accessed | tf_op | source)
XLA Modules:
  0.0 207.0 jit_solution(7820756531975210711)
XLA Ops:
  0.6 0.0 copy-start
  0.6 2.5 %broadcast_in_dim.8 = bf16[8,256,512]{2,1,0:T(8,128)(2,1)} broadcast(bf16[256,512]{1,0:T(8,128)(2,1)} %param.11), dimensions={1,2} | broadcast | bytes 2359296 | tf_op jit(solution)/shard_map/broadcast_in_dim | solution.py:183
  3.2 7.1 %all-to-all-start = ((bf16[8,256,512]{2,1,0:T(8,128)(2,1)}), bf16[8,256,512]{2,1,0:T(8,128)(2,1)S(1)}, u32[]{:S(2)}, u32[]{:S(2)}) async-start(bf16[8,256,512]{2,1,0:T(8,128)(2,1)} %broadcast_in_dim.8), calls=%async_computation | async-start | bytes 4194304 | tf_op jit(solution)/shard_map/all_to_all | solution.py:184
  11.0 0.0 copy-done.5
  11.0 0.5 add_bitcast_fusion.r
  11.5 3.3 %schedule.1 = (s32[17]{0:T(128)}, s32[144]{0:T(256)}, s32[144]{0:T(256)}, s32[9]{0:T(128)}, s32[112]{0:T(128)}, /*index=5*/s32[112]{0:T(128)}) custom-call(s32[80]{0:T(128)} %add_bitcast_fusion.r, s32[80]{0:T(128)} %bitcast.29, s32[1]{0:T(128)} %bitcast.19.n), custom_call_target="tpu_custom_call" | custom-call | tf_op jit(solution)/shard_map/schedule/pallas_call | solution.py:60
  14.7 24.0 %all-to-all-done.refs_4_ = bf16[8,256,512]{2,1,0:T(8,128)(2,1)S(1)} async-done(((bf16[8,256,512]{2,1,0:T(8,128)(2,1)}), bf16[8,256,512]{2,1,0:T(8,128)(2,1)S(1)}, u32[]{:S(2)}, u32[]{:S(2)}) %all-to-all-start) | async-done | bytes 2097184 | tf_op jit(solution)/shard_map/all_to_all | solution.py:184
  38.7 1.3 copy-done.1
  40.1 8.2 %spread.3 = bf16[8,256,512]{2,1,0:T(8,128)(2,1)} custom-call(s32[17]{0:T(128)} %get-tuple-element.9.refs_0_, s32[144]{0:T(256)} %get-tuple-element.10.refs_1_, s32[144]{0:T(256)} %get-tuple-element.11.refs_2_, bf16[80,256,256]{2,1,0:T(8,128)(2,1)} %bitcast.20, bf16[8,256,512]{2,1,0:T(8,128)(2,1)} %copy-done.1), custom_call_target="tpu_custom_call" | custom-call | tf_op jit(solution)/shard_map/spread/pallas_call | solution.py:148
  48.3 0.7 collective-permute-start
  49.0 9.2 %spread.2 = bf16[8,256,512]{2,1,0:T(8,128)(2,1)} custom-call(s32[17]{0:T(128)} %get-tuple-element.9.refs_0_, s32[144]{0:T(256)} %get-tuple-element.10.refs_1_, s32[144]{0:T(256)} %get-tuple-element.11.refs_2_, bf16[80,256,256]{2,1,0:T(8,128)(2,1)} %bitcast.21, bf16[8,256,512]{2,1,0:T(8,128)(2,1)} %copy-done.1), custom_call_target="tpu_custom_call" | custom-call | tf_op jit(solution)/shard_map/spread/pallas_call | solution.py:148
  58.2 0.0 collective-permute-done
  58.2 2.2 %add_convert_fusion = bf16[8,256,512]{2,1,0:T(8,128)(2,1)S(1)} fusion(bf16[8,256,512]{2,1,0:T(8,128)(2,1)S(1)} %collective-permute-done, bf16[8,256,512]{2,1,0:T(8,128)(2,1)} %spread.2), kind=kLoop, calls=%fused_computation | loop fusion | flops 4194304 | bytes 6291456 | tf_op jit(solution)/shard_map/convert_element_type | solution.py:188
  60.5 33.3 %all_to_all.35 = bf16[8,256,512]{2,1,0:T(8,128)(2,1)S(1)} all-to-all(bf16[8,256,512]{2,1,0:T(8,128)(2,1)S(1)} %add_convert_fusion), channel_id=1, replica_groups={{0,2,4,6,8,10,12,14},{1,3,5,7,9,11,13,15},{16,18,20,22,24,26,28,30},{17..., dimensions={0} | all-to-all | bytes 4194304 | tf_op jit(solution)/shard_map/all_to_all | solution.py:189
  93.7 0.4 reduce_sum.42
  94.1 0.0 copy-done
  94.1 0.0 copy-start.4
  94.1 1.1 multiply_convert_fusion.1
  95.2 0.0 copy-done.4
  95.2 0.4 fusion
  95.6 0.1 copy.13
  95.7 1.5 broadcast_in_dim.11
  97.2 3.9 %all-to-all-start.5 = ((bf16[8,512,256]{2,1,0:T(8,128)(2,1)}), bf16[8,512,256]{2,1,0:T(8,128)(2,1)S(1)}, u32[]{:S(2)}, u32[]{:S(2)}) async-start(bf16[8,512,256]{2,1,0:T(8,128)(2,1)} %broadcast_in_dim.11), calls=%async_computation.5 | async-start | bytes 4194304 | tf_op jit(solution)/shard_map/all_to_all | solution.py:202
  101.1 1.5 convolution_multiply_fusion
  102.7 0.0 copy-start.3
  102.7 0.9 dynamic-slice_bitcast_fusion
  103.6 0.2 copy-done.3
  103.8 0.4 collective-permute-start.1
  104.2 23.7 %all-to-all-done.5.refs_4_ = bf16[8,512,256]{2,1,0:T(8,128)(2,1)S(1)} async-done(((bf16[8,512,256]{2,1,0:T(8,128)(2,1)}), bf16[8,512,256]{2,1,0:T(8,128)(2,1)S(1)}, u32[]{:S(2)}, u32[]{:S(2)}) %all-to-all-start.5) | async-done | bytes 2097184 | tf_op jit(solution)/shard_map/all_to_all | solution.py:202
  127.9 0.0 collective-permute-start.3
  127.9 0.0 collective-permute-done.1
  127.9 1.5 bitcast_add_fusion
  129.4 13.9 %all_to_all.36 = f32[8,32,512]{2,1,0:T(8,128)S(1)} all-to-all(f32[8,32,512]{2,1,0:T(8,128)S(1)} %bitcast.25), channel_id=1, replica_groups={{0,2,4,6,8,10,12,14},{1,3,5,7,9,11,13,15},{16,18,20,22,24,26,28,30},{17..., dimensions={0} | all-to-all | bytes 1048576 | tf_op jit(solution)/shard_map/all_to_all | solution.py:219
  143.4 0.1 broadcast_in_dim.9
  143.5 14.3 %all_to_all.37 = f32[8,32,512]{2,1,0:T(8,128)S(1)} all-to-all(f32[8,32,512]{2,1,0:T(8,128)S(1)} %broadcast_in_dim.9), channel_id=1, replica_groups=mesh['row'=8,'col'=16] {'row'}, dimensions={0} | all-to-all | bytes 1048576 | tf_op jit(solution)/shard_map/all_to_all | solution.py:220
  157.8 0.0 copy-done.2
  157.9 0.9 broadcast_in_dim.10
  158.7 3.7 %all-to-all-start.4 = ((f32[8,32,512]{2,1,0:T(8,128)}), f32[8,32,512]{2,1,0:T(8,128)S(1)}, u32[]{:S(2)}, u32[]{:S(2)}) async-start(f32[8,32,512]{2,1,0:T(8,128)} %broadcast_in_dim.10), calls=%async_computation.4 | async-start | bytes 1048576 | tf_op jit(solution)/shard_map/all_to_all | solution.py:223
  162.4 0.0 collective-permute-done.3.refs_5_
  162.4 11.5 %spread_back.1 = bf16[8,512,256]{2,1,0:T(8,128)(2,1)} custom-call(s32[9]{0:T(128)} %get-tuple-element.12.refs_0_, s32[112]{0:T(128)} %get-tuple-element.13.refs_1_, s32[112]{0:T(128)} %get-tuple-element.14.refs_2_, bf16[80,256,256]{2,1,0:T(8,128)(2,1)} %bitcast.22, bf16[8,512,256]{2,1,0:T(8,128)(2,1)} %copy-done.2, ...), custom_call_target="tpu_custom_call" | custom-call | tf_op jit(solution)/shard_map/spread_back/pallas_call | solution.py:148
  173.9 0.0 all-to-all-done.4
  174.0 6.5 %all-to-all-start.6 = ((bf16[8,512,256]{2,1,0:T(8,128)(2,1)}), bf16[8,512,256]{2,1,0:T(8,128)(2,1)S(1)}, u32[]{:S(2)}, u32[]{:S(2)}) async-start(bf16[8,512,256]{2,1,0:T(8,128)(2,1)} %spread_back.1), calls=%async_computation.6 | async-start | bytes 4194304 | tf_op jit(solution)/shard_map/all_to_all | solution.py:211
  180.4 0.0 collective-permute-start.2
  180.4 2.0 collective-permute-done.2
  182.4 2.4 %maximum_select_fusion = f32[512,512]{1,0:T(8,128)} fusion(f32[256,512]{1,0:T(8,128)} %collective-permute-done.2, f32[256,512]{1,0:T(8,128)S(1)} %bitcast.24, pred[]{:T(512)S(6)} %eq.3), kind=kLoop, calls=%fused_computation.4 | loop fusion | flops 786432 | bytes 2097153 | tf_op jit(solution)/shard_map/jit(_where)/select_n | solution.py:231
  184.8 21.0 %all-to-all-done.6 = bf16[8,512,256]{2,1,0:T(8,128)(2,1)S(1)} async-done(((bf16[8,512,256]{2,1,0:T(8,128)(2,1)}), bf16[8,512,256]{2,1,0:T(8,128)(2,1)S(1)}, u32[]{:S(2)}, u32[]{:S(2)}) %all-to-all-start.6) | async-done | bytes 2097184 | tf_op jit(solution)/shard_map/all_to_all | solution.py:211
  205.8 0.4 reduce_sum.45
  206.2 0.8 copy.14
  (7 shorter events, 0.1 us)
Async XLA Ops:
  0.6 93.5 %copy-start = (bf16[512,512]{1,0:T(8,128)(2,1)S(1)}, bf16[512,512]{1,0:T(8,128)(2,1)}, u32[]{:S(2)}) copy-start(bf16[512,512]{1,0:T(8,128)(2,1)} %param.12) | copy-start | bytes 1572868
  3.2 7.8 %copy-start.5 = (s32[1,1,80]{2,1,0:T(1,128)S(1)}, s32[1,1,80]{2,1,0:T(1,128)}, u32[]{:S(2)}) copy-start(s32[1,1,80]{2,1,0:T(1,128)} %param.8) | copy-start | bytes 964
  3.2 35.6 %all-to-all-start = ((bf16[8,256,512]{2,1,0:T(8,128)(2,1)}), bf16[8,256,512]{2,1,0:T(8,128)(2,1)S(1)}, u32[]{:S(2)}, u32[]{:S(2)}) async-start(bf16[8,256,512]{2,1,0:T(8,128)(2,1)} %broadcast_in_dim.8), calls=%async_computation | async-start | bytes 4194304 | tf_op jit(solution)/shard_map/all_to_all | solution.py:184
  38.7 1.3 copy-start.1
  48.3 9.9 %collective-permute-start = (bf16[8,256,512]{2,1,0:T(8,128)(2,1)}, bf16[8,256,512]{2,1,0:T(8,128)(2,1)S(1)}, u32[]{:S(2)}, u32[]{:S(2)}) collective-permute-start(bf16[8,256,512]{2,1,0:T(8,128)(2,1)} %spread.3), channel_id=1, source_target_pairs={{0,1},{1,0},{2,3},{3,2},{4,5},{5,4},{6,7},{7,6},{8,9},{9,8},{10,11... | collective-permute-start | bytes 6291464 | tf_op jit(solution)/shard_map/ppermute | solution.py:186
  94.1 1.1 copy-start.4
  95.2 2.0 copy-start.6
  97.2 30.7 %all-to-all-start.5 = ((bf16[8,512,256]{2,1,0:T(8,128)(2,1)}), bf16[8,512,256]{2,1,0:T(8,128)(2,1)S(1)}, u32[]{:S(2)}, u32[]{:S(2)}) async-start(bf16[8,512,256]{2,1,0:T(8,128)(2,1)} %broadcast_in_dim.11), calls=%async_computation.5 | async-start | bytes 4194304 | tf_op jit(solution)/shard_map/all_to_all | solution.py:202
  102.7 1.1 copy-start.3
  103.8 24.1 %collective-permute-start.1 = (f32[256,512]{1,0:T(8,128)}, f32[256,512]{1,0:T(8,128)S(1)}, u32[]{:S(2)}, u32[]{:S(2)}) collective-permute-start(f32[256,512]{1,0:T(8,128)} %dynamic-slice_bitcast_fusion), channel_id=1, source_target_pairs={{0,1},{1,0},{2,3},{3,2},{4,5},{5,4},{6,7},{7,6},{8,9},{9,8},{10,11... | collective-permute-start | bytes 1572872 | tf_op jit(solution)/shard_map/ppermute | solution.py:217
  127.9 29.9 %copy-start.2 = (bf16[8,512,256]{2,1,0:T(8,128)(2,1)}, bf16[8,512,256]{2,1,0:T(8,128)(2,1)S(1)}, u32[]{:S(2)}) copy-start(bf16[8,512,256]{2,1,0:T(8,128)(2,1)S(1)} %all-to-all-done.5.refs_4_) | copy-start | bytes 6291460
  127.9 34.5 %collective-permute-start.3 = (bf16[8,512,256]{2,1,0:T(8,128)(2,1)S(1)}, bf16[8,512,256]{2,1,0:T(8,128)(2,1)}, u32[]{:S(2)}, u32[]{:S(2)}) collective-permute-start(bf16[8,512,256]{2,1,0:T(8,128)(2,1)S(1)} %all-to-all-done.5.refs_4_), channel_id=1, source_target_pairs={{0,1},{1,0},{2,3},{3,2},{4,5},{5,4},{6,7},{7,6},{8,9},{9,8},{10,11... | collective-permute-start | bytes 6291464 | tf_op jit(solution)/shard_map/ppermute | solution.py:209
  158.7 15.2 %all-to-all-start.4 = ((f32[8,32,512]{2,1,0:T(8,128)}), f32[8,32,512]{2,1,0:T(8,128)S(1)}, u32[]{:S(2)}, u32[]{:S(2)}) async-start(f32[8,32,512]{2,1,0:T(8,128)} %broadcast_in_dim.10), calls=%async_computation.4 | async-start | bytes 1048576 | tf_op jit(solution)/shard_map/all_to_all | solution.py:223
  174.0 31.8 %all-to-all-start.6 = ((bf16[8,512,256]{2,1,0:T(8,128)(2,1)}), bf16[8,512,256]{2,1,0:T(8,128)(2,1)S(1)}, u32[]{:S(2)}, u32[]{:S(2)}) async-start(bf16[8,512,256]{2,1,0:T(8,128)(2,1)} %spread_back.1), calls=%async_computation.6 | async-start | bytes 4194304 | tf_op jit(solution)/shard_map/all_to_all | solution.py:211
  180.4 2.0 collective-permute-start.2

commit v2 on v0

v2 whole, which is shorter than its diff:
```python
import jax
import jax.numpy as jnp
from jax import lax
from jax.experimental import pallas as pl
from jax.experimental.pallas import tpu as pltpu
from jax.sharding import PartitionSpec as P

BF = jnp.bfloat16
F32 = jnp.float32
GROUP = 2
RING = 4
CHUNKS = 8
SMEM = pl.BlockSpec(memory_space=pltpu.SMEM)
VMEM = pl.BlockSpec(memory_space=pltpu.VMEM)
HBM = pl.BlockSpec(memory_space=pltpu.HBM)


def room(total, dests):
    return total + dests * GROUP


def list_tiles(dest, source, count, total, dests, blank, table, fill):
    slots = dests + 1
    srcs = slots + room(total, dests)
    for d in range(dests):
        fill[d] = 0

    def tally(t, carry):
        fill[dest[t]] = fill[dest[t]] + 1
        return carry

    lax.fori_loop(0, count, tally, 0)

    def place(d, pos):
        table[d] = pos
        groups = jnp.maximum(lax.div(fill[d] + (GROUP - 1), GROUP), 1)
        fill[d] = pos * GROUP
        for k in range(GROUP):
            last = (pos + groups - 1) * GROUP + k
            table[slots + last] = 0
            table[srcs + last] = blank
        return pos + groups

    table[dests] = lax.fori_loop(0, dests, place, 0)

    def put(t, carry):
        d = dest[t]
        p = fill[d]
        fill[d] = p + 1
        table[slots + p] = t
        table[srcs + p] = source[t]
        return carry

    lax.fori_loop(0, count, put, 0)


def tile_copies(tiles, held, count, sem):
    total = tiles.shape[0]
    chunk = -(-total // CHUNKS)
    cuts = [(at, min(chunk, total - at)) for at in range(0, total, chunk)]
    copies = [
        pltpu.make_async_copy(tiles.at[pl.ds(at, n)], held.at[pl.ds(at, n)], sem.at[k])
        for k, (at, n) in enumerate(cuts)
    ]
    for (at, _), copy in zip(cuts, copies):
        pl.when(at < count)(copy.start)

    def wait():
        for (at, _), copy in zip(cuts, copies):
            pl.when(at < count)(copy.wait)

    return wait


def schedule(fdest, fsource, bdest, bsource, count, tiles, row_tiles, col_tiles):
    total = fdest.shape[0]

    def body(fd, fr, bd, br, n, tiles, forward, backward, held, fill, sem):
        wait = tile_copies(tiles, held, n[0], sem)
        list_tiles(fd, fr, n[0], total, row_tiles, col_tiles, forward, fill)
        list_tiles(bd, br, n[0], total, col_tiles, row_tiles, backward, fill)
        wait()

    def table(dests):
        return jax.ShapeDtypeStruct((dests + 1 + 2 * room(total, dests),), jnp.int32)

    return pl.pallas_call(
        body,
        in_specs=[SMEM] * 5 + [HBM],
        out_specs=[SMEM] * 2 + [VMEM],
        out_shape=[
            table(row_tiles),
            table(col_tiles),
            jax.ShapeDtypeStruct(tiles.shape, tiles.dtype),
        ],
        scratch_shapes=[
            pltpu.SMEM((max(row_tiles, col_tiles),), jnp.int32),
            pltpu.SemaphoreType.DMA((CHUNKS,)),
        ],
        compiler_params=pltpu.CompilerParams(vmem_limit_bytes=1024 * 1024),
        name="schedule",
    )(fdest, fsource, bdest, bsource, count, tiles)


def spread(table, tiles, sources, dests, start, outs, transposed):
    total, size = tiles.shape[:2]
    slots = dests + 1
    srcs = slots + room(total, dests)
    block = sources[0].shape
    n_in, n_out = len(sources), len(outs)
    groups_max = -(-n_in // GROUP)
    given = sum(outs)

    def body(*refs):
        table, tiles = refs[:2]
        ins = refs[2 : 2 + n_in]
        results = refs[2 + n_in : 2 + n_in + n_out]
        src, stage = refs[2 + n_in + n_out :]
        for k, ref in enumerate(ins):
            src[k] = ref[...]
        src[n_in] = jnp.zeros(block, BF)

        def product(p, n):
            held = [tiles[table[slots + p + k]] for k in range(n)]
            met = [src[table[srcs + p + k]] for k in range(n)]
            left, right = (met, held) if transposed else (held, met)
            return jnp.dot(
                jnp.concatenate(left, 1),
                jnp.concatenate(right, 0),
                preferred_element_type=F32,
            )

        def one(k, carry):
            lo = table[start + k]
            groups = table[start + k + 1] - lo
            for n in range(1, groups_max + 1):

                @pl.when(groups == n)
                def _():
                    stage[k] = product(lo * GROUP, n * GROUP).astype(BF)

            return carry

        lax.fori_loop(0, given, one, 0)
        at = 0
        for result, n in zip(results, outs):
            result[...] = stage[at : at + n] if n > 1 else stage[at]
            at += n

    flops = 2 * total * size * block[0] * block[1] * given // dests
    shapes = [((n,) if n > 1 else ()) + block for n in outs]
    return pl.pallas_call(
        body,
        in_specs=[SMEM] + [VMEM] * (1 + n_in),
        out_specs=[VMEM] * n_out,
        out_shape=[jax.ShapeDtypeStruct(s, BF) for s in shapes],
        scratch_shapes=[
            pltpu.VMEM((n_in + 1,) + block, BF),
            pltpu.VMEM((given,) + block, BF),
        ],
        compiler_params=pltpu.CompilerParams(vmem_limit_bytes=12 * 1024 * 1024),
        cost_estimate=pl.CostEstimate(
            flops=flops * 20, transcendentals=0, bytes_accessed=2 * total * size * size
        ),
        name="spread_back" if transposed else "spread",
    )(table, tiles, *sources)


def add_pairs(kept, met):
    n = kept.shape[0]

    def body(a, b, *outs):
        for k in range(n):
            outs[k][...] = a[k] + b[k]

    return pl.pallas_call(
        body,
        in_specs=[VMEM] * 2,
        out_specs=[VMEM] * n,
        out_shape=[jax.ShapeDtypeStruct(kept.shape[1:], BF)] * n,
        compiler_params=pltpu.CompilerParams(vmem_limit_bytes=1024 * 1024),
        name="add_pairs",
    )(kept, met)


def gather(block, axis, pair, step, between):
    far = lax.ppermute(block, axis, pair)
    near2 = lax.ppermute(block, axis, step(2))
    near1 = lax.ppermute(block, axis, step(3))
    near3 = lax.ppermute(block, axis, step(1))
    near2 = between(near2)
    far1 = lax.ppermute(far, axis, step(3))
    far3 = lax.ppermute(far, axis, step(1))
    far2 = lax.ppermute(near2, axis, pair)
    return [block, near1, near2, near3, far, far1, far2, far3]


def scatter(own, far, axis, pair, step):
    up = lax.ppermute(far[1], axis, step(1))
    down = lax.ppermute(far[3], axis, step(3))
    across = lax.ppermute(far[2], axis, pair)
    near1 = lax.ppermute(own[1], axis, step(1))
    near3 = lax.ppermute(own[3], axis, step(3))
    for_pair = far[0].astype(F32) + up.astype(F32) + down.astype(F32)
    for_two = own[2].astype(F32) + across.astype(F32)
    near2 = lax.ppermute(for_two.astype(BF), axis, step(2))
    met = lax.ppermute(for_pair.astype(BF), axis, pair)
    terms = [own[0], near1, near3, near2, met]
    return sum(t.astype(F32) for t in terms)


def local(adj_tiles, tile_rows, tile_cols, tile_counts, features, weight, node_grad):
    tiles = adj_tiles[0, 0]
    rows = tile_rows[0, 0]
    cols = tile_cols[0, 0]
    size = tiles.shape[1]
    row_devices = lax.axis_size("row")
    col_devices = lax.axis_size("col")
    half = col_devices // 2
    row_at = lax.axis_index("row")
    col_at = lax.axis_index("col")
    x_at, yh_at = row_at & 3, row_at >> 2
    core, z_at, yl_at = col_at & 1, (col_at >> 1) & 3, col_at >> 3
    places = (
        [core, 1 - core],
        [(z_at + k) & 3 for k in range(RING)],
        [yl_at, 1 - yl_at],
        ((RING - z_at) & 3) * (features.shape[1] // (2 * RING)),
        jnp.full((8, 128), core, jnp.int32),
        jnp.full((8, 128), yl_at, jnp.int32),
    )
    features, places = lax.optimization_barrier((features, places))
    tiles = pltpu.with_memory_space_constraint(tiles, pltpu.HBM)

    def along_x(k):
        return [(i, (i & 4) | ((i + k) & 3)) for i in range(row_devices)]

    def along_z(k):
        return [(i, (i & 9) | ((i + 2 * k) & 6)) for i in range(col_devices)]

    yh_swap = [(i, i ^ 4) for i in range(row_devices)]
    yl_swap = [(i, i ^ 8) for i in range(col_devices)]
    swap = [(i, i ^ 1) for i in range(col_devices)]

    r_ring, r_pair, r_core = ((rows >> 1) - z_at) & 3, (rows >> 3) ^ yl_at, (rows & 1) ^ core
    c_ring, c_pair = (cols - x_at) & 3, (cols >> 2) ^ yh_at
    lists = schedule(
        r_ring + 4 * (1 - r_core) + 8 * (1 - r_pair),
        c_ring + 4 * c_pair,
        c_ring + 4 * (1 - c_pair),
        r_ring + 4 * r_pair + 8 * r_core,
        tile_counts[0],
        tiles,
        col_devices,
        row_devices,
    )
    tied = []

    def meanwhile(near2):
        out, near2 = lax.optimization_barrier((lists, near2))
        tied.append(out)
        return near2

    column = gather(features, "row", yh_swap, along_x, meanwhile)
    forward, backward, held = tied.pop()
    pairs = []
    for start in (0, half):
        sent, kept = spread(forward, held, column, col_devices, start, (RING, RING), False)
        pairs.append(add_pairs(kept, lax.ppermute(sent, "col", swap)))
    agg = scatter(pairs[1], pairs[0], "col", yl_swap, along_z).astype(BF)

    pre = jnp.dot(agg, weight, preferred_element_type=F32)
    node_out = jax.nn.silu(pre).astype(BF)
    sigma = jax.nn.sigmoid(pre)
    dpre = (node_grad.astype(F32) * sigma * (1.0 + pre * (1.0 - sigma))).astype(BF)
    dagg = lax.dot_general(
        weight, dpre, (((1,), (1,)), ((), ())), preferred_element_type=F32
    ).astype(BF)
    scale = 1.0 / jnp.sqrt(jnp.float32(size * row_devices * col_devices))


    own = gather(dagg, "col", yl_swap, along_z, lambda near2: near2)
    other = [lax.ppermute(b, "col", swap) for b in own]
    term = lax.dot_general(agg, dpre, (((0,), (0,)), ((), ())), preferred_element_type=F32)
    backs = [
        spread(backward, held, own + other, row_devices, start, (1,) * RING, True)
        for start in (0, RING)
    ]
    feature_grad = scatter(backs[1], backs[0], "row", yh_swap, along_x).T.astype(BF)

    cores, rings, halves, turn, core_is, yl_is = places

    def split(block, n):
        return block.reshape((n, block.shape[0] // n) + block.shape[1:])

    def pick(cut, at):
        return lax.dynamic_index_in_dim(cut, at, 0, False, allow_negative_indices=False)

    cut = split(term * scale, 2)
    share = pick(cut, cores[0]) + lax.ppermute(pick(cut, cores[1]), "col", swap)
    cut = split(share, RING)
    share = pick(cut, rings[0]) + sum(
        lax.ppermute(pick(cut, rings[k]), "col", along_z(k)) for k in (2, 1, 3)
    )
    cut = split(share, 2)
    share = pick(cut, halves[0]) + lax.ppermute(pick(cut, halves[1]), "col", yl_swap)
    share = share + sum(lax.ppermute(share, "row", along_x(k)) for k in (2, 1, 3))
    share = share + lax.ppermute(share, "row", yh_swap)

    def doubled(block, bit, perm):
        met = lax.ppermute(block, "col", perm)
        return jnp.where(
            bit[0:1, 0:1] == 0,
            jnp.concatenate([block, met], 0),
            jnp.concatenate([met, block], 0),
        )

    share = doubled(share, yl_is, yl_swap)
    ring = [share] + [lax.ppermute(share, "col", along_z(RING - k)) for k in (1, 2, 3)]
    share = lax.dynamic_slice_in_dim(
        jnp.concatenate(ring + ring, 0), turn, RING * share.shape[0], allow_negative_indices=False
    )
    weight_grad = doubled(share, core_is, swap)
    return node_out, weight_grad, feature_grad


def solution(mesh):
    in_specs = (
        P("row", "col", None, None, None),
        P("row", "col", None),
        P("row", "col", None),
        P("row", "col"),
        P(("col", "row"), None),
        P(),
        P(("row", "col"), None),
    )
    out_specs = (P(("row", "col"), None), P(), P(("col", "row"), None))
    return jax.shard_map(local, mesh=mesh, in_specs=in_specs, out_specs=out_specs, check_vma=False)
```

time: 630 us -> 140 us (0.22)
  waiting for transfers between devices: 305 us -> 55.5 us
  matrix products: 190 us -> 2.05 us
  local copies, waits for them, and re-layouts: 110 us -> 3.41 us
  starting transfers between devices: 0.2 us -> 56.6 us
  Pallas kernels: 0 us -> 15.9 us
  between operations: 14.5 us -> 3.04 us
    reduce_scatter x2 -> x0, waiting for transfers between devices: 199 us -> none  [the longest x1 102 us: local(): lax.psum_scatter(partial_value.reshape(row_tiles * tile_size, feat_width)...]
    dot_general x19 -> x3, matrix products: 190 us -> 2.05 us  [the longest x1 1.09 us: local(): pre = jnp.dot(agg, weight, preferred_element_type=F32)]
    all_gather x2 -> x0, waiting for transfers between devices: 93.7 us -> none  [the longest x1 59.1 us: local(): column_feats = lax.all_gather(features, 'row', axis=0, tiled=True)]
    gather x40 -> x0, local copies, waits for them, and re-layouts: 89.3 us -> none  [the longest x8 42.7 us: add_block(): tile_block = jnp.take(cell_tiles, slot_ids, axis=0)]
    ppermute x0 -> x52, starting transfers between devices: none -> 56.6 us  [the longest x2 7.37 us: scatter(): down = lax.ppermute(far[3], axis, step(3))]
    ppermute x0 -> x52, waiting for transfers between devices: none -> 55.5 us  [the longest x2 6.87 us: gather(): far1 = lax.ppermute(far, axis, step(3))]
    pallas_call x0 -> x7, Pallas kernels: none -> 15.9 us  [the longest x4 12.3 us: spread(): pl.pallas_call(body, in_specs=[SMEM] + [VMEM] * (1 + n_in), out_specs=[VM...]
    psum x1 -> x0, waiting for transfers between devices: 11.3 us -> none  [local(): weight_grad = lax.psum(weight_term, ('row', 'col'))]
  transfers between devices with their start and end apart: 5 -> 52, of which waited for: 5 -> 19; matrix products, arithmetic and copies ran while one was open for 23% -> 3% of each run, Pallas kernels for 0% -> 9%
where the time goes in v2:
time: 140 us; the launch traced here: 139 us
  starting transfers between devices  56.6 us (40%)
  waiting for transfers between devices  55.5 us (40%)
  Pallas kernels  15.9 us (11%)
  local copies, waits for them, and re-layouts  3.41 us (2%)
  between operations  3.04 us (2%)
  other arithmetic  2.67 us (2%)
  matrix products  2.05 us (1%)
    pallas_call x4, Pallas kernels, spread(): pl.pallas_call(body, in_specs=[SMEM] + [VMEM] * (1 + n_in), out_specs=[VM...  12.3 us
    ppermute x2, starting transfers between devices, scatter(): down = lax.ppermute(far[3], axis, step(3))  7.37 us
    ppermute x2, waiting for transfers between devices, gather(): far1 = lax.ppermute(far, axis, step(3))  6.87 us
    ppermute x2, waiting for transfers between devices, scatter(): near3 = lax.ppermute(own[3], axis, step(3))  6.76 us
    ppermute x2, starting transfers between devices, gather(): far1 = lax.ppermute(far, axis, step(3))  6.39 us
    ppermute x2, starting transfers between devices, scatter(): near3 = lax.ppermute(own[3], axis, step(3))  5.64 us
    ppermute x3, waiting for transfers between devices, local(): lax.ppermute(share, 'col', along_z(RING - k))  4.91 us
    ppermute x2, starting transfers between devices, gather(): near2 = lax.ppermute(block, axis, step(2))  4.84 us
  transfers between devices with their start and end apart: 52, of which 19 were waited for; matrix products, arithmetic and copies ran while one was open for 3% of the time, Pallas kernels for 9%

profile of v2, /device:TPU:0, one launch (start us, length us, event | category | flops | bytes accessed | tf_op | source)
XLA Modules:
  0.0 139.2 jit_solution(6806374177203620452)
XLA Ops:
  1.3 3.1 %collective-permute-start = (bf16[256,512]{1,0:T(8,128)(2,1)}, bf16[256,512]{1,0:T(8,128)(2,1)S(1)}, u32[]{:S(2)}, u32[]{:S(2)}) collective-permute-start(bf16[256,512]{1,0:T(8,128)(2,1)} %refs_2_.1), channel_id=1, source_target_pairs={{0,32},{16,48},{32,0},{48,16},{64,96},{80,112},{96,64},{112,80},{1... | collective-permute-start | bytes 786440 | tf_op jit(solution)/shard_map/ppermute | solution.py:188
  4.4 3.2 %collective-permute-start.3 = (bf16[256,512]{1,0:T(8,128)(2,1)}, bf16[256,512]{1,0:T(8,128)(2,1)S(1)}, u32[]{:S(2)}, u32[]{:S(2)}) collective-permute-start(bf16[256,512]{1,0:T(8,128)(2,1)} %refs_2_.1), channel_id=1, source_target_pairs={{0,64},{16,80},{32,96},{48,112},{64,0},{80,16},{96,32},{112,48},{1... | collective-permute-start | bytes 786440 | tf_op jit(solution)/shard_map/ppermute | solution.py:187
  7.6 1.1 collective-permute-start.1
  8.7 0.9 collective-permute-start.2
  10.9 3.4 %schedule.1 = (s32[241]{0:T(256)S(1)}, s32[201]{0:T(256)S(1)}, bf16[80,256,256]{2,1,0:T(8,128)(2,1)S(1)}) custom-call(s32[80]{0:T(128)S(1)} %get-tuple-element.90.fd, s32[80]{0:T(128)S(1)} %get-tuple-element.95.fr, s32[80]{0:T(128)S(1)} %get-tuple-element.96.bd, s32[80]{0:T(128)S(1)} %get-tuple-element.89.br, s32[1]{0:T(128)} %bitcast.39.n, ...), custom_call_target="tpu_custom_call" | custom-call | tf_op jit(solution)/shard_map/schedule/pallas_call | solution.py:87
  14.3 2.8 %collective-permute-start.4 = (bf16[256,512]{1,0:T(8,128)(2,1)S(1)}, bf16[256,512]{1,0:T(8,128)(2,1)S(1)}, u32[]{:S(2)}, u32[]{:S(2)}) collective-permute-start(bf16[256,512]{1,0:T(8,128)(2,1)S(1)} %collective-permute-done.3.refs_6_), channel_id=1, source_target_pairs={{0,48},{16,0},{32,16},{48,32},{64,112},{80,64},{96,80},{112,96},{1... | collective-permute-start | bytes 786440 | tf_op jit(solution)/shard_map/ppermute | solution.py:192
  17.1 1.1 collective-permute-start.5
  18.3 0.8 collective-permute-start.6
  19.1 3.3 %collective-permute-done.4.refs_7_ = bf16[256,512]{1,0:T(8,128)(2,1)S(1)} collective-permute-done((bf16[256,512]{1,0:T(8,128)(2,1)S(1)}, bf16[256,512]{1,0:T(8,128)(2,1)S(1)}, u32[]{:S(2)}, u32[]{:S(2)}) %collective-permute-start.4) | collective-permute-done | bytes 262176 | tf_op jit(solution)/shard_map/ppermute | solution.py:192
  22.4 2.6 %collective-permute-done.5.refs_8_ = bf16[256,512]{1,0:T(8,128)(2,1)S(1)} collective-permute-done((bf16[256,512]{1,0:T(8,128)(2,1)S(1)}, bf16[256,512]{1,0:T(8,128)(2,1)S(1)}, u32[]{:S(2)}, u32[]{:S(2)}) %collective-permute-start.5) | collective-permute-done | bytes 262176 | tf_op jit(solution)/shard_map/ppermute | solution.py:194
  25.0 0.8 collective-permute-done.6.refs_9_
  25.8 3.4 %spread.3 = (bf16[4,256,512]{2,1,0:T(8,128)(2,1)S(1)}, bf16[4,256,512]{2,1,0:T(8,128)(2,1)S(1)}) custom-call(s32[241]{0:T(256)S(1)} %get-tuple-element.46.refs_0_, bf16[80,256,256]{2,1,0:T(8,128)(2,1)S(1)} %get-tuple-element.47.refs_1_, bf16[256,512]{1,0:T(8,128)(2,1)S(1)} %copy-done.1, bf16[256,512]{1,0:T(8,128)(2,1)S(1)} %collective-permute-done.1.refs_3_, ...), custom_call_target="tpu_custom_call" | custom-call | flops 53687091200 | bytes 10485760 | tf_op jit(solution)/shard_map/spread/pallas_call | solution.py:152
  29.4 3.6 %spread.2 = (bf16[4,256,512]{2,1,0:T(8,128)(2,1)S(1)}, bf16[4,256,512]{2,1,0:T(8,128)(2,1)S(1)}) custom-call(s32[241]{0:T(256)S(1)} %get-tuple-element.46.refs_0_, bf16[80,256,256]{2,1,0:T(8,128)(2,1)S(1)} %get-tuple-element.47.refs_1_, bf16[256,512]{1,0:T(8,128)(2,1)S(1)} %copy-done.1, bf16[256,512]{1,0:T(8,128)(2,1)S(1)} %collective-permute-done.1.refs_3_, ...), custom_call_target="tpu_custom_call" | custom-call | flops 53687091200 | bytes 10485760 | tf_op jit(solution)/shard_map/spread/pallas_call | solution.py:152
  33.0 1.2 collective-permute-start.7
  34.3 7.3 %collective-permute-start.14 = (bf16[256,512]{1,0:T(8,128)(2,1)S(1)}, bf16[256,512]{1,0:T(8,128)(2,1)S(1)}, u32[]{:S(2)}, u32[]{:S(2)}) collective-permute-start(bf16[256,512]{1,0:T(8,128)(2,1)S(1)} %get-tuple-element.60), channel_id=1, source_target_pairs={{0,6},{1,7},{2,0},{3,1},{4,2},{5,3},{6,4},{7,5},{8,14},{9,15},{10,... | collective-permute-start | bytes 786440 | tf_op jit(solution)/shard_map/ppermute | solution.py:200
  41.8 3.3 %collective-permute-start.9 = (bf16[256,512]{1,0:T(8,128)(2,1)S(1)}, bf16[256,512]{1,0:T(8,128)(2,1)S(1)}, u32[]{:S(2)}, u32[]{:S(2)}) collective-permute-start(bf16[256,512]{1,0:T(8,128)(2,1)S(1)} %get-tuple-element.53), channel_id=1, source_target_pairs={{0,6},{1,7},{2,0},{3,1},{4,2},{5,3},{6,4},{7,5},{8,14},{9,15},{10,... | collective-permute-start | bytes 786440 | tf_op jit(solution)/shard_map/ppermute | solution.py:203
  45.1 3.2 %collective-permute-done.14 = bf16[256,512]{1,0:T(8,128)(2,1)S(1)} collective-permute-done((bf16[256,512]{1,0:T(8,128)(2,1)S(1)}, bf16[256,512]{1,0:T(8,128)(2,1)S(1)}, u32[]{:S(2)}, u32[]{:S(2)}) %collective-permute-start.14) | collective-permute-done | bytes 262176 | tf_op jit(solution)/shard_map/ppermute | solution.py:200
  48.3 3.7 %collective-permute-done.13 = bf16[256,512]{1,0:T(8,128)(2,1)S(1)} collective-permute-done((bf16[256,512]{1,0:T(8,128)(2,1)S(1)}, bf16[256,512]{1,0:T(8,128)(2,1)S(1)}, u32[]{:S(2)}, u32[]{:S(2)}) %collective-permute-start.13) | collective-permute-done | bytes 262176 | tf_op jit(solution)/shard_map/ppermute | solution.py:199
  52.4 6.8 %collective-permute-done.9 = bf16[256,512]{1,0:T(8,128)(2,1)S(1)} collective-permute-done((bf16[256,512]{1,0:T(8,128)(2,1)S(1)}, bf16[256,512]{1,0:T(8,128)(2,1)S(1)}, u32[]{:S(2)}, u32[]{:S(2)}) %collective-permute-start.9) | collective-permute-done | bytes 262176 | tf_op jit(solution)/shard_map/ppermute | solution.py:203
  59.1 3.4 %collective-permute-done.8 = bf16[256,512]{1,0:T(8,128)(2,1)S(1)} collective-permute-done((bf16[256,512]{1,0:T(8,128)(2,1)S(1)}, bf16[256,512]{1,0:T(8,128)(2,1)S(1)}, u32[]{:S(2)}, u32[]{:S(2)}) %collective-permute-start.8) | collective-permute-done | bytes 262176 | tf_op jit(solution)/shard_map/ppermute | solution.py:202
  62.7 1.1 multiply_convert_fusion.1
  64.4 1.9 %collective-permute-done.16 = f32[256,512]{1,0:T(8,128)S(1)} collective-permute-done((f32[256,512]{1,0:T(8,128)S(1)}, f32[256,512]{1,0:T(8,128)S(1)}, u32[]{:S(2)}, u32[]{:S(2)}) %collective-permute-start.16) | collective-permute-done | bytes 524320 | tf_op jit(solution)/shard_map/ppermute | solution.py:300
  67.2 1.4 collective-permute-start.18
  69.1 2.7 %collective-permute-start.30 = (bf16[512,256]{1,0:T(8,128)(2,1)S(1)}, bf16[512,256]{1,0:T(8,128)(2,1)S(1)}, u32[]{:S(2)}, u32[]{:S(2)}) collective-permute-start(bf16[512,256]{1,0:T(8,128)(2,1)S(1)} %fusion.refs_2_), channel_id=1, source_target_pairs={{0,6},{1,7},{2,0},{3,1},{4,2},{5,3},{6,4},{7,5},{8,14},{9,15},{10,... | collective-permute-start | bytes 786440 | tf_op jit(solution)/shard_map/ppermute | solution.py:189
  71.8 1.7 %collective-permute-start.31 = (bf16[512,256]{1,0:T(8,128)(2,1)S(1)}, bf16[512,256]{1,0:T(8,128)(2,1)S(1)}, u32[]{:S(2)}, u32[]{:S(2)}) collective-permute-start(bf16[512,256]{1,0:T(8,128)(2,1)S(1)} %fusion.refs_2_), channel_id=1, source_target_pairs={{0,4},{1,5},{2,6},{3,7},{4,0},{5,1},{6,2},{7,3},{8,12},{9,13},{10,... | collective-permute-start | bytes 786440 | tf_op jit(solution)/shard_map/ppermute | solution.py:188
  73.5 1.1 collective-permute-start.32
  74.9 2.5 %collective-permute-done.18 = f32[64,512]{1,0:T(8,128)S(1)} collective-permute-done((f32[64,512]{1,0:T(8,128)S(1)}, f32[64,512]{1,0:T(8,128)S(1)}, u32[]{:S(2)}, u32[]{:S(2)}) %collective-permute-start.18) | collective-permute-done | bytes 131104 | tf_op jit(solution)/shard_map/ppermute | solution.py:303
  77.5 3.9 %collective-permute-done.30.refs_3_ = bf16[512,256]{1,0:T(8,128)(2,1)S(1)} collective-permute-done((bf16[512,256]{1,0:T(8,128)(2,1)S(1)}, bf16[512,256]{1,0:T(8,128)(2,1)S(1)}, u32[]{:S(2)}, u32[]{:S(2)}) %collective-permute-start.30) | collective-permute-done | bytes 262176 | tf_op jit(solution)/shard_map/ppermute | solution.py:189
  81.6 3.6 %collective-permute-start.34 = (bf16[512,256]{1,0:T(8,128)(2,1)S(1)}, bf16[512,256]{1,0:T(8,128)(2,1)S(1)}, u32[]{:S(2)}, u32[]{:S(2)}) collective-permute-start(bf16[512,256]{1,0:T(8,128)(2,1)S(1)} %collective-permute-done.33.refs_6_), channel_id=1, source_target_pairs={{0,6},{1,7},{2,0},{3,1},{4,2},{5,3},{6,4},{7,5},{8,14},{9,15},{10,... | collective-permute-start | bytes 786440 | tf_op jit(solution)/shard_map/ppermute | solution.py:192
  85.6 2.1 %collective-permute-done.32.refs_5_ = bf16[512,256]{1,0:T(8,128)(2,1)S(1)} collective-permute-done((bf16[512,256]{1,0:T(8,128)(2,1)S(1)}, bf16[512,256]{1,0:T(8,128)(2,1)S(1)}, u32[]{:S(2)}, u32[]{:S(2)}) %collective-permute-start.32) | collective-permute-done | bytes 262176 | tf_op jit(solution)/shard_map/ppermute | solution.py:190
  88.3 3.5 %collective-permute-done.34.refs_7_ = bf16[512,256]{1,0:T(8,128)(2,1)S(1)} collective-permute-done((bf16[512,256]{1,0:T(8,128)(2,1)S(1)}, bf16[512,256]{1,0:T(8,128)(2,1)S(1)}, u32[]{:S(2)}, u32[]{:S(2)}) %collective-permute-start.34) | collective-permute-done | bytes 262176 | tf_op jit(solution)/shard_map/ppermute | solution.py:192
  91.9 1.6 %collective-permute-start.21 = (f32[32,512]{1,0:T(8,128)S(1)}, f32[32,512]{1,0:T(8,128)S(1)}, u32[]{:S(2)}, u32[]{:S(2)}) collective-permute-start(f32[32,512]{1,0:T(8,128)S(1)} %bitcast_add_fusion.2), channel_id=1, source_target_pairs={{0,32},{16,48},{32,0},{48,16},{64,96},{80,112},{96,64},{112,80},{1... | collective-permute-start | bytes 196616 | tf_op jit(solution)/shard_map/ppermute | solution.py:307
  93.5 3.6 %collective-permute-done.36.refs_9_ = bf16[512,256]{1,0:T(8,128)(2,1)S(1)} collective-permute-done((bf16[512,256]{1,0:T(8,128)(2,1)S(1)}, bf16[512,256]{1,0:T(8,128)(2,1)S(1)}, u32[]{:S(2)}, u32[]{:S(2)}) %collective-permute-start.36) | collective-permute-done | bytes 262176 | tf_op jit(solution)/shard_map/ppermute | solution.py:193
  98.1 4.4 %collective-permute-done.22 = f32[32,512]{1,0:T(8,128)S(1)} collective-permute-done((f32[32,512]{1,0:T(8,128)S(1)}, f32[32,512]{1,0:T(8,128)S(1)}, u32[]{:S(2)}, u32[]{:S(2)}) %collective-permute-start.22) | collective-permute-done | bytes 65568 | tf_op jit(solution)/shard_map/ppermute | solution.py:307
  103.8 1.2 collective-permute-start.24
  105.0 2.9 %spread_back.3 = (bf16[512,256]{1,0:T(8,128)(2,1)S(1)}, bf16[512,256]{1,0:T(8,128)(2,1)S(1)}, bf16[512,256]{1,0:T(8,128)(2,1)S(1)}, bf16[512,256]{1,0:T(8,128)(2,1)S(1)}) custom-call(s32[201]{0:T(256)S(1)} %get-tuple-element.72.refs_0_, bf16[80,256,256]{2,1,0:T(8,128)(2,1)S(1)} %get-tuple-element.47.refs_1_, bf16[512,256]{1,0:T(8,128)(2,1)S(1)} %fusion.refs_2_, ...), custom_call_target="tpu_custom_call" | custom-call | flops 53687091200 | bytes 10485760 | tf_op jit(solution)/shard_map/spread_back/pallas_call | solution.py:152
  108.0 2.0 %collective-permute-start.49 = (bf16[512,256]{1,0:T(8,128)(2,1)S(1)}, bf16[512,256]{1,0:T(8,128)(2,1)S(1)}, u32[]{:S(2)}, u32[]{:S(2)}) collective-permute-start(bf16[512,256]{1,0:T(8,128)(2,1)S(1)} %get-tuple-element.79), channel_id=1, source_target_pairs={{0,16},{16,32},{32,48},{48,0},{64,80},{80,96},{96,112},{112,64},{1... | collective-permute-start | bytes 786440 | tf_op jit(solution)/shard_map/ppermute | solution.py:199
  110.0 2.5 %collective-permute-start.47 = (bf16[512,256]{1,0:T(8,128)(2,1)S(1)}, bf16[512,256]{1,0:T(8,128)(2,1)S(1)}, u32[]{:S(2)}, u32[]{:S(2)}) collective-permute-start(bf16[512,256]{1,0:T(8,128)(2,1)S(1)} %get-tuple-element.77), channel_id=1, source_target_pairs={{0,64},{16,80},{32,96},{48,112},{64,0},{80,16},{96,32},{112,48},{1... | collective-permute-start | bytes 786440 | tf_op jit(solution)/shard_map/ppermute | solution.py:201
  113.2 2.4 %spread_back.2 = (bf16[512,256]{1,0:T(8,128)(2,1)S(1)}, bf16[512,256]{1,0:T(8,128)(2,1)S(1)}, bf16[512,256]{1,0:T(8,128)(2,1)S(1)}, bf16[512,256]{1,0:T(8,128)(2,1)S(1)}) custom-call(s32[201]{0:T(256)S(1)} %get-tuple-element.72.refs_0_, bf16[80,256,256]{2,1,0:T(8,128)(2,1)S(1)} %get-tuple-element.47.refs_1_, bf16[512,256]{1,0:T(8,128)(2,1)S(1)} %fusion.refs_2_, ...), custom_call_target="tpu_custom_call" | custom-call | flops 53687091200 | bytes 10485760 | tf_op jit(solution)/shard_map/spread_back/pallas_call | solution.py:152
  115.7 2.3 %collective-permute-start.46 = (bf16[512,256]{1,0:T(8,128)(2,1)S(1)}, bf16[512,256]{1,0:T(8,128)(2,1)S(1)}, u32[]{:S(2)}, u32[]{:S(2)}) collective-permute-start(bf16[512,256]{1,0:T(8,128)(2,1)S(1)} %get-tuple-element.75), channel_id=1, source_target_pairs={{0,48},{16,0},{32,16},{48,32},{64,112},{80,64},{96,80},{112,96},{1... | collective-permute-start | bytes 786440 | tf_op jit(solution)/shard_map/ppermute | solution.py:203
  118.0 2.6 %collective-permute-done.25 = f32[32,512]{1,0:T(8,128)S(1)} collective-permute-done((f32[32,512]{1,0:T(8,128)S(1)}, f32[32,512]{1,0:T(8,128)S(1)}, u32[]{:S(2)}, u32[]{:S(2)}) %collective-permute-start.25) | collective-permute-done | bytes 65568 | tf_op jit(solution)/shard_map/ppermute | solution.py:311
  121.6 1.6 %collective-permute-start.28 = (f32[64,512]{1,0:T(8,128)S(1)}, f32[64,512]{1,0:T(8,128)S(1)}, u32[]{:S(2)}, u32[]{:S(2)}) collective-permute-start(f32[64,512]{1,0:T(8,128)S(1)} %get-tuple-element.85), channel_id=1, source_target_pairs={{0,2},{1,3},{2,4},{3,5},{4,6},{5,7},{6,0},{7,1},{8,10},{9,11},{10,... | collective-permute-start | bytes 393224 | tf_op jit(solution)/shard_map/ppermute | solution.py:319
  123.3 4.1 %collective-permute-done.26 = f32[64,512]{1,0:T(8,128)S(1)} collective-permute-done((f32[64,512]{1,0:T(8,128)S(1)}, f32[64,512]{1,0:T(8,128)S(1)}, u32[]{:S(2)}, u32[]{:S(2)}) %collective-permute-start.26) | collective-permute-done | bytes 131104 | tf_op jit(solution)/shard_map/ppermute | solution.py:319
  128.8 3.9 %collective-permute-start.48 = (bf16[512,256]{1,0:T(8,128)(2,1)S(1)}, bf16[512,256]{1,0:T(8,128)(2,1)S(1)}, u32[]{:S(2)}, u32[]{:S(2)}) collective-permute-start(bf16[512,256]{1,0:T(8,128)(2,1)S(1)} %add_convert_fusion.2), channel_id=1, source_target_pairs={{0,32},{16,48},{32,0},{48,16},{64,96},{80,112},{96,64},{112,80},{1... | collective-permute-start | bytes 786440 | tf_op jit(solution)/shard_map/ppermute | solution.py:206
  133.0 1.2 slice.6
  135.3 1.8 %collective-permute-done.48 = bf16[512,256]{1,0:T(8,128)(2,1)S(1)} collective-permute-done((bf16[512,256]{1,0:T(8,128)(2,1)S(1)}, bf16[512,256]{1,0:T(8,128)(2,1)S(1)}, u32[]{:S(2)}, u32[]{:S(2)}) %collective-permute-start.48) | collective-permute-done | bytes 262176 | tf_op jit(solution)/shard_map/ppermute | solution.py:206
  137.2 0.8 copy.11
  138.1 1.1 maximum_select_fusion
  (102 shorter events, 11.4 us)
Async XLA Ops:
  1.3 13.0 %collective-permute-start = (bf16[256,512]{1,0:T(8,128)(2,1)}, bf16[256,512]{1,0:T(8,128)(2,1)S(1)}, u32[]{:S(2)}, u32[]{:S(2)}) collective-permute-start(bf16[256,512]{1,0:T(8,128)(2,1)} %refs_2_.1), channel_id=1, source_target_pairs={{0,32},{16,48},{32,0},{48,16},{64,96},{80,112},{96,64},{112,80},{1... | collective-permute-start | bytes 786440 | tf_op jit(solution)/shard_map/ppermute | solution.py:188
  4.4 9.9 %collective-permute-start.3 = (bf16[256,512]{1,0:T(8,128)(2,1)}, bf16[256,512]{1,0:T(8,128)(2,1)S(1)}, u32[]{:S(2)}, u32[]{:S(2)}) collective-permute-start(bf16[256,512]{1,0:T(8,128)(2,1)} %refs_2_.1), channel_id=1, source_target_pairs={{0,64},{16,80},{32,96},{48,112},{64,0},{80,16},{96,32},{112,48},{1... | collective-permute-start | bytes 786440 | tf_op jit(solution)/shard_map/ppermute | solution.py:187
  7.6 11.5 %collective-permute-start.1 = (bf16[256,512]{1,0:T(8,128)(2,1)}, bf16[256,512]{1,0:T(8,128)(2,1)S(1)}, u32[]{:S(2)}, u32[]{:S(2)}) collective-permute-start(bf16[256,512]{1,0:T(8,128)(2,1)} %refs_2_.1), channel_id=1, source_target_pairs={{0,48},{16,0},{32,16},{48,32},{64,112},{80,64},{96,80},{112,96},{1... | collective-permute-start | bytes 786440 | tf_op jit(solution)/shard_map/ppermute | solution.py:189
  8.7 10.4 %collective-permute-start.2 = (bf16[256,512]{1,0:T(8,128)(2,1)}, bf16[256,512]{1,0:T(8,128)(2,1)S(1)}, u32[]{:S(2)}, u32[]{:S(2)}) collective-permute-start(bf16[256,512]{1,0:T(8,128)(2,1)} %refs_2_.1), channel_id=1, source_target_pairs={{0,16},{16,32},{32,48},{48,0},{64,80},{80,96},{96,112},{112,64},{1... | collective-permute-start | bytes 786440 | tf_op jit(solution)/shard_map/ppermute | solution.py:190
  14.3 8.1 %collective-permute-start.4 = (bf16[256,512]{1,0:T(8,128)(2,1)S(1)}, bf16[256,512]{1,0:T(8,128)(2,1)S(1)}, u32[]{:S(2)}, u32[]{:S(2)}) collective-permute-start(bf16[256,512]{1,0:T(8,128)(2,1)S(1)} %collective-permute-done.3.refs_6_), channel_id=1, source_target_pairs={{0,48},{16,0},{32,16},{48,32},{64,112},{80,64},{96,80},{112,96},{1... | collective-permute-start | bytes 786440 | tf_op jit(solution)/shard_map/ppermute | solution.py:192
  17.1 7.9 %collective-permute-start.5 = (bf16[256,512]{1,0:T(8,128)(2,1)S(1)}, bf16[256,512]{1,0:T(8,128)(2,1)S(1)}, u32[]{:S(2)}, u32[]{:S(2)}) collective-permute-start(bf16[256,512]{1,0:T(8,128)(2,1)S(1)} %collective-permute-done.refs_4_), channel_id=1, source_target_pairs={{0,64},{16,80},{32,96},{48,112},{64,0},{80,16},{96,32},{112,48},{1... | collective-permute-start | bytes 786440 | tf_op jit(solution)/shard_map/ppermute | solution.py:194
  18.3 7.6 %collective-permute-start.6 = (bf16[256,512]{1,0:T(8,128)(2,1)S(1)}, bf16[256,512]{1,0:T(8,128)(2,1)S(1)}, u32[]{:S(2)}, u32[]{:S(2)}) collective-permute-start(bf16[256,512]{1,0:T(8,128)(2,1)S(1)} %collective-permute-done.3.refs_6_), channel_id=1, source_target_pairs={{0,16},{16,32},{32,48},{48,0},{64,80},{80,96},{96,112},{112,64},{1... | collective-permute-start | bytes 786440 | tf_op jit(solution)/shard_map/ppermute | solution.py:193
  33.0 8.7 %collective-permute-start.7 = (bf16[4,256,512]{2,1,0:T(8,128)(2,1)S(1)}, bf16[4,256,512]{2,1,0:T(8,128)(2,1)S(1)}, u32[]{:S(2)}, u32[]{:S(2)}) collective-permute-start(bf16[4,256,512]{2,1,0:T(8,128)(2,1)S(1)} %get-tuple-element.50), channel_id=1, source_target_pairs={{0,1},{1,0},{2,3},{3,2},{4,5},{5,4},{6,7},{7,6},{8,9},{9,8},{10,11... | collective-permute-start | bytes 3145736 | tf_op jit(solution)/shard_map/ppermute | solution.py:269
  34.3 13.9 %collective-permute-start.14 = (bf16[256,512]{1,0:T(8,128)(2,1)S(1)}, bf16[256,512]{1,0:T(8,128)(2,1)S(1)}, u32[]{:S(2)}, u32[]{:S(2)}) collective-permute-start(bf16[256,512]{1,0:T(8,128)(2,1)S(1)} %get-tuple-element.60), channel_id=1, source_target_pairs={{0,6},{1,7},{2,0},{3,1},{4,2},{5,3},{6,4},{7,5},{8,14},{9,15},{10,... | collective-permute-start | bytes 786440 | tf_op jit(solution)/shard_map/ppermute | solution.py:200
  41.6 10.4 %collective-permute-start.13 = (bf16[256,512]{1,0:T(8,128)(2,1)S(1)}, bf16[256,512]{1,0:T(8,128)(2,1)S(1)}, u32[]{:S(2)}, u32[]{:S(2)}) collective-permute-start(bf16[256,512]{1,0:T(8,128)(2,1)S(1)} %get-tuple-element.59), channel_id=1, source_target_pairs={{0,2},{1,3},{2,4},{3,5},{4,6},{5,7},{6,0},{7,1},{8,10},{9,11},{10,... | collective-permute-start | bytes 786440 | tf_op jit(solution)/shard_map/ppermute | solution.py:199
  41.6 10.6 %collective-permute-start.11 = (bf16[256,512]{1,0:T(8,128)(2,1)S(1)}, bf16[256,512]{1,0:T(8,128)(2,1)S(1)}, u32[]{:S(2)}, u32[]{:S(2)}) collective-permute-start(bf16[256,512]{1,0:T(8,128)(2,1)S(1)} %get-tuple-element.57), channel_id=1, source_target_pairs={{0,8},{1,9},{2,10},{3,11},{4,12},{5,13},{6,14},{7,15},{8,0},{9,1},... | collective-permute-start | bytes 786440 | tf_op jit(solution)/shard_map/ppermute | solution.py:201
  41.8 17.4 %collective-permute-start.9 = (bf16[256,512]{1,0:T(8,128)(2,1)S(1)}, bf16[256,512]{1,0:T(8,128)(2,1)S(1)}, u32[]{:S(2)}, u32[]{:S(2)}) collective-permute-start(bf16[256,512]{1,0:T(8,128)(2,1)S(1)} %get-tuple-element.53), channel_id=1, source_target_pairs={{0,6},{1,7},{2,0},{3,1},{4,2},{5,3},{6,4},{7,5},{8,14},{9,15},{10,... | collective-permute-start | bytes 786440 | tf_op jit(solution)/shard_map/ppermute | solution.py:203
  45.1 17.4 %collective-permute-start.8 = (bf16[256,512]{1,0:T(8,128)(2,1)S(1)}, bf16[256,512]{1,0:T(8,128)(2,1)S(1)}, u32[]{:S(2)}, u32[]{:S(2)}) collective-permute-start(bf16[256,512]{1,0:T(8,128)(2,1)S(1)} %get-tuple-element.52), channel_id=1, source_target_pairs={{0,2},{1,3},{2,4},{3,5},{4,6},{5,7},{6,0},{7,1},{8,10},{9,11},{10,... | collective-permute-start | bytes 786440 | tf_op jit(solution)/shard_map/ppermute | solution.py:202
  52.1 10.4 %collective-permute-start.15 = (bf16[256,512]{1,0:T(8,128)(2,1)S(1)}, bf16[256,512]{1,0:T(8,128)(2,1)S(1)}, u32[]{:S(2)}, u32[]{:S(2)}) collective-permute-start(bf16[256,512]{1,0:T(8,128)(2,1)S(1)} %add_convert_fusion.4), channel_id=1, source_target_pairs={{0,8},{1,9},{2,10},{3,11},{4,12},{5,13},{6,14},{7,15},{8,0},{9,1},... | collective-permute-start | bytes 786440 | tf_op jit(solution)/shard_map/ppermute | solution.py:207
  52.3 10.2 %collective-permute-start.12 = (bf16[256,512]{1,0:T(8,128)(2,1)S(1)}, bf16[256,512]{1,0:T(8,128)(2,1)S(1)}, u32[]{:S(2)}, u32[]{:S(2)}) collective-permute-start(bf16[256,512]{1,0:T(8,128)(2,1)S(1)} %add_convert_fusion.5), channel_id=1, source_target_pairs={{0,4},{1,5},{2,6},{3,7},{4,0},{5,1},{6,2},{7,3},{8,12},{9,13},{10,... | collective-permute-start | bytes 786440 | tf_op jit(solution)/shard_map/ppermute | solution.py:206
  66.5 7.1 %collective-permute-start.19 = (f32[64,512]{1,0:T(8,128)S(1)}, f32[64,512]{1,0:T(8,128)S(1)}, u32[]{:S(2)}, u32[]{:S(2)}) collective-permute-start(f32[64,512]{1,0:T(8,128)S(1)} %get-tuple-element.87), channel_id=1, source_target_pairs={{0,6},{1,7},{2,0},{3,1},{4,2},{5,3},{6,4},{7,5},{8,14},{9,15},{10,... | collective-permute-start | bytes 393224 | tf_op jit(solution)/shard_map/ppermute | solution.py:303
  66.8 7.9 %collective-permute-start.17 = (f32[64,512]{1,0:T(8,128)S(1)}, f32[64,512]{1,0:T(8,128)S(1)}, u32[]{:S(2)}, u32[]{:S(2)}) collective-permute-start(f32[64,512]{1,0:T(8,128)S(1)} %get-tuple-element.88), channel_id=1, source_target_pairs={{0,4},{1,5},{2,6},{3,7},{4,0},{5,1},{6,2},{7,3},{8,12},{9,13},{10,... | collective-permute-start | bytes 393224 | tf_op jit(solution)/shard_map/ppermute | solution.py:303
  67.2 10.2 %collective-permute-start.18 = (f32[64,512]{1,0:T(8,128)S(1)}, f32[64,512]{1,0:T(8,128)S(1)}, u32[]{:S(2)}, u32[]{:S(2)}) collective-permute-start(f32[64,512]{1,0:T(8,128)S(1)} %get-tuple-element.86), channel_id=1, source_target_pairs={{0,2},{1,3},{2,4},{3,5},{4,6},{5,7},{6,0},{7,1},{8,10},{9,11},{10,... | collective-permute-start | bytes 393224 | tf_op jit(solution)/shard_map/ppermute | solution.py:303
  69.1 12.3 %collective-permute-start.30 = (bf16[512,256]{1,0:T(8,128)(2,1)S(1)}, bf16[512,256]{1,0:T(8,128)(2,1)S(1)}, u32[]{:S(2)}, u32[]{:S(2)}) collective-permute-start(bf16[512,256]{1,0:T(8,128)(2,1)S(1)} %fusion.refs_2_), channel_id=1, source_target_pairs={{0,6},{1,7},{2,0},{3,1},{4,2},{5,3},{6,4},{7,5},{8,14},{9,15},{10,... | collective-permute-start | bytes 786440 | tf_op jit(solution)/shard_map/ppermute | solution.py:189
  71.8 13.3 %collective-permute-start.31 = (bf16[512,256]{1,0:T(8,128)(2,1)S(1)}, bf16[512,256]{1,0:T(8,128)(2,1)S(1)}, u32[]{:S(2)}, u32[]{:S(2)}) collective-permute-start(bf16[512,256]{1,0:T(8,128)(2,1)S(1)} %fusion.refs_2_), channel_id=1, source_target_pairs={{0,4},{1,5},{2,6},{3,7},{4,0},{5,1},{6,2},{7,3},{8,12},{9,13},{10,... | collective-permute-start | bytes 786440 | tf_op jit(solution)/shard_map/ppermute | solution.py:188
  73.5 14.2 %collective-permute-start.32 = (bf16[512,256]{1,0:T(8,128)(2,1)S(1)}, bf16[512,256]{1,0:T(8,128)(2,1)S(1)}, u32[]{:S(2)}, u32[]{:S(2)}) collective-permute-start(bf16[512,256]{1,0:T(8,128)(2,1)S(1)} %fusion.refs_2_), channel_id=1, source_target_pairs={{0,2},{1,3},{2,4},{3,5},{4,6},{5,7},{6,0},{7,1},{8,10},{9,11},{10,... | collective-permute-start | bytes 786440 | tf_op jit(solution)/shard_map/ppermute | solution.py:190
  74.7 6.9 %collective-permute-start.33 = (bf16[512,256]{1,0:T(8,128)(2,1)S(1)}, bf16[512,256]{1,0:T(8,128)(2,1)S(1)}, u32[]{:S(2)}, u32[]{:S(2)}) collective-permute-start(bf16[512,256]{1,0:T(8,128)(2,1)S(1)} %fusion.refs_2_), channel_id=1, source_target_pairs={{0,8},{1,9},{2,10},{3,11},{4,12},{5,13},{6,14},{7,15},{8,0},{9,1},... | collective-permute-start | bytes 786440 | tf_op jit(solution)/shard_map/ppermute | solution.py:187
  77.4 10.3 %collective-permute-start.37 = (bf16[512,256]{1,0:T(8,128)(2,1)S(1)}, bf16[512,256]{1,0:T(8,128)(2,1)S(1)}, u32[]{:S(2)}, u32[]{:S(2)}) collective-permute-start(bf16[512,256]{1,0:T(8,128)(2,1)S(1)} %fusion.refs_2_), channel_id=1, source_target_pairs={{0,1},{1,0},{2,3},{3,2},{4,5},{5,4},{6,7},{7,6},{8,9},{9,8},{10,11... | collective-permute-start | bytes 786440 | tf_op jit(solution)/shard_map/ppermute | solution.py:283
  81.4 6.4 %collective-permute-start.20 = (f32[32,512]{1,0:T(8,128)S(1)}, f32[32,512]{1,0:T(8,128)S(1)}, u32[]{:S(2)}, u32[]{:S(2)}) collective-permute-start(f32[32,512]{1,0:T(8,128)S(1)} %dynamic-slice_bitcast_fusion.4), channel_id=1, source_target_pairs={{0,8},{1,9},{2,10},{3,11},{4,12},{5,13},{6,14},{7,15},{8,0},{9,1},... | collective-permute-start | bytes 196616 | tf_op jit(solution)/shard_map/ppermute | solution.py:306
  81.6 10.2 %collective-permute-start.34 = (bf16[512,256]{1,0:T(8,128)(2,1)S(1)}, bf16[512,256]{1,0:T(8,128)(2,1)S(1)}, u32[]{:S(2)}, u32[]{:S(2)}) collective-permute-start(bf16[512,256]{1,0:T(8,128)(2,1)S(1)} %collective-permute-done.33.refs_6_), channel_id=1, source_target_pairs={{0,6},{1,7},{2,0},{3,1},{4,2},{5,3},{6,4},{7,5},{8,14},{9,15},{10,... | collective-permute-start | bytes 786440 | tf_op jit(solution)/shard_map/ppermute | solution.py:192
  85.1 6.8 %collective-permute-start.35 = (bf16[512,256]{1,0:T(8,128)(2,1)S(1)}, bf16[512,256]{1,0:T(8,128)(2,1)S(1)}, u32[]{:S(2)}, u32[]{:S(2)}) collective-permute-start(bf16[512,256]{1,0:T(8,128)(2,1)S(1)} %collective-permute-done.31.refs_4_), channel_id=1, source_target_pairs={{0,8},{1,9},{2,10},{3,11},{4,12},{5,13},{6,14},{7,15},{8,0},{9,1},... | collective-permute-start | bytes 786440 | tf_op jit(solution)/shard_map/ppermute | solution.py:194
  87.7 9.4 %collective-permute-start.36 = (bf16[512,256]{1,0:T(8,128)(2,1)S(1)}, bf16[512,256]{1,0:T(8,128)(2,1)S(1)}, u32[]{:S(2)}, u32[]{:S(2)}) collective-permute-start(bf16[512,256]{1,0:T(8,128)(2,1)S(1)} %collective-permute-done.33.refs_6_), channel_id=1, source_target_pairs={{0,2},{1,3},{2,4},{3,5},{4,6},{5,7},{6,0},{7,1},{8,10},{9,11},{10,... | collective-permute-start | bytes 786440 | tf_op jit(solution)/shard_map/ppermute | solution.py:193
  87.7 9.4 %collective-permute-start.39 = (bf16[512,256]{1,0:T(8,128)(2,1)S(1)}, bf16[512,256]{1,0:T(8,128)(2,1)S(1)}, u32[]{:S(2)}, u32[]{:S(2)}) collective-permute-start(bf16[512,256]{1,0:T(8,128)(2,1)S(1)} %collective-permute-done.31.refs_4_), channel_id=1, source_target_pairs={{0,1},{1,0},{2,3},{3,2},{4,5},{5,4},{6,7},{7,6},{8,9},{9,8},{10,11... | collective-permute-start | bytes 786440 | tf_op jit(solution)/shard_map/ppermute | solution.py:283
  87.8 9.4 %collective-permute-start.38 = (bf16[512,256]{1,0:T(8,128)(2,1)S(1)}, bf16[512,256]{1,0:T(8,128)(2,1)S(1)}, u32[]{:S(2)}, u32[]{:S(2)}) collective-permute-start(bf16[512,256]{1,0:T(8,128)(2,1)S(1)} %collective-permute-done.30.refs_3_), channel_id=1, source_target_pairs={{0,1},{1,0},{2,3},{3,2},{4,5},{5,4},{6,7},{7,6},{8,9},{9,8},{10,11... | collective-permute-start | bytes 786440 | tf_op jit(solution)/shard_map/ppermute | solution.py:283
  91.8 5.8 %collective-permute-start.23 = (f32[32,512]{1,0:T(8,128)S(1)}, f32[32,512]{1,0:T(8,128)S(1)}, u32[]{:S(2)}, u32[]{:S(2)}) collective-permute-start(f32[32,512]{1,0:T(8,128)S(1)} %bitcast_add_fusion.2), channel_id=1, source_target_pairs={{0,48},{16,0},{32,16},{48,32},{64,112},{80,64},{96,80},{112,96},{1... | collective-permute-start | bytes 196616 | tf_op jit(solution)/shard_map/ppermute | solution.py:307
  91.9 5.8 %collective-permute-start.21 = (f32[32,512]{1,0:T(8,128)S(1)}, f32[32,512]{1,0:T(8,128)S(1)}, u32[]{:S(2)}, u32[]{:S(2)}) collective-permute-start(f32[32,512]{1,0:T(8,128)S(1)} %bitcast_add_fusion.2), channel_id=1, source_target_pairs={{0,32},{16,48},{32,0},{48,16},{64,96},{80,112},{96,64},{112,80},{1... | collective-permute-start | bytes 196616 | tf_op jit(solution)/shard_map/ppermute | solution.py:307
  97.1 5.5 %collective-permute-start.22 = (f32[32,512]{1,0:T(8,128)S(1)}, f32[32,512]{1,0:T(8,128)S(1)}, u32[]{:S(2)}, u32[]{:S(2)}) collective-permute-start(f32[32,512]{1,0:T(8,128)S(1)} %bitcast_add_fusion.2), channel_id=1, source_target_pairs={{0,16},{16,32},{32,48},{48,0},{64,80},{80,96},{96,112},{112,64},{1... | collective-permute-start | bytes 196616 | tf_op jit(solution)/shard_map/ppermute | solution.py:307
  97.1 7.8 %collective-permute-start.41 = (bf16[512,256]{1,0:T(8,128)(2,1)S(1)}, bf16[512,256]{1,0:T(8,128)(2,1)S(1)}, u32[]{:S(2)}, u32[]{:S(2)}) collective-permute-start(bf16[512,256]{1,0:T(8,128)(2,1)S(1)} %collective-permute-done.33.refs_6_), channel_id=1, source_target_pairs={{0,1},{1,0},{2,3},{3,2},{4,5},{5,4},{6,7},{7,6},{8,9},{9,8},{10,11... | collective-permute-start | bytes 786440 | tf_op jit(solution)/shard_map/ppermute | solution.py:283
  97.1 6.7 %collective-permute-start.40 = (bf16[512,256]{1,0:T(8,128)(2,1)S(1)}, bf16[512,256]{1,0:T(8,128)(2,1)S(1)}, u32[]{:S(2)}, u32[]{:S(2)}) collective-permute-start(bf16[512,256]{1,0:T(8,128)(2,1)S(1)} %collective-permute-done.32.refs_5_), channel_id=1, source_target_pairs={{0,1},{1,0},{2,3},{3,2},{4,5},{5,4},{6,7},{7,6},{8,9},{9,8},{10,11... | collective-permute-start | bytes 786440 | tf_op jit(solution)/shard_map/ppermute | solution.py:283
  97.6 7.3 %collective-permute-start.42 = (bf16[512,256]{1,0:T(8,128)(2,1)S(1)}, bf16[512,256]{1,0:T(8,128)(2,1)S(1)}, u32[]{:S(2)}, u32[]{:S(2)}) collective-permute-start(bf16[512,256]{1,0:T(8,128)(2,1)S(1)} %collective-permute-done.34.refs_7_), channel_id=1, source_target_pairs={{0,1},{1,0},{2,3},{3,2},{4,5},{5,4},{6,7},{7,6},{8,9},{9,8},{10,11... | collective-permute-start | bytes 786440 | tf_op jit(solution)/shard_map/ppermute | solution.py:283
  97.7 7.2 %collective-permute-start.43 = (bf16[512,256]{1,0:T(8,128)(2,1)S(1)}, bf16[512,256]{1,0:T(8,128)(2,1)S(1)}, u32[]{:S(2)}, u32[]{:S(2)}) collective-permute-start(bf16[512,256]{1,0:T(8,128)(2,1)S(1)} %collective-permute-done.35.refs_8_), channel_id=1, source_target_pairs={{0,1},{1,0},{2,3},{3,2},{4,5},{5,4},{6,7},{7,6},{8,9},{9,8},{10,11... | collective-permute-start | bytes 786440 | tf_op jit(solution)/shard_map/ppermute | solution.py:283
  103.8 8.6 %collective-permute-start.24 = (f32[32,512]{1,0:T(8,128)S(1)}, f32[32,512]{1,0:T(8,128)S(1)}, u32[]{:S(2)}, u32[]{:S(2)}) collective-permute-start(f32[32,512]{1,0:T(8,128)S(1)} %add_add_fusion), channel_id=1, source_target_pairs={{0,64},{16,80},{32,96},{48,112},{64,0},{80,16},{96,32},{112,48},{1... | collective-permute-start | bytes 196616 | tf_op jit(solution)/shard_map/ppermute | solution.py:308
  107.9 13.0 %collective-permute-start.50 = (bf16[512,256]{1,0:T(8,128)(2,1)S(1)}, bf16[512,256]{1,0:T(8,128)(2,1)S(1)}, u32[]{:S(2)}, u32[]{:S(2)}) collective-permute-start(bf16[512,256]{1,0:T(8,128)(2,1)S(1)} %get-tuple-element.80), channel_id=1, source_target_pairs={{0,48},{16,0},{32,16},{48,32},{64,112},{80,64},{96,80},{112,96},{1... | collective-permute-start | bytes 786440 | tf_op jit(solution)/shard_map/ppermute | solution.py:200
  108.0 13.5 %collective-permute-start.49 = (bf16[512,256]{1,0:T(8,128)(2,1)S(1)}, bf16[512,256]{1,0:T(8,128)(2,1)S(1)}, u32[]{:S(2)}, u32[]{:S(2)}) collective-permute-start(bf16[512,256]{1,0:T(8,128)(2,1)S(1)} %get-tuple-element.79), channel_id=1, source_target_pairs={{0,16},{16,32},{32,48},{48,0},{64,80},{80,96},{96,112},{112,64},{1... | collective-permute-start | bytes 786440 | tf_op jit(solution)/shard_map/ppermute | solution.py:199
  110.0 11.6 %collective-permute-start.47 = (bf16[512,256]{1,0:T(8,128)(2,1)S(1)}, bf16[512,256]{1,0:T(8,128)(2,1)S(1)}, u32[]{:S(2)}, u32[]{:S(2)}) collective-permute-start(bf16[512,256]{1,0:T(8,128)(2,1)S(1)} %get-tuple-element.77), channel_id=1, source_target_pairs={{0,64},{16,80},{32,96},{48,112},{64,0},{80,16},{96,32},{112,48},{1... | collective-permute-start | bytes 786440 | tf_op jit(solution)/shard_map/ppermute | solution.py:201
  112.4 8.2 %collective-permute-start.25 = (f32[32,512]{1,0:T(8,128)S(1)}, f32[32,512]{1,0:T(8,128)S(1)}, u32[]{:S(2)}, u32[]{:S(2)}) collective-permute-start(f32[32,512]{1,0:T(8,128)S(1)} %add.130), channel_id=1, source_target_pairs={{0,8},{1,9},{2,10},{3,11},{4,12},{5,13},{6,14},{7,15},{8,0},{9,1},... | collective-permute-start | bytes 196616 | tf_op jit(solution)/shard_map/ppermute | solution.py:311
  115.7 19.2 %collective-permute-start.46 = (bf16[512,256]{1,0:T(8,128)(2,1)S(1)}, bf16[512,256]{1,0:T(8,128)(2,1)S(1)}, u32[]{:S(2)}, u32[]{:S(2)}) collective-permute-start(bf16[512,256]{1,0:T(8,128)(2,1)S(1)} %get-tuple-element.75), channel_id=1, source_target_pairs={{0,48},{16,0},{32,16},{48,32},{64,112},{80,64},{96,80},{112,96},{1... | collective-permute-start | bytes 786440 | tf_op jit(solution)/shard_map/ppermute | solution.py:203
  120.6 14.3 %collective-permute-start.45 = (bf16[512,256]{1,0:T(8,128)(2,1)S(1)}, bf16[512,256]{1,0:T(8,128)(2,1)S(1)}, u32[]{:S(2)}, u32[]{:S(2)}) collective-permute-start(bf16[512,256]{1,0:T(8,128)(2,1)S(1)} %get-tuple-element.74), channel_id=1, source_target_pairs={{0,16},{16,32},{32,48},{48,0},{64,80},{80,96},{96,112},{112,64},{1... | collective-permute-start | bytes 786440 | tf_op jit(solution)/shard_map/ppermute | solution.py:202
  120.9 6.5 %collective-permute-start.26 = (f32[64,512]{1,0:T(8,128)S(1)}, f32[64,512]{1,0:T(8,128)S(1)}, u32[]{:S(2)}, u32[]{:S(2)}) collective-permute-start(f32[64,512]{1,0:T(8,128)S(1)} %get-tuple-element.85), channel_id=1, source_target_pairs={{0,6},{1,7},{2,0},{3,1},{4,2},{5,3},{6,4},{7,5},{8,14},{9,15},{10,... | collective-permute-start | bytes 393224 | tf_op jit(solution)/shard_map/ppermute | solution.py:319
  121.5 7.4 %collective-permute-start.27 = (f32[64,512]{1,0:T(8,128)S(1)}, f32[64,512]{1,0:T(8,128)S(1)}, u32[]{:S(2)}, u32[]{:S(2)}) collective-permute-start(f32[64,512]{1,0:T(8,128)S(1)} %get-tuple-element.85), channel_id=1, source_target_pairs={{0,4},{1,5},{2,6},{3,7},{4,0},{5,1},{6,2},{7,3},{8,12},{9,13},{10,... | collective-permute-start | bytes 393224 | tf_op jit(solution)/shard_map/ppermute | solution.py:319
  121.6 11.1 %collective-permute-start.28 = (f32[64,512]{1,0:T(8,128)S(1)}, f32[64,512]{1,0:T(8,128)S(1)}, u32[]{:S(2)}, u32[]{:S(2)}) collective-permute-start(f32[64,512]{1,0:T(8,128)S(1)} %get-tuple-element.85), channel_id=1, source_target_pairs={{0,2},{1,3},{2,4},{3,5},{4,6},{5,7},{6,0},{7,1},{8,10},{9,11},{10,... | collective-permute-start | bytes 393224 | tf_op jit(solution)/shard_map/ppermute | solution.py:319
  127.4 7.9 %collective-permute-start.51 = (bf16[512,256]{1,0:T(8,128)(2,1)S(1)}, bf16[512,256]{1,0:T(8,128)(2,1)S(1)}, u32[]{:S(2)}, u32[]{:S(2)}) collective-permute-start(bf16[512,256]{1,0:T(8,128)(2,1)S(1)} %add_convert_fusion.1), channel_id=1, source_target_pairs={{0,64},{16,80},{32,96},{48,112},{64,0},{80,16},{96,32},{112,48},{1... | collective-permute-start | bytes 786440 | tf_op jit(solution)/shard_map/ppermute | solution.py:207
  128.8 8.2 %collective-permute-start.48 = (bf16[512,256]{1,0:T(8,128)(2,1)S(1)}, bf16[512,256]{1,0:T(8,128)(2,1)S(1)}, u32[]{:S(2)}, u32[]{:S(2)}) collective-permute-start(bf16[512,256]{1,0:T(8,128)(2,1)S(1)} %add_convert_fusion.2), channel_id=1, source_target_pairs={{0,32},{16,48},{32,0},{48,16},{64,96},{80,112},{96,64},{112,80},{1... | collective-permute-start | bytes 786440 | tf_op jit(solution)/shard_map/ppermute | solution.py:206
  (7 other events, 132.6 us)

commit v3 on v2

--- a/solution.py
+++ b/solution.py
@@ -195,6 +195,10 @@
     return [block, near1, near2, near3, far, far1, far2, far3]
 
 
+def after(value, events):
+    return lax.optimization_barrier((value, events))[0]
+
+
 def scatter(own, far, axis, pair, step):
     up = lax.ppermute(far[1], axis, step(1))
     down = lax.ppermute(far[3], axis, step(3))
@@ -206,7 +210,7 @@
     near2 = lax.ppermute(for_two.astype(BF), axis, step(2))
     met = lax.ppermute(for_pair.astype(BF), axis, pair)
     terms = [own[0], near1, near3, near2, met]
-    return sum(t.astype(F32) for t in terms)
+    return sum(t.astype(F32) for t in terms), (up, down, across), (near1, near3)
 
 
 def local(adj_tiles, tile_rows, tile_cols, tile_counts, features, weight, node_grad):
@@ -221,14 +225,10 @@
     col_at = lax.axis_index("col")
     x_at, yh_at = row_at & 3, row_at >> 2
     core, z_at, yl_at = col_at & 1, (col_at >> 1) & 3, col_at >> 3
-    places = (
-        [core, 1 - core],
-        [(z_at + k) & 3 for k in range(RING)],
-        [yl_at, 1 - yl_at],
-        ((RING - z_at) & 3) * (features.shape[1] // (2 * RING)),
-        jnp.full((8, 128), core, jnp.int32),
-        jnp.full((8, 128), yl_at, jnp.int32),
-    )
+    places = [
+        [bit, 1 - bit, (1 - bit) * (features.shape[1] >> (k + 1))]
+        for k, bit in enumerate((core, (z_at & 1) ^ (z_at >> 1), z_at >> 1))
+    ]
     features, places = lax.optimization_barrier((features, places))
     tiles = pltpu.with_memory_space_constraint(tiles, pltpu.HBM)
 
@@ -267,7 +267,8 @@
     for start in (0, half):
         sent, kept = spread(forward, held, column, col_devices, start, (RING, RING), False)
         pairs.append(add_pairs(kept, lax.ppermute(sent, "col", swap)))
-    agg = scatter(pairs[1], pairs[0], "col", yl_swap, along_z).astype(BF)
+    agg, _, _ = scatter(pairs[1], pairs[0], "col", yl_swap, along_z)
+    agg = agg.astype(BF)
 
     pre = jnp.dot(agg, weight, preferred_element_type=F32)
     node_out = jax.nn.silu(pre).astype(BF)
@@ -281,46 +282,49 @@
 
     own = gather(dagg, "col", yl_swap, along_z, lambda near2: near2)
     other = [lax.ppermute(b, "col", swap) for b in own]
-    term = lax.dot_general(agg, dpre, (((0,), (0,)), ((), ())), preferred_element_type=F32)
+    late_agg, late_dpre = after((agg, dpre), own[4])
+    term = lax.dot_general(
+        late_agg, late_dpre, (((0,), (0,)), ((), ())), preferred_element_type=F32
+    )
     backs = [
         spread(backward, held, own + other, row_devices, start, (1,) * RING, True)
         for start in (0, RING)
     ]
-    feature_grad = scatter(backs[1], backs[0], "row", yh_swap, along_x).T.astype(BF)
-
-    cores, rings, halves, turn, core_is, yl_is = places
-
-    def split(block, n):
-        return block.reshape((n, block.shape[0] // n) + block.shape[1:])
-
-    def pick(cut, at):
-        return lax.dynamic_index_in_dim(cut, at, 0, False, allow_negative_indices=False)
-
-    cut = split(term * scale, 2)
-    share = pick(cut, cores[0]) + lax.ppermute(pick(cut, cores[1]), "col", swap)
-    cut = split(share, RING)
-    share = pick(cut, rings[0]) + sum(
-        lax.ppermute(pick(cut, rings[k]), "col", along_z(k)) for k in (2, 1, 3)
-    )
-    cut = split(share, 2)
-    share = pick(cut, halves[0]) + lax.ppermute(pick(cut, halves[1]), "col", yl_swap)
-    share = share + sum(lax.ppermute(share, "row", along_x(k)) for k in (2, 1, 3))
-    share = share + lax.ppermute(share, "row", yh_swap)
-
-    def doubled(block, bit, perm):
-        met = lax.ppermute(block, "col", perm)
-        return jnp.where(
-            bit[0:1, 0:1] == 0,
-            jnp.concatenate([block, met], 0),
-            jnp.concatenate([met, block], 0),
+    summed, for_far, for_own = scatter(backs[1], backs[0], "row", yh_swap, along_x)
+    feature_grad = summed.T.astype(BF)
+
+    def flips(axis, bits):
+        n = row_devices if axis == "row" else col_devices
+        return axis, [(i, i ^ bits) for i in range(n)]
+
+    def halved(block, at, *way):
+        cut = block.reshape((2, block.shape[0] // 2) + block.shape[1:])
+        mine, yours = (
+            lax.dynamic_index_in_dim(cut, k, 0, False, allow_negative_indices=False) for k in at
         )
-
-    share = doubled(share, yl_is, yl_swap)
-    ring = [share] + [lax.ppermute(share, "col", along_z(RING - k)) for k in (1, 2, 3)]
-    share = lax.dynamic_slice_in_dim(
-        jnp.concatenate(ring + ring, 0), turn, RING * share.shape[0], allow_negative_indices=False
-    )
-    weight_grad = doubled(share, core_is, swap)
+        return mine + lax.ppermute(yours.astype(BF), *way).astype(F32)
+
+    def doubled(block, at, *way):
+        met = lax.ppermute(block, *way)
+        rows = block.shape[0]
+        both = jnp.concatenate([met, block, met], 0)
+        return lax.dynamic_slice_in_dim(both, at[2], 2 * rows, allow_negative_indices=False)
+
+    steps = list(zip(places, (1, 2, 6)))
+    share = term * scale
+    events = {2: own[5:], 4: backs[0], 6: (for_far, backs[1])}
+    for k, (at, bits) in enumerate(steps):
+        if k in events:
+            share = after(share, events[k])
+        share = halved(share, at[:2], *flips("col", bits))
+    for k, way in enumerate((("col", 8), ("row", 4), ("row", 1), ("row", 3)), len(steps)):
+        if k in events:
+            share = after(share, events[k])
+        share = share + lax.ppermute(share.astype(BF), *flips(*way)).astype(F32)
+    share = share.astype(BF)
+    for at, bits in reversed(steps):
+        share = doubled(share, at, *flips("col", bits))
+    weight_grad = share.astype(F32)
     return node_out, weight_grad, feature_grad
 
 

time: 140 us -> 138 us (0.986)
  starting transfers between devices: 56.6 us -> 47.9 us
  waiting for transfers between devices: 55.5 us -> 60.7 us
  Pallas kernels: 15.9 us -> 18.5 us
  local copies, waits for them, and re-layouts: 3.41 us -> 0.95 us
  other arithmetic: 2.67 us -> 4.32 us
    ppermute x2, waiting for transfers between devices: 6.76 us -> 0.01 us  [scatter(): near3 = lax.ppermute(own[3], axis, step(3))]
    ppermute x2, waiting for transfers between devices: 0.01 us -> 5.28 us  [gather(): far = lax.ppermute(block, axis, pair)]
    ppermute x2, waiting for transfers between devices: 3.38 us -> 8.27 us  [scatter(): near1 = lax.ppermute(own[1], axis, step(1))]
    ppermute x14 -> x10, waiting for transfers between devices: 16.3 us -> 20.9 us  [the longest x3 10.1 us: doubled(): met = lax.ppermute(block, *way)]
    ppermute x2, waiting for transfers between devices: 4.4 us -> 0.01 us  [gather(): far3 = lax.ppermute(far, axis, step(1))]
    ppermute x2, starting transfers between devices: 3.95 us -> 0.78 us  [scatter(): near2 = lax.ppermute(for_two.astype(BF), axis, step(2))]
    ppermute x2, starting transfers between devices: 0.71 us -> 3.58 us  [scatter(): met = lax.ppermute(for_pair.astype(BF), axis, pair)]
    ppermute x2, starting transfers between devices: 6.39 us -> 3.52 us  [gather(): far1 = lax.ppermute(far, axis, step(3))]
  transfers between devices with their start and end apart: 52 -> 48, of which waited for: 19 -> 18; matrix products, arithmetic and copies ran while one was open for 3% -> 2% of each run, Pallas kernels for 9% -> 11%
where the time goes in v3:
time: 138 us; the launch traced here: 136 us
  waiting for transfers between devices  60.7 us (44%)
  starting transfers between devices  47.9 us (35%)
  Pallas kernels  18.5 us (13%)
  other arithmetic  4.32 us (3%)
  matrix products  1.84 us (1%)
  between operations  1.74 us (1%)
    pallas_call x4, Pallas kernels, spread(): pl.pallas_call(body, in_specs=[SMEM] + [VMEM] * (1 + n_in), out_specs=[VM...  14.5 us
    ppermute x3, waiting for transfers between devices, doubled(): met = lax.ppermute(block, *way)  10.1 us
    ppermute x2, waiting for transfers between devices, gather(): far1 = lax.ppermute(far, axis, step(3))  9.62 us
    ppermute x2, waiting for transfers between devices, scatter(): near1 = lax.ppermute(own[1], axis, step(1))  8.27 us
    ppermute x4, starting transfers between devices, local(): share = share + lax.ppermute(share.astype(BF), *flips(*way)).astype(F32)  7.37 us
    ppermute x4, waiting for transfers between devices, local(): share = share + lax.ppermute(share.astype(BF), *flips(*way)).astype(F32)  6 us
    ppermute x2, starting transfers between devices, scatter(): down = lax.ppermute(far[3], axis, step(3))  5.76 us
    ppermute x2, waiting for transfers between devices, gather(): far = lax.ppermute(block, axis, pair)  5.28 us
  transfers between devices with their start and end apart: 48, of which 18 were waited for; matrix products, arithmetic and copies ran while one was open for 2% of the time, Pallas kernels for 11%

profile of v3, /device:TPU:0, one launch (start us, length us, event | category | flops | bytes accessed | tf_op | source)
XLA Modules:
  0.0 136.0 jit_solution(13400155113387089434)
XLA Ops:
  0.7 3.2 %collective-permute-start = (bf16[256,512]{1,0:T(8,128)(2,1)}, bf16[256,512]{1,0:T(8,128)(2,1)S(1)}, u32[]{:S(2)}, u32[]{:S(2)}) collective-permute-start(bf16[256,512]{1,0:T(8,128)(2,1)} %refs_2_.1), channel_id=1, source_target_pairs={{0,32},{16,48},{32,0},{48,16},{64,96},{80,112},{96,64},{112,80},{1... | collective-permute-start | bytes 786440 | tf_op jit(solution)/shard_map/ppermute | solution.py:188
  3.9 3.2 %collective-permute-start.3 = (bf16[256,512]{1,0:T(8,128)(2,1)}, bf16[256,512]{1,0:T(8,128)(2,1)S(1)}, u32[]{:S(2)}, u32[]{:S(2)}) collective-permute-start(bf16[256,512]{1,0:T(8,128)(2,1)} %refs_2_.1), channel_id=1, source_target_pairs={{0,64},{16,80},{32,96},{48,112},{64,0},{80,16},{96,32},{112,48},{1... | collective-permute-start | bytes 786440 | tf_op jit(solution)/shard_map/ppermute | solution.py:187
  7.1 1.1 collective-permute-start.1
  8.2 0.9 collective-permute-start.2
  10.4 3.8 %schedule.1 = (s32[241]{0:T(256)S(1)}, s32[201]{0:T(256)S(1)}, bf16[80,256,256]{2,1,0:T(8,128)(2,1)S(1)}) custom-call(s32[80]{0:T(128)S(1)} %get-tuple-element.93.fd, s32[80]{0:T(128)S(1)} %get-tuple-element.96.fr, s32[80]{0:T(128)S(1)} %get-tuple-element.97.bd, s32[80]{0:T(128)S(1)} %get-tuple-element.92.br, s32[1]{0:T(128)} %bitcast.39.n, ...), custom_call_target="tpu_custom_call" | custom-call | tf_op jit(solution)/shard_map/schedule/pallas_call | solution.py:87
  14.2 2.8 %collective-permute-start.4 = (bf16[256,512]{1,0:T(8,128)(2,1)S(1)}, bf16[256,512]{1,0:T(8,128)(2,1)S(1)}, u32[]{:S(2)}, u32[]{:S(2)}) collective-permute-start(bf16[256,512]{1,0:T(8,128)(2,1)S(1)} %collective-permute-done.3.refs_6_), channel_id=1, source_target_pairs={{0,48},{16,0},{32,16},{48,32},{64,112},{80,64},{96,80},{112,96},{1... | collective-permute-start | bytes 786440 | tf_op jit(solution)/shard_map/ppermute | solution.py:192
  17.0 0.7 collective-permute-start.5
  17.7 0.8 collective-permute-start.6
  18.6 4.0 %collective-permute-done.4.refs_7_ = bf16[256,512]{1,0:T(8,128)(2,1)S(1)} collective-permute-done((bf16[256,512]{1,0:T(8,128)(2,1)S(1)}, bf16[256,512]{1,0:T(8,128)(2,1)S(1)}, u32[]{:S(2)}, u32[]{:S(2)}) %collective-permute-start.4) | collective-permute-done | bytes 262176 | tf_op jit(solution)/shard_map/ppermute | solution.py:192
  22.6 3.7 %collective-permute-done.5.refs_8_ = bf16[256,512]{1,0:T(8,128)(2,1)S(1)} collective-permute-done((bf16[256,512]{1,0:T(8,128)(2,1)S(1)}, bf16[256,512]{1,0:T(8,128)(2,1)S(1)}, u32[]{:S(2)}, u32[]{:S(2)}) %collective-permute-start.5) | collective-permute-done | bytes 262176 | tf_op jit(solution)/shard_map/ppermute | solution.py:194
  26.3 4.1 %spread.3 = (bf16[4,256,512]{2,1,0:T(8,128)(2,1)S(1)}, bf16[4,256,512]{2,1,0:T(8,128)(2,1)S(1)}) custom-call(s32[241]{0:T(256)S(1)} %get-tuple-element.49.refs_0_, bf16[80,256,256]{2,1,0:T(8,128)(2,1)S(1)} %get-tuple-element.50.refs_1_, bf16[256,512]{1,0:T(8,128)(2,1)S(1)} %copy-done.1, bf16[256,512]{1,0:T(8,128)(2,1)S(1)} %collective-permute-done.1.refs_3_, ...), custom_call_target="tpu_custom_call" | custom-call | flops 53687091200 | bytes 10485760 | tf_op jit(solution)/shard_map/spread/pallas_call | solution.py:152
  30.5 4.0 %spread.2 = (bf16[4,256,512]{2,1,0:T(8,128)(2,1)S(1)}, bf16[4,256,512]{2,1,0:T(8,128)(2,1)S(1)}) custom-call(s32[241]{0:T(256)S(1)} %get-tuple-element.49.refs_0_, bf16[80,256,256]{2,1,0:T(8,128)(2,1)S(1)} %get-tuple-element.50.refs_1_, bf16[256,512]{1,0:T(8,128)(2,1)S(1)} %copy-done.1, bf16[256,512]{1,0:T(8,128)(2,1)S(1)} %collective-permute-done.1.refs_3_, ...), custom_call_target="tpu_custom_call" | custom-call | flops 53687091200 | bytes 10485760 | tf_op jit(solution)/shard_map/spread/pallas_call | solution.py:152
  34.7 4.1 %collective-permute-start.14 = (bf16[256,512]{1,0:T(8,128)(2,1)S(1)}, bf16[256,512]{1,0:T(8,128)(2,1)S(1)}, u32[]{:S(2)}, u32[]{:S(2)}) collective-permute-start(bf16[256,512]{1,0:T(8,128)(2,1)S(1)} %get-tuple-element.63), channel_id=1, source_target_pairs={{0,6},{1,7},{2,0},{3,1},{4,2},{5,3},{6,4},{7,5},{8,14},{9,15},{10,... | collective-permute-start | bytes 786440 | tf_op jit(solution)/shard_map/ppermute | solution.py:204
  38.8 1.4 %collective-permute-start.11 = (bf16[256,512]{1,0:T(8,128)(2,1)S(1)}, bf16[256,512]{1,0:T(8,128)(2,1)S(1)}, u32[]{:S(2)}, u32[]{:S(2)}) collective-permute-start(bf16[256,512]{1,0:T(8,128)(2,1)S(1)} %get-tuple-element.60), channel_id=1, source_target_pairs={{0,8},{1,9},{2,10},{3,11},{4,12},{5,13},{6,14},{7,15},{8,0},{9,1},... | collective-permute-start | bytes 786440 | tf_op jit(solution)/shard_map/ppermute | solution.py:205
  40.3 3.3 %collective-permute-start.9 = (bf16[256,512]{1,0:T(8,128)(2,1)S(1)}, bf16[256,512]{1,0:T(8,128)(2,1)S(1)}, u32[]{:S(2)}, u32[]{:S(2)}) collective-permute-start(bf16[256,512]{1,0:T(8,128)(2,1)S(1)} %get-tuple-element.56), channel_id=1, source_target_pairs={{0,6},{1,7},{2,0},{3,1},{4,2},{5,3},{6,4},{7,5},{8,14},{9,15},{10,... | collective-permute-start | bytes 786440 | tf_op jit(solution)/shard_map/ppermute | solution.py:207
  43.6 1.8 %collective-permute-done.14 = bf16[256,512]{1,0:T(8,128)(2,1)S(1)} collective-permute-done((bf16[256,512]{1,0:T(8,128)(2,1)S(1)}, bf16[256,512]{1,0:T(8,128)(2,1)S(1)}, u32[]{:S(2)}, u32[]{:S(2)}) %collective-permute-start.14) | collective-permute-done | bytes 262176 | tf_op jit(solution)/shard_map/ppermute | solution.py:204
  45.5 3.6 %collective-permute-done.13 = bf16[256,512]{1,0:T(8,128)(2,1)S(1)} collective-permute-done((bf16[256,512]{1,0:T(8,128)(2,1)S(1)}, bf16[256,512]{1,0:T(8,128)(2,1)S(1)}, u32[]{:S(2)}, u32[]{:S(2)}) %collective-permute-start.13) | collective-permute-done | bytes 262176 | tf_op jit(solution)/shard_map/ppermute | solution.py:203
  49.2 1.6 %collective-permute-start.15 = (bf16[256,512]{1,0:T(8,128)(2,1)S(1)}, bf16[256,512]{1,0:T(8,128)(2,1)S(1)}, u32[]{:S(2)}, u32[]{:S(2)}) collective-permute-start(bf16[256,512]{1,0:T(8,128)(2,1)S(1)} %add_convert_fusion.4), channel_id=1, source_target_pairs={{0,8},{1,9},{2,10},{3,11},{4,12},{5,13},{6,14},{7,15},{8,0},{9,1},... | collective-permute-start | bytes 786440 | tf_op jit(solution)/shard_map/ppermute | solution.py:211
  50.9 8.3 %collective-permute-done.8 = bf16[256,512]{1,0:T(8,128)(2,1)S(1)} collective-permute-done((bf16[256,512]{1,0:T(8,128)(2,1)S(1)}, bf16[256,512]{1,0:T(8,128)(2,1)S(1)}, u32[]{:S(2)}, u32[]{:S(2)}) %collective-permute-start.8) | collective-permute-done | bytes 262176 | tf_op jit(solution)/shard_map/ppermute | solution.py:206
  59.4 1.2 multiply_convert_fusion
  60.9 2.0 %collective-permute-start.16 = (bf16[512,256]{1,0:T(8,128)(2,1)S(1)}, bf16[512,256]{1,0:T(8,128)(2,1)S(1)}, u32[]{:S(2)}, u32[]{:S(2)}) collective-permute-start(bf16[512,256]{1,0:T(8,128)(2,1)S(1)} %fusion.refs_2_), channel_id=1, source_target_pairs={{0,8},{1,9},{2,10},{3,11},{4,12},{5,13},{6,14},{7,15},{8,0},{9,1},... | collective-permute-start | bytes 786440 | tf_op jit(solution)/shard_map/ppermute | solution.py:187
  63.5 5.3 %collective-permute-done.16.refs_6_ = bf16[512,256]{1,0:T(8,128)(2,1)S(1)} collective-permute-done((bf16[512,256]{1,0:T(8,128)(2,1)S(1)}, bf16[512,256]{1,0:T(8,128)(2,1)S(1)}, u32[]{:S(2)}, u32[]{:S(2)}) %collective-permute-start.16) | collective-permute-done | bytes 262176 | tf_op jit(solution)/shard_map/ppermute | solution.py:187
  69.9 0.7 collective-permute-start.19
  70.6 1.1 collective-permute-done.20.refs_4_
  72.5 1.4 %collective-permute-start.18 = (bf16[128,512]{1,0:T(8,128)(2,1)S(1)}, bf16[128,512]{1,0:T(8,128)(2,1)S(1)}, u32[]{:S(2)}, u32[]{:S(2)}) collective-permute-start(bf16[128,512]{1,0:T(8,128)(2,1)S(1)} %fusion.10), channel_id=1, source_target_pairs={{0,2},{1,3},{2,0},{3,1},{4,6},{5,7},{6,4},{7,5},{8,10},{9,11},{10,... | collective-permute-start | bytes 393224 | tf_op jit(solution)/shard_map/ppermute | solution.py:305
  73.8 0.7 collective-permute-start.22
  74.6 3.8 %collective-permute-done.25.refs_3_ = bf16[512,256]{1,0:T(8,128)(2,1)S(1)} collective-permute-done((bf16[512,256]{1,0:T(8,128)(2,1)S(1)}, bf16[512,256]{1,0:T(8,128)(2,1)S(1)}, u32[]{:S(2)}, u32[]{:S(2)}) %collective-permute-start.25) | collective-permute-done | bytes 262176 | tf_op jit(solution)/shard_map/ppermute | solution.py:189
  78.4 5.6 %collective-permute-done.19.refs_7_ = bf16[512,256]{1,0:T(8,128)(2,1)S(1)} collective-permute-done((bf16[512,256]{1,0:T(8,128)(2,1)S(1)}, bf16[512,256]{1,0:T(8,128)(2,1)S(1)}, u32[]{:S(2)}, u32[]{:S(2)}) %collective-permute-start.19) | collective-permute-done | bytes 262176 | tf_op jit(solution)/shard_map/ppermute | solution.py:192
  84.5 1.8 %collective-permute-done.18 = bf16[128,512]{1,0:T(8,128)(2,1)S(1)} collective-permute-done((bf16[128,512]{1,0:T(8,128)(2,1)S(1)}, bf16[128,512]{1,0:T(8,128)(2,1)S(1)}, u32[]{:S(2)}, u32[]{:S(2)}) %collective-permute-start.18) | collective-permute-done | bytes 131104 | tf_op jit(solution)/shard_map/ppermute | solution.py:305
  86.5 1.7 %collective-permute-done.26.refs_5_ = bf16[512,256]{1,0:T(8,128)(2,1)S(1)} collective-permute-done((bf16[512,256]{1,0:T(8,128)(2,1)S(1)}, bf16[512,256]{1,0:T(8,128)(2,1)S(1)}, u32[]{:S(2)}, u32[]{:S(2)}) %collective-permute-start.26) | collective-permute-done | bytes 262176 | tf_op jit(solution)/shard_map/ppermute | solution.py:190
  89.2 3.0 %collective-permute-done.23 = bf16[64,512]{1,0:T(8,128)(2,1)S(1)} collective-permute-done((bf16[64,512]{1,0:T(8,128)(2,1)S(1)}, bf16[64,512]{1,0:T(8,128)(2,1)S(1)}, u32[]{:S(2)}, u32[]{:S(2)}) %collective-permute-start.23) | collective-permute-done | bytes 65568 | tf_op jit(solution)/shard_map/ppermute | solution.py:305
  92.3 1.8 %collective-permute-start.24 = (bf16[64,512]{1,0:T(8,128)(2,1)S(1)}, bf16[64,512]{1,0:T(8,128)(2,1)S(1)}, u32[]{:S(2)}, u32[]{:S(2)}) collective-permute-start(bf16[64,512]{1,0:T(8,128)(2,1)S(1)} %fusion.12), channel_id=1, source_target_pairs={{0,8},{1,9},{2,10},{3,11},{4,12},{5,13},{6,14},{7,15},{8,0},{9,1},... | collective-permute-start | bytes 196616 | tf_op jit(solution)/shard_map/ppermute | solution.py:323
  94.1 3.2 %spread_back.2 = (bf16[512,256]{1,0:T(8,128)(2,1)S(1)}, bf16[512,256]{1,0:T(8,128)(2,1)S(1)}, bf16[512,256]{1,0:T(8,128)(2,1)S(1)}, bf16[512,256]{1,0:T(8,128)(2,1)S(1)}) custom-call(s32[201]{0:T(256)S(1)} %get-tuple-element.73.refs_0_, bf16[80,256,256]{2,1,0:T(8,128)(2,1)S(1)} %get-tuple-element.50.refs_1_, bf16[512,256]{1,0:T(8,128)(2,1)S(1)} %fusion.refs_2_, ...), custom_call_target="tpu_custom_call" | custom-call | flops 53687091200 | bytes 10485760 | tf_op jit(solution)/shard_map/spread_back/pallas_call | solution.py:152
  97.3 2.7 %collective-permute-start.35 = (bf16[64,512]{1,0:T(8,128)(2,1)S(1)}, bf16[64,512]{1,0:T(8,128)(2,1)S(1)}, u32[]{:S(2)}, u32[]{:S(2)}) collective-permute-start(bf16[64,512]{1,0:T(8,128)(2,1)S(1)} %convert_element_type.181), channel_id=1, source_target_pairs={{0,64},{16,80},{32,96},{48,112},{64,0},{80,16},{96,32},{112,48},{1... | collective-permute-start | bytes 196616 | tf_op jit(solution)/shard_map/ppermute | solution.py:323
  100.0 1.5 %collective-permute-start.37 = (bf16[512,256]{1,0:T(8,128)(2,1)S(1)}, bf16[512,256]{1,0:T(8,128)(2,1)S(1)}, u32[]{:S(2)}, u32[]{:S(2)}) collective-permute-start(bf16[512,256]{1,0:T(8,128)(2,1)S(1)} %get-tuple-element.75), channel_id=1, source_target_pairs={{0,16},{16,32},{32,48},{48,0},{64,80},{80,96},{96,112},{112,64},{1... | collective-permute-start | bytes 786440 | tf_op jit(solution)/shard_map/ppermute | solution.py:203
  101.6 1.7 %collective-permute-start.38 = (bf16[512,256]{1,0:T(8,128)(2,1)S(1)}, bf16[512,256]{1,0:T(8,128)(2,1)S(1)}, u32[]{:S(2)}, u32[]{:S(2)}) collective-permute-start(bf16[512,256]{1,0:T(8,128)(2,1)S(1)} %get-tuple-element.77), channel_id=1, source_target_pairs={{0,48},{16,0},{32,16},{48,32},{64,112},{80,64},{96,80},{112,96},{1... | collective-permute-start | bytes 786440 | tf_op jit(solution)/shard_map/ppermute | solution.py:204
  103.3 0.9 collective-permute-start.39
  104.5 3.3 %spread_back.3 = (bf16[512,256]{1,0:T(8,128)(2,1)S(1)}, bf16[512,256]{1,0:T(8,128)(2,1)S(1)}, bf16[512,256]{1,0:T(8,128)(2,1)S(1)}, bf16[512,256]{1,0:T(8,128)(2,1)S(1)}) custom-call(s32[201]{0:T(256)S(1)} %get-tuple-element.73.refs_0_, bf16[80,256,256]{2,1,0:T(8,128)(2,1)S(1)} %get-tuple-element.50.refs_1_, bf16[512,256]{1,0:T(8,128)(2,1)S(1)} %fusion.refs_2_, ...), custom_call_target="tpu_custom_call" | custom-call | flops 53687091200 | bytes 10485760 | tf_op jit(solution)/shard_map/spread_back/pallas_call | solution.py:152
  107.8 1.7 %collective-permute-start.45 = (bf16[512,256]{1,0:T(8,128)(2,1)S(1)}, bf16[512,256]{1,0:T(8,128)(2,1)S(1)}, u32[]{:S(2)}, u32[]{:S(2)}) collective-permute-start(bf16[512,256]{1,0:T(8,128)(2,1)S(1)} %get-tuple-element.82), channel_id=1, source_target_pairs={{0,48},{16,0},{32,16},{48,32},{64,112},{80,64},{96,80},{112,96},{1... | collective-permute-start | bytes 786440 | tf_op jit(solution)/shard_map/ppermute | solution.py:207
  109.5 0.8 collective-permute-done.36
  110.4 0.8 collective-permute-done.39
  111.2 2.5 %collective-permute-start.40 = (bf16[64,512]{1,0:T(8,128)(2,1)S(1)}, bf16[64,512]{1,0:T(8,128)(2,1)S(1)}, u32[]{:S(2)}, u32[]{:S(2)}) collective-permute-start(bf16[64,512]{1,0:T(8,128)(2,1)S(1)} %convert_element_type.185), channel_id=1, source_target_pairs={{0,48},{16,32},{32,16},{48,0},{64,112},{80,96},{96,80},{112,64},{1... | collective-permute-start | bytes 196616 | tf_op jit(solution)/shard_map/ppermute | solution.py:323
  113.8 2.0 %collective-permute-start.47 = (bf16[512,256]{1,0:T(8,128)(2,1)S(1)}, bf16[512,256]{1,0:T(8,128)(2,1)S(1)}, u32[]{:S(2)}, u32[]{:S(2)}) collective-permute-start(bf16[512,256]{1,0:T(8,128)(2,1)S(1)} %add_convert_fusion.1), channel_id=1, source_target_pairs={{0,64},{16,80},{32,96},{48,112},{64,0},{80,16},{96,32},{112,48},{1... | collective-permute-start | bytes 786440 | tf_op jit(solution)/shard_map/ppermute | solution.py:211
  115.8 5.1 %collective-permute-done.40 = bf16[64,512]{1,0:T(8,128)(2,1)S(1)} collective-permute-done((bf16[64,512]{1,0:T(8,128)(2,1)S(1)}, bf16[64,512]{1,0:T(8,128)(2,1)S(1)}, u32[]{:S(2)}, u32[]{:S(2)}) %collective-permute-start.40) | collective-permute-done | bytes 65568 | tf_op jit(solution)/shard_map/ppermute | solution.py:323
  121.8 4.7 %collective-permute-done.41 = bf16[64,512]{1,0:T(8,128)(2,1)S(1)} collective-permute-done((bf16[64,512]{1,0:T(8,128)(2,1)S(1)}, bf16[64,512]{1,0:T(8,128)(2,1)S(1)}, u32[]{:S(2)}, u32[]{:S(2)}) %collective-permute-start.41) | collective-permute-done | bytes 65568 | tf_op jit(solution)/shard_map/ppermute | solution.py:308
  126.8 5.0 %collective-permute-done.42 = bf16[128,512]{1,0:T(8,128)(2,1)S(1)} collective-permute-done((bf16[128,512]{1,0:T(8,128)(2,1)S(1)}, bf16[128,512]{1,0:T(8,128)(2,1)S(1)}, u32[]{:S(2)}, u32[]{:S(2)}) %collective-permute-start.42) | collective-permute-done | bytes 131104 | tf_op jit(solution)/shard_map/ppermute | solution.py:308
  132.6 0.8 copy.11
  134.0 2.0 %fusion.3 = f32[512,512]{1,0:T(8,128)} fusion(s32[]{:T(128)S(6)} %mul.76, bf16[256,512]{1,0:T(8,128)(2,1)S(1)} %collective-permute-done.43, bf16[256,512]{1,0:T(8,128)(2,1)S(1)} %fusion.5), kind=kLoop, calls=%fused_computation.8 | loop fusion | flops 1572864 | bytes 1572868 | tf_op jit(solution)/shard_map/convert_element_type | solution.py:327
  (87 shorter events, 9.0 us)
Async XLA Ops:
  0.7 13.5 %collective-permute-start = (bf16[256,512]{1,0:T(8,128)(2,1)}, bf16[256,512]{1,0:T(8,128)(2,1)S(1)}, u32[]{:S(2)}, u32[]{:S(2)}) collective-permute-start(bf16[256,512]{1,0:T(8,128)(2,1)} %refs_2_.1), channel_id=1, source_target_pairs={{0,32},{16,48},{32,0},{48,16},{64,96},{80,112},{96,64},{112,80},{1... | collective-permute-start | bytes 786440 | tf_op jit(solution)/shard_map/ppermute | solution.py:188
  3.9 10.3 %collective-permute-start.3 = (bf16[256,512]{1,0:T(8,128)(2,1)}, bf16[256,512]{1,0:T(8,128)(2,1)S(1)}, u32[]{:S(2)}, u32[]{:S(2)}) collective-permute-start(bf16[256,512]{1,0:T(8,128)(2,1)} %refs_2_.1), channel_id=1, source_target_pairs={{0,64},{16,80},{32,96},{48,112},{64,0},{80,16},{96,32},{112,48},{1... | collective-permute-start | bytes 786440 | tf_op jit(solution)/shard_map/ppermute | solution.py:187
  7.1 11.5 %collective-permute-start.1 = (bf16[256,512]{1,0:T(8,128)(2,1)}, bf16[256,512]{1,0:T(8,128)(2,1)S(1)}, u32[]{:S(2)}, u32[]{:S(2)}) collective-permute-start(bf16[256,512]{1,0:T(8,128)(2,1)} %refs_2_.1), channel_id=1, source_target_pairs={{0,48},{16,0},{32,16},{48,32},{64,112},{80,64},{96,80},{112,96},{1... | collective-permute-start | bytes 786440 | tf_op jit(solution)/shard_map/ppermute | solution.py:189
  8.2 10.4 %collective-permute-start.2 = (bf16[256,512]{1,0:T(8,128)(2,1)}, bf16[256,512]{1,0:T(8,128)(2,1)S(1)}, u32[]{:S(2)}, u32[]{:S(2)}) collective-permute-start(bf16[256,512]{1,0:T(8,128)(2,1)} %refs_2_.1), channel_id=1, source_target_pairs={{0,16},{16,32},{32,48},{48,0},{64,80},{80,96},{96,112},{112,64},{1... | collective-permute-start | bytes 786440 | tf_op jit(solution)/shard_map/ppermute | solution.py:190
  14.2 8.4 %collective-permute-start.4 = (bf16[256,512]{1,0:T(8,128)(2,1)S(1)}, bf16[256,512]{1,0:T(8,128)(2,1)S(1)}, u32[]{:S(2)}, u32[]{:S(2)}) collective-permute-start(bf16[256,512]{1,0:T(8,128)(2,1)S(1)} %collective-permute-done.3.refs_6_), channel_id=1, source_target_pairs={{0,48},{16,0},{32,16},{48,32},{64,112},{80,64},{96,80},{112,96},{1... | collective-permute-start | bytes 786440 | tf_op jit(solution)/shard_map/ppermute | solution.py:192
  17.0 9.3 %collective-permute-start.5 = (bf16[256,512]{1,0:T(8,128)(2,1)S(1)}, bf16[256,512]{1,0:T(8,128)(2,1)S(1)}, u32[]{:S(2)}, u32[]{:S(2)}) collective-permute-start(bf16[256,512]{1,0:T(8,128)(2,1)S(1)} %collective-permute-done.refs_4_), channel_id=1, source_target_pairs={{0,64},{16,80},{32,96},{48,112},{64,0},{80,16},{96,32},{112,48},{1... | collective-permute-start | bytes 786440 | tf_op jit(solution)/shard_map/ppermute | solution.py:194
  17.7 8.5 %collective-permute-start.6 = (bf16[256,512]{1,0:T(8,128)(2,1)S(1)}, bf16[256,512]{1,0:T(8,128)(2,1)S(1)}, u32[]{:S(2)}, u32[]{:S(2)}) collective-permute-start(bf16[256,512]{1,0:T(8,128)(2,1)S(1)} %collective-permute-done.3.refs_6_), channel_id=1, source_target_pairs={{0,16},{16,32},{32,48},{48,0},{64,80},{80,96},{96,112},{112,64},{1... | collective-permute-start | bytes 786440 | tf_op jit(solution)/shard_map/ppermute | solution.py:193
  30.4 4.2 %collective-permute-start.10 = (bf16[4,256,512]{2,1,0:T(8,128)(2,1)S(1)}, bf16[4,256,512]{2,1,0:T(8,128)(2,1)S(1)}, u32[]{:S(2)}, u32[]{:S(2)}) collective-permute-start(bf16[4,256,512]{2,1,0:T(8,128)(2,1)S(1)} %get-tuple-element.59), channel_id=1, source_target_pairs={{0,1},{1,0},{2,3},{3,2},{4,5},{5,4},{6,7},{7,6},{8,9},{9,8},{10,11... | collective-permute-start | bytes 3145736 | tf_op jit(solution)/shard_map/ppermute | solution.py:269
  34.5 5.7 %collective-permute-start.7 = (bf16[4,256,512]{2,1,0:T(8,128)(2,1)S(1)}, bf16[4,256,512]{2,1,0:T(8,128)(2,1)S(1)}, u32[]{:S(2)}, u32[]{:S(2)}) collective-permute-start(bf16[4,256,512]{2,1,0:T(8,128)(2,1)S(1)} %get-tuple-element.53), channel_id=1, source_target_pairs={{0,1},{1,0},{2,3},{3,2},{4,5},{5,4},{6,7},{7,6},{8,9},{9,8},{10,11... | collective-permute-start | bytes 3145736 | tf_op jit(solution)/shard_map/ppermute | solution.py:269
  34.7 10.8 %collective-permute-start.14 = (bf16[256,512]{1,0:T(8,128)(2,1)S(1)}, bf16[256,512]{1,0:T(8,128)(2,1)S(1)}, u32[]{:S(2)}, u32[]{:S(2)}) collective-permute-start(bf16[256,512]{1,0:T(8,128)(2,1)S(1)} %get-tuple-element.63), channel_id=1, source_target_pairs={{0,6},{1,7},{2,0},{3,1},{4,2},{5,3},{6,4},{7,5},{8,14},{9,15},{10,... | collective-permute-start | bytes 786440 | tf_op jit(solution)/shard_map/ppermute | solution.py:204
  38.8 10.3 %collective-permute-start.13 = (bf16[256,512]{1,0:T(8,128)(2,1)S(1)}, bf16[256,512]{1,0:T(8,128)(2,1)S(1)}, u32[]{:S(2)}, u32[]{:S(2)}) collective-permute-start(bf16[256,512]{1,0:T(8,128)(2,1)S(1)} %get-tuple-element.62), channel_id=1, source_target_pairs={{0,2},{1,3},{2,4},{3,5},{4,6},{5,7},{6,0},{7,1},{8,10},{9,11},{10,... | collective-permute-start | bytes 786440 | tf_op jit(solution)/shard_map/ppermute | solution.py:203
  38.8 12.0 %collective-permute-start.11 = (bf16[256,512]{1,0:T(8,128)(2,1)S(1)}, bf16[256,512]{1,0:T(8,128)(2,1)S(1)}, u32[]{:S(2)}, u32[]{:S(2)}) collective-permute-start(bf16[256,512]{1,0:T(8,128)(2,1)S(1)} %get-tuple-element.60), channel_id=1, source_target_pairs={{0,8},{1,9},{2,10},{3,11},{4,12},{5,13},{6,14},{7,15},{8,0},{9,1},... | collective-permute-start | bytes 786440 | tf_op jit(solution)/shard_map/ppermute | solution.py:205
  40.3 10.6 %collective-permute-start.9 = (bf16[256,512]{1,0:T(8,128)(2,1)S(1)}, bf16[256,512]{1,0:T(8,128)(2,1)S(1)}, u32[]{:S(2)}, u32[]{:S(2)}) collective-permute-start(bf16[256,512]{1,0:T(8,128)(2,1)S(1)} %get-tuple-element.56), channel_id=1, source_target_pairs={{0,6},{1,7},{2,0},{3,1},{4,2},{5,3},{6,4},{7,5},{8,14},{9,15},{10,... | collective-permute-start | bytes 786440 | tf_op jit(solution)/shard_map/ppermute | solution.py:207
  43.6 15.6 %collective-permute-start.8 = (bf16[256,512]{1,0:T(8,128)(2,1)S(1)}, bf16[256,512]{1,0:T(8,128)(2,1)S(1)}, u32[]{:S(2)}, u32[]{:S(2)}) collective-permute-start(bf16[256,512]{1,0:T(8,128)(2,1)S(1)} %get-tuple-element.55), channel_id=1, source_target_pairs={{0,2},{1,3},{2,4},{3,5},{4,6},{5,7},{6,0},{7,1},{8,10},{9,11},{10,... | collective-permute-start | bytes 786440 | tf_op jit(solution)/shard_map/ppermute | solution.py:206
  49.2 10.0 %collective-permute-start.15 = (bf16[256,512]{1,0:T(8,128)(2,1)S(1)}, bf16[256,512]{1,0:T(8,128)(2,1)S(1)}, u32[]{:S(2)}, u32[]{:S(2)}) collective-permute-start(bf16[256,512]{1,0:T(8,128)(2,1)S(1)} %add_convert_fusion.4), channel_id=1, source_target_pairs={{0,8},{1,9},{2,10},{3,11},{4,12},{5,13},{6,14},{7,15},{8,0},{9,1},... | collective-permute-start | bytes 786440 | tf_op jit(solution)/shard_map/ppermute | solution.py:211
  50.8 8.4 %collective-permute-start.12 = (bf16[256,512]{1,0:T(8,128)(2,1)S(1)}, bf16[256,512]{1,0:T(8,128)(2,1)S(1)}, u32[]{:S(2)}, u32[]{:S(2)}) collective-permute-start(bf16[256,512]{1,0:T(8,128)(2,1)S(1)} %add_convert_fusion.5), channel_id=1, source_target_pairs={{0,4},{1,5},{2,6},{3,7},{4,0},{5,1},{6,2},{7,3},{8,12},{9,13},{10,... | collective-permute-start | bytes 786440 | tf_op jit(solution)/shard_map/ppermute | solution.py:210
  60.9 7.8 %collective-permute-start.16 = (bf16[512,256]{1,0:T(8,128)(2,1)S(1)}, bf16[512,256]{1,0:T(8,128)(2,1)S(1)}, u32[]{:S(2)}, u32[]{:S(2)}) collective-permute-start(bf16[512,256]{1,0:T(8,128)(2,1)S(1)} %fusion.refs_2_), channel_id=1, source_target_pairs={{0,8},{1,9},{2,10},{3,11},{4,12},{5,13},{6,14},{7,15},{8,0},{9,1},... | collective-permute-start | bytes 786440 | tf_op jit(solution)/shard_map/ppermute | solution.py:187
  62.9 8.8 %collective-permute-start.20 = (bf16[512,256]{1,0:T(8,128)(2,1)S(1)}, bf16[512,256]{1,0:T(8,128)(2,1)S(1)}, u32[]{:S(2)}, u32[]{:S(2)}) collective-permute-start(bf16[512,256]{1,0:T(8,128)(2,1)S(1)} %fusion.refs_2_), channel_id=1, source_target_pairs={{0,4},{1,5},{2,6},{3,7},{4,0},{5,1},{6,2},{7,3},{8,12},{9,13},{10,... | collective-permute-start | bytes 786440 | tf_op jit(solution)/shard_map/ppermute | solution.py:188
  69.1 3.2 %collective-permute-start.17 = (bf16[256,512]{1,0:T(8,128)(2,1)S(1)}, bf16[256,512]{1,0:T(8,128)(2,1)S(1)}, u32[]{:S(2)}, u32[]{:S(2)}) collective-permute-start(bf16[256,512]{1,0:T(8,128)(2,1)S(1)} %fusion.6), channel_id=1, source_target_pairs={{0,1},{1,0},{2,3},{3,2},{4,5},{5,4},{6,7},{7,6},{8,9},{9,8},{10,11... | collective-permute-start | bytes 786440 | tf_op jit(solution)/shard_map/ppermute | solution.py:305
  69.2 9.2 %collective-permute-start.25 = (bf16[512,256]{1,0:T(8,128)(2,1)S(1)}, bf16[512,256]{1,0:T(8,128)(2,1)S(1)}, u32[]{:S(2)}, u32[]{:S(2)}) collective-permute-start(bf16[512,256]{1,0:T(8,128)(2,1)S(1)} %fusion.refs_2_), channel_id=1, source_target_pairs={{0,6},{1,7},{2,0},{3,1},{4,2},{5,3},{6,4},{7,5},{8,14},{9,15},{10,... | collective-permute-start | bytes 786440 | tf_op jit(solution)/shard_map/ppermute | solution.py:189
  69.9 14.1 %collective-permute-start.19 = (bf16[512,256]{1,0:T(8,128)(2,1)S(1)}, bf16[512,256]{1,0:T(8,128)(2,1)S(1)}, u32[]{:S(2)}, u32[]{:S(2)}) collective-permute-start(bf16[512,256]{1,0:T(8,128)(2,1)S(1)} %collective-permute-done.16.refs_6_), channel_id=1, source_target_pairs={{0,6},{1,7},{2,0},{3,1},{4,2},{5,3},{6,4},{7,5},{8,14},{9,15},{10,... | collective-permute-start | bytes 786440 | tf_op jit(solution)/shard_map/ppermute | solution.py:192
  71.7 12.3 %collective-permute-start.21 = (bf16[512,256]{1,0:T(8,128)(2,1)S(1)}, bf16[512,256]{1,0:T(8,128)(2,1)S(1)}, u32[]{:S(2)}, u32[]{:S(2)}) collective-permute-start(bf16[512,256]{1,0:T(8,128)(2,1)S(1)} %collective-permute-done.20.refs_4_), channel_id=1, source_target_pairs={{0,8},{1,9},{2,10},{3,11},{4,12},{5,13},{6,14},{7,15},{8,0},{9,1},... | collective-permute-start | bytes 786440 | tf_op jit(solution)/shard_map/ppermute | solution.py:194
  72.5 13.9 %collective-permute-start.18 = (bf16[128,512]{1,0:T(8,128)(2,1)S(1)}, bf16[128,512]{1,0:T(8,128)(2,1)S(1)}, u32[]{:S(2)}, u32[]{:S(2)}) collective-permute-start(bf16[128,512]{1,0:T(8,128)(2,1)S(1)} %fusion.10), channel_id=1, source_target_pairs={{0,2},{1,3},{2,0},{3,1},{4,6},{5,7},{6,4},{7,5},{8,10},{9,11},{10,... | collective-permute-start | bytes 393224 | tf_op jit(solution)/shard_map/ppermute | solution.py:305
  73.8 12.5 %collective-permute-start.22 = (bf16[512,256]{1,0:T(8,128)(2,1)S(1)}, bf16[512,256]{1,0:T(8,128)(2,1)S(1)}, u32[]{:S(2)}, u32[]{:S(2)}) collective-permute-start(bf16[512,256]{1,0:T(8,128)(2,1)S(1)} %collective-permute-done.16.refs_6_), channel_id=1, source_target_pairs={{0,2},{1,3},{2,4},{3,5},{4,6},{5,7},{6,0},{7,1},{8,10},{9,11},{10,... | collective-permute-start | bytes 786440 | tf_op jit(solution)/shard_map/ppermute | solution.py:193
  78.4 9.8 %collective-permute-start.26 = (bf16[512,256]{1,0:T(8,128)(2,1)S(1)}, bf16[512,256]{1,0:T(8,128)(2,1)S(1)}, u32[]{:S(2)}, u32[]{:S(2)}) collective-permute-start(bf16[512,256]{1,0:T(8,128)(2,1)S(1)} %fusion.refs_2_), channel_id=1, source_target_pairs={{0,2},{1,3},{2,4},{3,5},{4,6},{5,7},{6,0},{7,1},{8,10},{9,11},{10,... | collective-permute-start | bytes 786440 | tf_op jit(solution)/shard_map/ppermute | solution.py:190
  84.0 4.2 %collective-permute-start.27 = (bf16[512,256]{1,0:T(8,128)(2,1)S(1)}, bf16[512,256]{1,0:T(8,128)(2,1)S(1)}, u32[]{:S(2)}, u32[]{:S(2)}) collective-permute-start(bf16[512,256]{1,0:T(8,128)(2,1)S(1)} %fusion.refs_2_), channel_id=1, source_target_pairs={{0,1},{1,0},{2,3},{3,2},{4,5},{5,4},{6,7},{7,6},{8,9},{9,8},{10,11... | collective-permute-start | bytes 786440 | tf_op jit(solution)/shard_map/ppermute | solution.py:284
  84.0 4.8 %collective-permute-start.29 = (bf16[512,256]{1,0:T(8,128)(2,1)S(1)}, bf16[512,256]{1,0:T(8,128)(2,1)S(1)}, u32[]{:S(2)}, u32[]{:S(2)}) collective-permute-start(bf16[512,256]{1,0:T(8,128)(2,1)S(1)} %collective-permute-done.20.refs_4_), channel_id=1, source_target_pairs={{0,1},{1,0},{2,3},{3,2},{4,5},{5,4},{6,7},{7,6},{8,9},{9,8},{10,11... | collective-permute-start | bytes 786440 | tf_op jit(solution)/shard_map/ppermute | solution.py:284
  86.4 2.4 %collective-permute-start.28 = (bf16[512,256]{1,0:T(8,128)(2,1)S(1)}, bf16[512,256]{1,0:T(8,128)(2,1)S(1)}, u32[]{:S(2)}, u32[]{:S(2)}) collective-permute-start(bf16[512,256]{1,0:T(8,128)(2,1)S(1)} %collective-permute-done.25.refs_3_), channel_id=1, source_target_pairs={{0,1},{1,0},{2,3},{3,2},{4,5},{5,4},{6,7},{7,6},{8,9},{9,8},{10,11... | collective-permute-start | bytes 786440 | tf_op jit(solution)/shard_map/ppermute | solution.py:284
  86.4 5.8 %collective-permute-start.23 = (bf16[64,512]{1,0:T(8,128)(2,1)S(1)}, bf16[64,512]{1,0:T(8,128)(2,1)S(1)}, u32[]{:S(2)}, u32[]{:S(2)}) collective-permute-start(bf16[64,512]{1,0:T(8,128)(2,1)S(1)} %fusion.13), channel_id=1, source_target_pairs={{0,6},{1,7},{2,4},{3,5},{4,2},{5,3},{6,0},{7,1},{8,14},{9,15},{10,... | collective-permute-start | bytes 196616 | tf_op jit(solution)/shard_map/ppermute | solution.py:305
  88.2 5.9 %collective-permute-start.31 = (bf16[512,256]{1,0:T(8,128)(2,1)S(1)}, bf16[512,256]{1,0:T(8,128)(2,1)S(1)}, u32[]{:S(2)}, u32[]{:S(2)}) collective-permute-start(bf16[512,256]{1,0:T(8,128)(2,1)S(1)} %collective-permute-done.16.refs_6_), channel_id=1, source_target_pairs={{0,1},{1,0},{2,3},{3,2},{4,5},{5,4},{6,7},{7,6},{8,9},{9,8},{10,11... | collective-permute-start | bytes 786440 | tf_op jit(solution)/shard_map/ppermute | solution.py:284
  88.2 4.0 %collective-permute-start.30 = (bf16[512,256]{1,0:T(8,128)(2,1)S(1)}, bf16[512,256]{1,0:T(8,128)(2,1)S(1)}, u32[]{:S(2)}, u32[]{:S(2)}) collective-permute-start(bf16[512,256]{1,0:T(8,128)(2,1)S(1)} %collective-permute-done.26.refs_5_), channel_id=1, source_target_pairs={{0,1},{1,0},{2,3},{3,2},{4,5},{5,4},{6,7},{7,6},{8,9},{9,8},{10,11... | collective-permute-start | bytes 786440 | tf_op jit(solution)/shard_map/ppermute | solution.py:284
  88.7 5.4 %collective-permute-start.32 = (bf16[512,256]{1,0:T(8,128)(2,1)S(1)}, bf16[512,256]{1,0:T(8,128)(2,1)S(1)}, u32[]{:S(2)}, u32[]{:S(2)}) collective-permute-start(bf16[512,256]{1,0:T(8,128)(2,1)S(1)} %collective-permute-done.19.refs_7_), channel_id=1, source_target_pairs={{0,1},{1,0},{2,3},{3,2},{4,5},{5,4},{6,7},{7,6},{8,9},{9,8},{10,11... | collective-permute-start | bytes 786440 | tf_op jit(solution)/shard_map/ppermute | solution.py:284
  88.8 5.3 %collective-permute-start.33 = (bf16[512,256]{1,0:T(8,128)(2,1)S(1)}, bf16[512,256]{1,0:T(8,128)(2,1)S(1)}, u32[]{:S(2)}, u32[]{:S(2)}) collective-permute-start(bf16[512,256]{1,0:T(8,128)(2,1)S(1)} %collective-permute-done.21.refs_8_), channel_id=1, source_target_pairs={{0,1},{1,0},{2,3},{3,2},{4,5},{5,4},{6,7},{7,6},{8,9},{9,8},{10,11... | collective-permute-start | bytes 786440 | tf_op jit(solution)/shard_map/ppermute | solution.py:284
  92.2 1.9 %collective-permute-start.34 = (bf16[512,256]{1,0:T(8,128)(2,1)S(1)}, bf16[512,256]{1,0:T(8,128)(2,1)S(1)}, u32[]{:S(2)}, u32[]{:S(2)}) collective-permute-start(bf16[512,256]{1,0:T(8,128)(2,1)S(1)} %collective-permute-done.22.refs_9_), channel_id=1, source_target_pairs={{0,1},{1,0},{2,3},{3,2},{4,5},{5,4},{6,7},{7,6},{8,9},{9,8},{10,11... | collective-permute-start | bytes 786440 | tf_op jit(solution)/shard_map/ppermute | solution.py:284
  92.3 5.0 %collective-permute-start.24 = (bf16[64,512]{1,0:T(8,128)(2,1)S(1)}, bf16[64,512]{1,0:T(8,128)(2,1)S(1)}, u32[]{:S(2)}, u32[]{:S(2)}) collective-permute-start(bf16[64,512]{1,0:T(8,128)(2,1)S(1)} %fusion.12), channel_id=1, source_target_pairs={{0,8},{1,9},{2,10},{3,11},{4,12},{5,13},{6,14},{7,15},{8,0},{9,1},... | collective-permute-start | bytes 196616 | tf_op jit(solution)/shard_map/ppermute | solution.py:323
  97.3 6.9 %collective-permute-start.35 = (bf16[64,512]{1,0:T(8,128)(2,1)S(1)}, bf16[64,512]{1,0:T(8,128)(2,1)S(1)}, u32[]{:S(2)}, u32[]{:S(2)}) collective-permute-start(bf16[64,512]{1,0:T(8,128)(2,1)S(1)} %convert_element_type.181), channel_id=1, source_target_pairs={{0,64},{16,80},{32,96},{48,112},{64,0},{80,16},{96,32},{112,48},{1... | collective-permute-start | bytes 196616 | tf_op jit(solution)/shard_map/ppermute | solution.py:323
  100.0 10.3 %collective-permute-start.37 = (bf16[512,256]{1,0:T(8,128)(2,1)S(1)}, bf16[512,256]{1,0:T(8,128)(2,1)S(1)}, u32[]{:S(2)}, u32[]{:S(2)}) collective-permute-start(bf16[512,256]{1,0:T(8,128)(2,1)S(1)} %get-tuple-element.75), channel_id=1, source_target_pairs={{0,16},{16,32},{32,48},{48,0},{64,80},{80,96},{96,112},{112,64},{1... | collective-permute-start | bytes 786440 | tf_op jit(solution)/shard_map/ppermute | solution.py:203
  101.6 8.8 %collective-permute-start.38 = (bf16[512,256]{1,0:T(8,128)(2,1)S(1)}, bf16[512,256]{1,0:T(8,128)(2,1)S(1)}, u32[]{:S(2)}, u32[]{:S(2)}) collective-permute-start(bf16[512,256]{1,0:T(8,128)(2,1)S(1)} %get-tuple-element.77), channel_id=1, source_target_pairs={{0,48},{16,0},{32,16},{48,32},{64,112},{80,64},{96,80},{112,96},{1... | collective-permute-start | bytes 786440 | tf_op jit(solution)/shard_map/ppermute | solution.py:204
  103.3 7.9 %collective-permute-start.39 = (bf16[512,256]{1,0:T(8,128)(2,1)S(1)}, bf16[512,256]{1,0:T(8,128)(2,1)S(1)}, u32[]{:S(2)}, u32[]{:S(2)}) collective-permute-start(bf16[512,256]{1,0:T(8,128)(2,1)S(1)} %get-tuple-element.76), channel_id=1, source_target_pairs={{0,64},{16,80},{32,96},{48,112},{64,0},{80,16},{96,32},{112,48},{1... | collective-permute-start | bytes 786440 | tf_op jit(solution)/shard_map/ppermute | solution.py:205
  104.2 6.1 %collective-permute-start.36 = (bf16[64,512]{1,0:T(8,128)(2,1)S(1)}, bf16[64,512]{1,0:T(8,128)(2,1)S(1)}, u32[]{:S(2)}, u32[]{:S(2)}) collective-permute-start(bf16[64,512]{1,0:T(8,128)(2,1)S(1)} %fusion.11), channel_id=1, source_target_pairs={{0,16},{16,0},{32,48},{48,32},{64,80},{80,64},{96,112},{112,96},{1... | collective-permute-start | bytes 196616 | tf_op jit(solution)/shard_map/ppermute | solution.py:323
  107.8 24.6 %collective-permute-start.45 = (bf16[512,256]{1,0:T(8,128)(2,1)S(1)}, bf16[512,256]{1,0:T(8,128)(2,1)S(1)}, u32[]{:S(2)}, u32[]{:S(2)}) collective-permute-start(bf16[512,256]{1,0:T(8,128)(2,1)S(1)} %get-tuple-element.82), channel_id=1, source_target_pairs={{0,48},{16,0},{32,16},{48,32},{64,112},{80,64},{96,80},{112,96},{1... | collective-permute-start | bytes 786440 | tf_op jit(solution)/shard_map/ppermute | solution.py:207
  110.3 22.1 %collective-permute-start.44 = (bf16[512,256]{1,0:T(8,128)(2,1)S(1)}, bf16[512,256]{1,0:T(8,128)(2,1)S(1)}, u32[]{:S(2)}, u32[]{:S(2)}) collective-permute-start(bf16[512,256]{1,0:T(8,128)(2,1)S(1)} %get-tuple-element.80), channel_id=1, source_target_pairs={{0,16},{16,32},{32,48},{48,0},{64,80},{80,96},{96,112},{112,64},{1... | collective-permute-start | bytes 786440 | tf_op jit(solution)/shard_map/ppermute | solution.py:206
  111.2 9.8 %collective-permute-start.40 = (bf16[64,512]{1,0:T(8,128)(2,1)S(1)}, bf16[64,512]{1,0:T(8,128)(2,1)S(1)}, u32[]{:S(2)}, u32[]{:S(2)}) collective-permute-start(bf16[64,512]{1,0:T(8,128)(2,1)S(1)} %convert_element_type.185), channel_id=1, source_target_pairs={{0,48},{16,32},{32,16},{48,0},{64,112},{80,96},{96,80},{112,64},{1... | collective-permute-start | bytes 196616 | tf_op jit(solution)/shard_map/ppermute | solution.py:323
  113.8 18.6 %collective-permute-start.47 = (bf16[512,256]{1,0:T(8,128)(2,1)S(1)}, bf16[512,256]{1,0:T(8,128)(2,1)S(1)}, u32[]{:S(2)}, u32[]{:S(2)}) collective-permute-start(bf16[512,256]{1,0:T(8,128)(2,1)S(1)} %add_convert_fusion.1), channel_id=1, source_target_pairs={{0,64},{16,80},{32,96},{48,112},{64,0},{80,16},{96,32},{112,48},{1... | collective-permute-start | bytes 786440 | tf_op jit(solution)/shard_map/ppermute | solution.py:211
  121.0 5.6 %collective-permute-start.41 = (bf16[64,512]{1,0:T(8,128)(2,1)S(1)}, bf16[64,512]{1,0:T(8,128)(2,1)S(1)}, u32[]{:S(2)}, u32[]{:S(2)}) collective-permute-start(bf16[64,512]{1,0:T(8,128)(2,1)S(1)} %add_convert_fusion.6), channel_id=1, source_target_pairs={{0,6},{1,7},{2,4},{3,5},{4,2},{5,3},{6,0},{7,1},{8,14},{9,15},{10,... | collective-permute-start | bytes 196616 | tf_op jit(solution)/shard_map/ppermute | solution.py:308
  121.1 11.3 %collective-permute-start.46 = (bf16[512,256]{1,0:T(8,128)(2,1)S(1)}, bf16[512,256]{1,0:T(8,128)(2,1)S(1)}, u32[]{:S(2)}, u32[]{:S(2)}) collective-permute-start(bf16[512,256]{1,0:T(8,128)(2,1)S(1)} %add_convert_fusion.2), channel_id=1, source_target_pairs={{0,32},{16,48},{32,0},{48,16},{64,96},{80,112},{96,64},{112,80},{1... | collective-permute-start | bytes 786440 | tf_op jit(solution)/shard_map/ppermute | solution.py:210
  126.7 5.0 %collective-permute-start.42 = (bf16[128,512]{1,0:T(8,128)(2,1)S(1)}, bf16[128,512]{1,0:T(8,128)(2,1)S(1)}, u32[]{:S(2)}, u32[]{:S(2)}) collective-permute-start(bf16[128,512]{1,0:T(8,128)(2,1)S(1)} %fusion.9), channel_id=1, source_target_pairs={{0,2},{1,3},{2,0},{3,1},{4,6},{5,7},{6,4},{7,5},{8,10},{9,11},{10,... | collective-permute-start | bytes 393224 | tf_op jit(solution)/shard_map/ppermute | solution.py:308
  132.3 1.6 %collective-permute-start.43 = (bf16[256,512]{1,0:T(8,128)(2,1)S(1)}, bf16[256,512]{1,0:T(8,128)(2,1)S(1)}, u32[]{:S(2)}, u32[]{:S(2)}) collective-permute-start(bf16[256,512]{1,0:T(8,128)(2,1)S(1)} %fusion.5), channel_id=1, source_target_pairs={{0,1},{1,0},{2,3},{3,2},{4,5},{5,4},{6,7},{7,6},{8,9},{9,8},{10,11... | collective-permute-start | bytes 786440 | tf_op jit(solution)/shard_map/ppermute | solution.py:308
  (3 other events, 113.4 us)

commit v4 on v3

--- a/solution.py
+++ b/solution.py
@@ -183,6 +183,22 @@
     )(kept, met)
 
 
+def sum_turned(terms):
+    rows, width = terms[0].shape
+
+    def body(*refs):
+        refs[-1][...] = sum(t[...].astype(F32) for t in refs[:-1]).T.astype(BF)
+
+    return pl.pallas_call(
+        body,
+        in_specs=[VMEM] * len(terms),
+        out_specs=VMEM,
+        out_shape=jax.ShapeDtypeStruct((width, rows), BF),
+        compiler_params=pltpu.CompilerParams(vmem_limit_bytes=4 * 1024 * 1024),
+        name="sum_turned",
+    )(*terms)
+
+
 def gather(block, axis, pair, step, between):
     far = lax.ppermute(block, axis, pair)
     near2 = lax.ppermute(block, axis, step(2))
@@ -210,7 +226,7 @@
     near2 = lax.ppermute(for_two.astype(BF), axis, step(2))
     met = lax.ppermute(for_pair.astype(BF), axis, pair)
     terms = [own[0], near1, near3, near2, met]
-    return sum(t.astype(F32) for t in terms), (up, down, across), (near1, near3)
+    return terms, (up, down, across), (near1, near3)
 
 
 def local(adj_tiles, tile_rows, tile_cols, tile_counts, features, weight, node_grad):
@@ -267,8 +283,8 @@
     for start in (0, half):
         sent, kept = spread(forward, held, column, col_devices, start, (RING, RING), False)
         pairs.append(add_pairs(kept, lax.ppermute(sent, "col", swap)))
-    agg, _, _ = scatter(pairs[1], pairs[0], "col", yl_swap, along_z)
-    agg = agg.astype(BF)
+    terms, _, _ = scatter(pairs[1], pairs[0], "col", yl_swap, along_z)
+    agg = sum(t.astype(F32) for t in terms).astype(BF)
 
     pre = jnp.dot(agg, weight, preferred_element_type=F32)
     node_out = jax.nn.silu(pre).astype(BF)
@@ -290,8 +306,8 @@
         spread(backward, held, own + other, row_devices, start, (1,) * RING, True)
         for start in (0, RING)
     ]
-    summed, for_far, for_own = scatter(backs[1], backs[0], "row", yh_swap, along_x)
-    feature_grad = summed.T.astype(BF)
+    terms, for_far, for_own = scatter(backs[1], backs[0], "row", yh_swap, along_x)
+    feature_grad = sum_turned(terms)
 
     def flips(axis, bits):
         n = row_devices if axis == "row" else col_devices

time: 138 us -> 137 us (level)
  starting transfers between devices: 47.9 us -> 42.3 us
  Pallas kernels: 18.5 us -> 23.6 us
    ppermute x2, waiting for transfers between devices: 0.01 us -> 6.76 us  [scatter(): near3 = lax.ppermute(own[3], axis, step(3))]
    ppermute x2, waiting for transfers between devices: 8.27 us -> 3.38 us  [scatter(): near1 = lax.ppermute(own[1], axis, step(1))]
    ppermute x4, starting transfers between devices: 7.37 us -> 2.96 us  [local(): share = share + lax.ppermute(share.astype(BF), *flips(*way)).astype(F32)]
    ppermute x4, waiting for transfers between devices: 6 us -> 2.1 us  [local(): share = share + lax.ppermute(share.astype(BF), *flips(*way)).astype(F32)]
    ppermute x3, waiting for transfers between devices: 10.1 us -> 6.7 us  [doubled(): met = lax.ppermute(block, *way)]
    pallas_call x4, Pallas kernels: 14.5 us -> 17.5 us  [spread(): pl.pallas_call(body, in_specs=[SMEM] + [VMEM] * (1 + n_in), out_specs=[VM...]
    ppermute x2, waiting for transfers between devices: 0.01 us -> 2.45 us  [scatter(): met = lax.ppermute(for_pair.astype(BF), axis, pair)]
    ppermute x2, starting transfers between devices: 5.76 us -> 8 us  [scatter(): down = lax.ppermute(far[3], axis, step(3))]
  transfers between devices with their start and end apart: 48 -> 48, of which waited for: 18 -> 20; matrix products, arithmetic and copies ran while one was open for 2% -> 2% of each run, Pallas kernels for 11% -> 14%
where the time goes in v4:
time: 137 us; the launch traced here: 136 us
  waiting for transfers between devices  61.9 us (45%)
  starting transfers between devices  42.3 us (31%)
  Pallas kernels  23.6 us (17%)
  other arithmetic  4.17 us (3%)
  matrix products  1.84 us (1%)
  between operations  1.73 us (1%)
    pallas_call x4, Pallas kernels, spread(): pl.pallas_call(body, in_specs=[SMEM] + [VMEM] * (1 + n_in), out_specs=[VM...  17.5 us
    ppermute x2, waiting for transfers between devices, gather(): far1 = lax.ppermute(far, axis, step(3))  9.07 us
    ppermute x2, starting transfers between devices, scatter(): down = lax.ppermute(far[3], axis, step(3))  8 us
    ppermute x2, waiting for transfers between devices, gather(): far = lax.ppermute(block, axis, pair)  6.93 us
    ppermute x2, waiting for transfers between devices, scatter(): near3 = lax.ppermute(own[3], axis, step(3))  6.76 us
    ppermute x3, waiting for transfers between devices, doubled(): met = lax.ppermute(block, *way)  6.7 us
    ppermute x2, starting transfers between devices, scatter(): near3 = lax.ppermute(own[3], axis, step(3))  6.53 us
    ppermute x3, waiting for transfers between devices, halved(): return mine + lax.ppermute(yours.astype(BF), *way).astype(F32)  5.65 us
  transfers between devices with their start and end apart: 48, of which 20 were waited for; matrix products, arithmetic and copies ran while one was open for 2% of the time, Pallas kernels for 14%

profile of v4, /device:TPU:0, one launch (start us, length us, event | category | flops | bytes accessed | tf_op | source)
XLA Modules:
  0.0 135.7 jit_solution(237565820136327832)
XLA Ops:
  0.7 3.2 %collective-permute-start = (bf16[256,512]{1,0:T(8,128)(2,1)}, bf16[256,512]{1,0:T(8,128)(2,1)S(1)}, u32[]{:S(2)}, u32[]{:S(2)}) collective-permute-start(bf16[256,512]{1,0:T(8,128)(2,1)} %refs_2_.1), channel_id=1, source_target_pairs={{0,32},{16,48},{32,0},{48,16},{64,96},{80,112},{96,64},{112,80},{1... | collective-permute-start | bytes 786440 | tf_op jit(solution)/shard_map/ppermute | solution.py:204
  3.9 3.2 %collective-permute-start.3 = (bf16[256,512]{1,0:T(8,128)(2,1)}, bf16[256,512]{1,0:T(8,128)(2,1)S(1)}, u32[]{:S(2)}, u32[]{:S(2)}) collective-permute-start(bf16[256,512]{1,0:T(8,128)(2,1)} %refs_2_.1), channel_id=1, source_target_pairs={{0,64},{16,80},{32,96},{48,112},{64,0},{80,16},{96,32},{112,48},{1... | collective-permute-start | bytes 786440 | tf_op jit(solution)/shard_map/ppermute | solution.py:203
  7.1 1.1 collective-permute-start.1
  8.2 0.9 collective-permute-start.2
  9.7 0.7 add_bitcast_fusion
  10.4 4.9 %schedule.1 = (s32[241]{0:T(256)S(1)}, s32[201]{0:T(256)S(1)}, bf16[80,256,256]{2,1,0:T(8,128)(2,1)S(1)}) custom-call(s32[80]{0:T(128)S(1)} %get-tuple-element.90.fd, s32[80]{0:T(128)S(1)} %get-tuple-element.93.fr, s32[80]{0:T(128)S(1)} %get-tuple-element.94.bd, s32[80]{0:T(128)S(1)} %get-tuple-element.89.br, s32[1]{0:T(128)} %bitcast.37.n, ...), custom_call_target="tpu_custom_call" | custom-call | tf_op jit(solution)/shard_map/schedule/pallas_call | solution.py:87
  15.3 2.8 %collective-permute-start.4 = (bf16[256,512]{1,0:T(8,128)(2,1)S(1)}, bf16[256,512]{1,0:T(8,128)(2,1)S(1)}, u32[]{:S(2)}, u32[]{:S(2)}) collective-permute-start(bf16[256,512]{1,0:T(8,128)(2,1)S(1)} %collective-permute-done.3.refs_6_), channel_id=1, source_target_pairs={{0,48},{16,0},{32,16},{48,32},{64,112},{80,64},{96,80},{112,96},{1... | collective-permute-start | bytes 786440 | tf_op jit(solution)/shard_map/ppermute | solution.py:208
  18.1 0.4 collective-permute-start.6
  18.6 3.5 %collective-permute-done.4.refs_7_ = bf16[256,512]{1,0:T(8,128)(2,1)S(1)} collective-permute-done((bf16[256,512]{1,0:T(8,128)(2,1)S(1)}, bf16[256,512]{1,0:T(8,128)(2,1)S(1)}, u32[]{:S(2)}, u32[]{:S(2)}) %collective-permute-start.4) | collective-permute-done | bytes 262176 | tf_op jit(solution)/shard_map/ppermute | solution.py:208
  22.0 4.0 %collective-permute-done.5.refs_8_ = bf16[256,512]{1,0:T(8,128)(2,1)S(1)} collective-permute-done((bf16[256,512]{1,0:T(8,128)(2,1)S(1)}, bf16[256,512]{1,0:T(8,128)(2,1)S(1)}, u32[]{:S(2)}, u32[]{:S(2)}) %collective-permute-start.5) | collective-permute-done | bytes 262176 | tf_op jit(solution)/shard_map/ppermute | solution.py:210
  26.0 4.5 %spread.3 = (bf16[4,256,512]{2,1,0:T(8,128)(2,1)S(1)}, bf16[4,256,512]{2,1,0:T(8,128)(2,1)S(1)}) custom-call(s32[241]{0:T(256)S(1)} %get-tuple-element.49.refs_0_, bf16[80,256,256]{2,1,0:T(8,128)(2,1)S(1)} %get-tuple-element.50.refs_1_, bf16[256,512]{1,0:T(8,128)(2,1)S(1)} %copy-done.1, bf16[256,512]{1,0:T(8,128)(2,1)S(1)} %collective-permute-done.1.refs_3_, ...), custom_call_target="tpu_custom_call" | custom-call | flops 53687091200 | bytes 10485760 | tf_op jit(solution)/shard_map/spread/pallas_call | solution.py:152
  30.6 4.9 %spread.2 = (bf16[4,256,512]{2,1,0:T(8,128)(2,1)S(1)}, bf16[4,256,512]{2,1,0:T(8,128)(2,1)S(1)}) custom-call(s32[241]{0:T(256)S(1)} %get-tuple-element.49.refs_0_, bf16[80,256,256]{2,1,0:T(8,128)(2,1)S(1)} %get-tuple-element.50.refs_1_, bf16[256,512]{1,0:T(8,128)(2,1)S(1)} %copy-done.1, bf16[256,512]{1,0:T(8,128)(2,1)S(1)} %collective-permute-done.1.refs_3_, ...), custom_call_target="tpu_custom_call" | custom-call | flops 53687091200 | bytes 10485760 | tf_op jit(solution)/shard_map/spread/pallas_call | solution.py:152
  35.8 4.8 %collective-permute-start.14 = (bf16[256,512]{1,0:T(8,128)(2,1)S(1)}, bf16[256,512]{1,0:T(8,128)(2,1)S(1)}, u32[]{:S(2)}, u32[]{:S(2)}) collective-permute-start(bf16[256,512]{1,0:T(8,128)(2,1)S(1)} %get-tuple-element.63), channel_id=1, source_target_pairs={{0,6},{1,7},{2,0},{3,1},{4,2},{5,3},{6,4},{7,5},{8,14},{9,15},{10,... | collective-permute-start | bytes 786440 | tf_op jit(solution)/shard_map/ppermute | solution.py:220
  40.7 3.3 %collective-permute-start.9 = (bf16[256,512]{1,0:T(8,128)(2,1)S(1)}, bf16[256,512]{1,0:T(8,128)(2,1)S(1)}, u32[]{:S(2)}, u32[]{:S(2)}) collective-permute-start(bf16[256,512]{1,0:T(8,128)(2,1)S(1)} %get-tuple-element.56), channel_id=1, source_target_pairs={{0,6},{1,7},{2,0},{3,1},{4,2},{5,3},{6,4},{7,5},{8,14},{9,15},{10,... | collective-permute-start | bytes 786440 | tf_op jit(solution)/shard_map/ppermute | solution.py:223
  44.0 3.2 %collective-permute-done.14 = bf16[256,512]{1,0:T(8,128)(2,1)S(1)} collective-permute-done((bf16[256,512]{1,0:T(8,128)(2,1)S(1)}, bf16[256,512]{1,0:T(8,128)(2,1)S(1)}, u32[]{:S(2)}, u32[]{:S(2)}) %collective-permute-start.14) | collective-permute-done | bytes 262176 | tf_op jit(solution)/shard_map/ppermute | solution.py:220
  47.2 3.7 %collective-permute-done.13 = bf16[256,512]{1,0:T(8,128)(2,1)S(1)} collective-permute-done((bf16[256,512]{1,0:T(8,128)(2,1)S(1)}, bf16[256,512]{1,0:T(8,128)(2,1)S(1)}, u32[]{:S(2)}, u32[]{:S(2)}) %collective-permute-start.13) | collective-permute-done | bytes 262176 | tf_op jit(solution)/shard_map/ppermute | solution.py:219
  51.3 6.8 %collective-permute-done.9 = bf16[256,512]{1,0:T(8,128)(2,1)S(1)} collective-permute-done((bf16[256,512]{1,0:T(8,128)(2,1)S(1)}, bf16[256,512]{1,0:T(8,128)(2,1)S(1)}, u32[]{:S(2)}, u32[]{:S(2)}) %collective-permute-start.9) | collective-permute-done | bytes 262176 | tf_op jit(solution)/shard_map/ppermute | solution.py:223
  58.1 3.4 %collective-permute-done.8 = bf16[256,512]{1,0:T(8,128)(2,1)S(1)} collective-permute-done((bf16[256,512]{1,0:T(8,128)(2,1)S(1)}, bf16[256,512]{1,0:T(8,128)(2,1)S(1)}, u32[]{:S(2)}, u32[]{:S(2)}) %collective-permute-start.8) | collective-permute-done | bytes 262176 | tf_op jit(solution)/shard_map/ppermute | solution.py:222
  61.6 1.2 multiply_convert_fusion
  63.3 0.6 collective-permute-start.20
  63.9 6.9 %collective-permute-done.16.refs_6_ = bf16[512,256]{1,0:T(8,128)(2,1)S(1)} collective-permute-done((bf16[512,256]{1,0:T(8,128)(2,1)S(1)}, bf16[512,256]{1,0:T(8,128)(2,1)S(1)}, u32[]{:S(2)}, u32[]{:S(2)}) %collective-permute-start.16) | collective-permute-done | bytes 262176 | tf_op jit(solution)/shard_map/ppermute | solution.py:203
  71.3 0.7 collective-permute-start.25
  72.0 0.8 collective-permute-start.19
  72.8 1.2 collective-permute-start.21
  74.5 1.8 %collective-permute-start.22 = (bf16[512,256]{1,0:T(8,128)(2,1)S(1)}, bf16[512,256]{1,0:T(8,128)(2,1)S(1)}, u32[]{:S(2)}, u32[]{:S(2)}) collective-permute-start(bf16[512,256]{1,0:T(8,128)(2,1)S(1)} %collective-permute-done.16.refs_6_), channel_id=1, source_target_pairs={{0,2},{1,3},{2,4},{3,5},{4,6},{5,7},{6,0},{7,1},{8,10},{9,11},{10,... | collective-permute-start | bytes 786440 | tf_op jit(solution)/shard_map/ppermute | solution.py:209
  76.3 4.2 %collective-permute-done.25.refs_3_ = bf16[512,256]{1,0:T(8,128)(2,1)S(1)} collective-permute-done((bf16[512,256]{1,0:T(8,128)(2,1)S(1)}, bf16[512,256]{1,0:T(8,128)(2,1)S(1)}, u32[]{:S(2)}, u32[]{:S(2)}) %collective-permute-start.25) | collective-permute-done | bytes 262176 | tf_op jit(solution)/shard_map/ppermute | solution.py:205
  80.5 5.6 %collective-permute-done.19.refs_7_ = bf16[512,256]{1,0:T(8,128)(2,1)S(1)} collective-permute-done((bf16[512,256]{1,0:T(8,128)(2,1)S(1)}, bf16[512,256]{1,0:T(8,128)(2,1)S(1)}, u32[]{:S(2)}, u32[]{:S(2)}) %collective-permute-start.19) | collective-permute-done | bytes 262176 | tf_op jit(solution)/shard_map/ppermute | solution.py:208
  86.1 0.5 collective-permute-start.29
  86.6 1.8 %collective-permute-done.18 = bf16[128,512]{1,0:T(8,128)(2,1)S(1)} collective-permute-done((bf16[128,512]{1,0:T(8,128)(2,1)S(1)}, bf16[128,512]{1,0:T(8,128)(2,1)S(1)}, u32[]{:S(2)}, u32[]{:S(2)}) %collective-permute-start.18) | collective-permute-done | bytes 131104 | tf_op jit(solution)/shard_map/ppermute | solution.py:321
  88.6 0.5 collective-permute-done.26.refs_5_
  90.5 3.8 %collective-permute-done.23 = bf16[64,512]{1,0:T(8,128)(2,1)S(1)} collective-permute-done((bf16[64,512]{1,0:T(8,128)(2,1)S(1)}, bf16[64,512]{1,0:T(8,128)(2,1)S(1)}, u32[]{:S(2)}, u32[]{:S(2)}) %collective-permute-start.23) | collective-permute-done | bytes 65568 | tf_op jit(solution)/shard_map/ppermute | solution.py:321
  94.7 1.1 collective-permute-done.34.refs_17_
  95.9 4.0 %spread_back.2 = (bf16[512,256]{1,0:T(8,128)(2,1)S(1)}, bf16[512,256]{1,0:T(8,128)(2,1)S(1)}, bf16[512,256]{1,0:T(8,128)(2,1)S(1)}, bf16[512,256]{1,0:T(8,128)(2,1)S(1)}) custom-call(s32[201]{0:T(256)S(1)} %get-tuple-element.73.refs_0_, bf16[80,256,256]{2,1,0:T(8,128)(2,1)S(1)} %get-tuple-element.50.refs_1_, bf16[512,256]{1,0:T(8,128)(2,1)S(1)} %fusion.refs_2_, ...), custom_call_target="tpu_custom_call" | custom-call | flops 53687091200 | bytes 10485760 | tf_op jit(solution)/shard_map/spread_back/pallas_call | solution.py:152
  99.9 1.9 %collective-permute-start.35 = (bf16[64,512]{1,0:T(8,128)(2,1)S(1)}, bf16[64,512]{1,0:T(8,128)(2,1)S(1)}, u32[]{:S(2)}, u32[]{:S(2)}) collective-permute-start(bf16[64,512]{1,0:T(8,128)(2,1)S(1)} %convert_element_type.160), channel_id=1, source_target_pairs={{0,64},{16,80},{32,96},{48,112},{64,0},{80,16},{96,32},{112,48},{1... | collective-permute-start | bytes 196616 | tf_op jit(solution)/shard_map/ppermute | solution.py:339
  101.8 3.2 %collective-permute-start.38 = (bf16[512,256]{1,0:T(8,128)(2,1)S(1)}, bf16[512,256]{1,0:T(8,128)(2,1)S(1)}, u32[]{:S(2)}, u32[]{:S(2)}) collective-permute-start(bf16[512,256]{1,0:T(8,128)(2,1)S(1)} %get-tuple-element.77), channel_id=1, source_target_pairs={{0,48},{16,0},{32,16},{48,32},{64,112},{80,64},{96,80},{112,96},{1... | collective-permute-start | bytes 786440 | tf_op jit(solution)/shard_map/ppermute | solution.py:220
  105.1 1.7 %collective-permute-start.39 = (bf16[512,256]{1,0:T(8,128)(2,1)S(1)}, bf16[512,256]{1,0:T(8,128)(2,1)S(1)}, u32[]{:S(2)}, u32[]{:S(2)}) collective-permute-start(bf16[512,256]{1,0:T(8,128)(2,1)S(1)} %get-tuple-element.76), channel_id=1, source_target_pairs={{0,64},{16,80},{32,96},{48,112},{64,0},{80,16},{96,32},{112,48},{1... | collective-permute-start | bytes 786440 | tf_op jit(solution)/shard_map/ppermute | solution.py:221
  107.1 4.1 %spread_back.3 = (bf16[512,256]{1,0:T(8,128)(2,1)S(1)}, bf16[512,256]{1,0:T(8,128)(2,1)S(1)}, bf16[512,256]{1,0:T(8,128)(2,1)S(1)}, bf16[512,256]{1,0:T(8,128)(2,1)S(1)}) custom-call(s32[201]{0:T(256)S(1)} %get-tuple-element.73.refs_0_, bf16[80,256,256]{2,1,0:T(8,128)(2,1)S(1)} %get-tuple-element.50.refs_1_, bf16[512,256]{1,0:T(8,128)(2,1)S(1)} %fusion.refs_2_, ...), custom_call_target="tpu_custom_call" | custom-call | flops 53687091200 | bytes 10485760 | tf_op jit(solution)/shard_map/spread_back/pallas_call | solution.py:152
  111.4 1.8 %collective-permute-done.39 = bf16[512,256]{1,0:T(8,128)(2,1)S(1)} collective-permute-done((bf16[512,256]{1,0:T(8,128)(2,1)S(1)}, bf16[512,256]{1,0:T(8,128)(2,1)S(1)}, u32[]{:S(2)}, u32[]{:S(2)}) %collective-permute-start.39) | collective-permute-done | bytes 262176 | tf_op jit(solution)/shard_map/ppermute | solution.py:221
  113.6 3.2 %collective-permute-start.45 = (bf16[512,256]{1,0:T(8,128)(2,1)S(1)}, bf16[512,256]{1,0:T(8,128)(2,1)S(1)}, u32[]{:S(2)}, u32[]{:S(2)}) collective-permute-start(bf16[512,256]{1,0:T(8,128)(2,1)S(1)} %get-tuple-element.82), channel_id=1, source_target_pairs={{0,48},{16,0},{32,16},{48,32},{64,112},{80,64},{96,80},{112,96},{1... | collective-permute-start | bytes 786440 | tf_op jit(solution)/shard_map/ppermute | solution.py:223
  116.8 2.0 %collective-permute-done.40 = bf16[64,512]{1,0:T(8,128)(2,1)S(1)} collective-permute-done((bf16[64,512]{1,0:T(8,128)(2,1)S(1)}, bf16[64,512]{1,0:T(8,128)(2,1)S(1)}, u32[]{:S(2)}, u32[]{:S(2)}) %collective-permute-start.40) | collective-permute-done | bytes 65568 | tf_op jit(solution)/shard_map/ppermute | solution.py:339
  118.8 1.3 collective-permute-start.41
  120.2 4.1 %collective-permute-done.41 = bf16[64,512]{1,0:T(8,128)(2,1)S(1)} collective-permute-done((bf16[64,512]{1,0:T(8,128)(2,1)S(1)}, bf16[64,512]{1,0:T(8,128)(2,1)S(1)}, u32[]{:S(2)}, u32[]{:S(2)}) %collective-permute-start.41) | collective-permute-done | bytes 65568 | tf_op jit(solution)/shard_map/ppermute | solution.py:324
  124.8 2.3 %collective-permute-start.47 = (bf16[512,256]{1,0:T(8,128)(2,1)S(1)}, bf16[512,256]{1,0:T(8,128)(2,1)S(1)}, u32[]{:S(2)}, u32[]{:S(2)}) collective-permute-start(bf16[512,256]{1,0:T(8,128)(2,1)S(1)} %add_convert_fusion), channel_id=1, source_target_pairs={{0,64},{16,80},{32,96},{48,112},{64,0},{80,16},{96,32},{112,48},{1... | collective-permute-start | bytes 786440 | tf_op jit(solution)/shard_map/ppermute | solution.py:227
  127.0 2.6 %collective-permute-done.42 = bf16[128,512]{1,0:T(8,128)(2,1)S(1)} collective-permute-done((bf16[128,512]{1,0:T(8,128)(2,1)S(1)}, bf16[128,512]{1,0:T(8,128)(2,1)S(1)}, u32[]{:S(2)}, u32[]{:S(2)}) %collective-permute-start.42) | collective-permute-done | bytes 131104 | tf_op jit(solution)/shard_map/ppermute | solution.py:324
  129.6 0.5 fusion.5
  130.3 2.4 %collective-permute-done.47.refs_4_ = bf16[512,256]{1,0:T(8,128)(2,1)S(1)} collective-permute-done((bf16[512,256]{1,0:T(8,128)(2,1)S(1)}, bf16[512,256]{1,0:T(8,128)(2,1)S(1)}, u32[]{:S(2)}, u32[]{:S(2)}) %collective-permute-start.47) | collective-permute-done | bytes 262176 | tf_op jit(solution)/shard_map/ppermute | solution.py:227
  132.7 0.9 sum_turned.1
  133.7 2.0 %fusion.3 = f32[512,512]{1,0:T(8,128)} fusion(s32[]{:T(128)S(6)} %mul.76, bf16[256,512]{1,0:T(8,128)(2,1)S(1)} %collective-permute-done.43, bf16[256,512]{1,0:T(8,128)(2,1)S(1)} %fusion.5), kind=kLoop, calls=%fused_computation.8 | loop fusion | flops 1572864 | bytes 1572868 | tf_op jit(solution)/shard_map/convert_element_type | solution.py:343
  (86 shorter events, 5.8 us)
Async XLA Ops:
  0.7 14.6 %collective-permute-start = (bf16[256,512]{1,0:T(8,128)(2,1)}, bf16[256,512]{1,0:T(8,128)(2,1)S(1)}, u32[]{:S(2)}, u32[]{:S(2)}) collective-permute-start(bf16[256,512]{1,0:T(8,128)(2,1)} %refs_2_.1), channel_id=1, source_target_pairs={{0,32},{16,48},{32,0},{48,16},{64,96},{80,112},{96,64},{112,80},{1... | collective-permute-start | bytes 786440 | tf_op jit(solution)/shard_map/ppermute | solution.py:204
  3.9 11.5 %collective-permute-start.3 = (bf16[256,512]{1,0:T(8,128)(2,1)}, bf16[256,512]{1,0:T(8,128)(2,1)S(1)}, u32[]{:S(2)}, u32[]{:S(2)}) collective-permute-start(bf16[256,512]{1,0:T(8,128)(2,1)} %refs_2_.1), channel_id=1, source_target_pairs={{0,64},{16,80},{32,96},{48,112},{64,0},{80,16},{96,32},{112,48},{1... | collective-permute-start | bytes 786440 | tf_op jit(solution)/shard_map/ppermute | solution.py:203
  7.1 11.5 %collective-permute-start.1 = (bf16[256,512]{1,0:T(8,128)(2,1)}, bf16[256,512]{1,0:T(8,128)(2,1)S(1)}, u32[]{:S(2)}, u32[]{:S(2)}) collective-permute-start(bf16[256,512]{1,0:T(8,128)(2,1)} %refs_2_.1), channel_id=1, source_target_pairs={{0,48},{16,0},{32,16},{48,32},{64,112},{80,64},{96,80},{112,96},{1... | collective-permute-start | bytes 786440 | tf_op jit(solution)/shard_map/ppermute | solution.py:205
  8.2 10.4 %collective-permute-start.2 = (bf16[256,512]{1,0:T(8,128)(2,1)}, bf16[256,512]{1,0:T(8,128)(2,1)S(1)}, u32[]{:S(2)}, u32[]{:S(2)}) collective-permute-start(bf16[256,512]{1,0:T(8,128)(2,1)} %refs_2_.1), channel_id=1, source_target_pairs={{0,16},{16,32},{32,48},{48,0},{64,80},{80,96},{96,112},{112,64},{1... | collective-permute-start | bytes 786440 | tf_op jit(solution)/shard_map/ppermute | solution.py:206
  15.3 6.7 %collective-permute-start.4 = (bf16[256,512]{1,0:T(8,128)(2,1)S(1)}, bf16[256,512]{1,0:T(8,128)(2,1)S(1)}, u32[]{:S(2)}, u32[]{:S(2)}) collective-permute-start(bf16[256,512]{1,0:T(8,128)(2,1)S(1)} %collective-permute-done.3.refs_6_), channel_id=1, source_target_pairs={{0,48},{16,0},{32,16},{48,32},{64,112},{80,64},{96,80},{112,96},{1... | collective-permute-start | bytes 786440 | tf_op jit(solution)/shard_map/ppermute | solution.py:208
  18.1 7.9 %collective-permute-start.5 = (bf16[256,512]{1,0:T(8,128)(2,1)S(1)}, bf16[256,512]{1,0:T(8,128)(2,1)S(1)}, u32[]{:S(2)}, u32[]{:S(2)}) collective-permute-start(bf16[256,512]{1,0:T(8,128)(2,1)S(1)} %collective-permute-done.refs_4_), channel_id=1, source_target_pairs={{0,64},{16,80},{32,96},{48,112},{64,0},{80,16},{96,32},{112,48},{1... | collective-permute-start | bytes 786440 | tf_op jit(solution)/shard_map/ppermute | solution.py:210
  18.1 7.9 %collective-permute-start.6 = (bf16[256,512]{1,0:T(8,128)(2,1)S(1)}, bf16[256,512]{1,0:T(8,128)(2,1)S(1)}, u32[]{:S(2)}, u32[]{:S(2)}) collective-permute-start(bf16[256,512]{1,0:T(8,128)(2,1)S(1)} %collective-permute-done.3.refs_6_), channel_id=1, source_target_pairs={{0,16},{16,32},{32,48},{48,0},{64,80},{80,96},{96,112},{112,64},{1... | collective-permute-start | bytes 786440 | tf_op jit(solution)/shard_map/ppermute | solution.py:209
  30.5 5.1 %collective-permute-start.10 = (bf16[4,256,512]{2,1,0:T(8,128)(2,1)S(1)}, bf16[4,256,512]{2,1,0:T(8,128)(2,1)S(1)}, u32[]{:S(2)}, u32[]{:S(2)}) collective-permute-start(bf16[4,256,512]{2,1,0:T(8,128)(2,1)S(1)} %get-tuple-element.59), channel_id=1, source_target_pairs={{0,1},{1,0},{2,3},{3,2},{4,5},{5,4},{6,7},{7,6},{8,9},{9,8},{10,11... | collective-permute-start | bytes 3145736 | tf_op jit(solution)/shard_map/ppermute | solution.py:285
  35.6 5.0 %collective-permute-start.7 = (bf16[4,256,512]{2,1,0:T(8,128)(2,1)S(1)}, bf16[4,256,512]{2,1,0:T(8,128)(2,1)S(1)}, u32[]{:S(2)}, u32[]{:S(2)}) collective-permute-start(bf16[4,256,512]{2,1,0:T(8,128)(2,1)S(1)} %get-tuple-element.53), channel_id=1, source_target_pairs={{0,1},{1,0},{2,3},{3,2},{4,5},{5,4},{6,7},{7,6},{8,9},{9,8},{10,11... | collective-permute-start | bytes 3145736 | tf_op jit(solution)/shard_map/ppermute | solution.py:285
  35.8 11.4 %collective-permute-start.14 = (bf16[256,512]{1,0:T(8,128)(2,1)S(1)}, bf16[256,512]{1,0:T(8,128)(2,1)S(1)}, u32[]{:S(2)}, u32[]{:S(2)}) collective-permute-start(bf16[256,512]{1,0:T(8,128)(2,1)S(1)} %get-tuple-element.63), channel_id=1, source_target_pairs={{0,6},{1,7},{2,0},{3,1},{4,2},{5,3},{6,4},{7,5},{8,14},{9,15},{10,... | collective-permute-start | bytes 786440 | tf_op jit(solution)/shard_map/ppermute | solution.py:220
  40.6 10.4 %collective-permute-start.13 = (bf16[256,512]{1,0:T(8,128)(2,1)S(1)}, bf16[256,512]{1,0:T(8,128)(2,1)S(1)}, u32[]{:S(2)}, u32[]{:S(2)}) collective-permute-start(bf16[256,512]{1,0:T(8,128)(2,1)S(1)} %get-tuple-element.62), channel_id=1, source_target_pairs={{0,2},{1,3},{2,4},{3,5},{4,6},{5,7},{6,0},{7,1},{8,10},{9,11},{10,... | collective-permute-start | bytes 786440 | tf_op jit(solution)/shard_map/ppermute | solution.py:219
  40.6 10.6 %collective-permute-start.11 = (bf16[256,512]{1,0:T(8,128)(2,1)S(1)}, bf16[256,512]{1,0:T(8,128)(2,1)S(1)}, u32[]{:S(2)}, u32[]{:S(2)}) collective-permute-start(bf16[256,512]{1,0:T(8,128)(2,1)S(1)} %get-tuple-element.60), channel_id=1, source_target_pairs={{0,8},{1,9},{2,10},{3,11},{4,12},{5,13},{6,14},{7,15},{8,0},{9,1},... | collective-permute-start | bytes 786440 | tf_op jit(solution)/shard_map/ppermute | solution.py:221
  40.7 17.4 %collective-permute-start.9 = (bf16[256,512]{1,0:T(8,128)(2,1)S(1)}, bf16[256,512]{1,0:T(8,128)(2,1)S(1)}, u32[]{:S(2)}, u32[]{:S(2)}) collective-permute-start(bf16[256,512]{1,0:T(8,128)(2,1)S(1)} %get-tuple-element.56), channel_id=1, source_target_pairs={{0,6},{1,7},{2,0},{3,1},{4,2},{5,3},{6,4},{7,5},{8,14},{9,15},{10,... | collective-permute-start | bytes 786440 | tf_op jit(solution)/shard_map/ppermute | solution.py:223
  44.0 17.4 %collective-permute-start.8 = (bf16[256,512]{1,0:T(8,128)(2,1)S(1)}, bf16[256,512]{1,0:T(8,128)(2,1)S(1)}, u32[]{:S(2)}, u32[]{:S(2)}) collective-permute-start(bf16[256,512]{1,0:T(8,128)(2,1)S(1)} %get-tuple-element.55), channel_id=1, source_target_pairs={{0,2},{1,3},{2,4},{3,5},{4,6},{5,7},{6,0},{7,1},{8,10},{9,11},{10,... | collective-permute-start | bytes 786440 | tf_op jit(solution)/shard_map/ppermute | solution.py:222
  51.0 10.4 %collective-permute-start.15 = (bf16[256,512]{1,0:T(8,128)(2,1)S(1)}, bf16[256,512]{1,0:T(8,128)(2,1)S(1)}, u32[]{:S(2)}, u32[]{:S(2)}) collective-permute-start(bf16[256,512]{1,0:T(8,128)(2,1)S(1)} %add_convert_fusion.3), channel_id=1, source_target_pairs={{0,8},{1,9},{2,10},{3,11},{4,12},{5,13},{6,14},{7,15},{8,0},{9,1},... | collective-permute-start | bytes 786440 | tf_op jit(solution)/shard_map/ppermute | solution.py:227
  51.2 10.2 %collective-permute-start.12 = (bf16[256,512]{1,0:T(8,128)(2,1)S(1)}, bf16[256,512]{1,0:T(8,128)(2,1)S(1)}, u32[]{:S(2)}, u32[]{:S(2)}) collective-permute-start(bf16[256,512]{1,0:T(8,128)(2,1)S(1)} %add_convert_fusion.4), channel_id=1, source_target_pairs={{0,4},{1,5},{2,6},{3,7},{4,0},{5,1},{6,2},{7,3},{8,12},{9,13},{10,... | collective-permute-start | bytes 786440 | tf_op jit(solution)/shard_map/ppermute | solution.py:226
  63.2 7.7 %collective-permute-start.16 = (bf16[512,256]{1,0:T(8,128)(2,1)S(1)}, bf16[512,256]{1,0:T(8,128)(2,1)S(1)}, u32[]{:S(2)}, u32[]{:S(2)}) collective-permute-start(bf16[512,256]{1,0:T(8,128)(2,1)S(1)} %fusion.refs_2_), channel_id=1, source_target_pairs={{0,8},{1,9},{2,10},{3,11},{4,12},{5,13},{6,14},{7,15},{8,0},{9,1},... | collective-permute-start | bytes 786440 | tf_op jit(solution)/shard_map/ppermute | solution.py:203
  63.3 9.6 %collective-permute-start.20 = (bf16[512,256]{1,0:T(8,128)(2,1)S(1)}, bf16[512,256]{1,0:T(8,128)(2,1)S(1)}, u32[]{:S(2)}, u32[]{:S(2)}) collective-permute-start(bf16[512,256]{1,0:T(8,128)(2,1)S(1)} %fusion.refs_2_), channel_id=1, source_target_pairs={{0,4},{1,5},{2,6},{3,7},{4,0},{5,1},{6,2},{7,3},{8,12},{9,13},{10,... | collective-permute-start | bytes 786440 | tf_op jit(solution)/shard_map/ppermute | solution.py:204
  71.2 2.9 %collective-permute-start.17 = (bf16[256,512]{1,0:T(8,128)(2,1)S(1)}, bf16[256,512]{1,0:T(8,128)(2,1)S(1)}, u32[]{:S(2)}, u32[]{:S(2)}) collective-permute-start(bf16[256,512]{1,0:T(8,128)(2,1)S(1)} %fusion.6), channel_id=1, source_target_pairs={{0,1},{1,0},{2,3},{3,2},{4,5},{5,4},{6,7},{7,6},{8,9},{9,8},{10,11... | collective-permute-start | bytes 786440 | tf_op jit(solution)/shard_map/ppermute | solution.py:321
  71.3 9.2 %collective-permute-start.25 = (bf16[512,256]{1,0:T(8,128)(2,1)S(1)}, bf16[512,256]{1,0:T(8,128)(2,1)S(1)}, u32[]{:S(2)}, u32[]{:S(2)}) collective-permute-start(bf16[512,256]{1,0:T(8,128)(2,1)S(1)} %fusion.refs_2_), channel_id=1, source_target_pairs={{0,6},{1,7},{2,0},{3,1},{4,2},{5,3},{6,4},{7,5},{8,14},{9,15},{10,... | collective-permute-start | bytes 786440 | tf_op jit(solution)/shard_map/ppermute | solution.py:205
  72.0 14.1 %collective-permute-start.19 = (bf16[512,256]{1,0:T(8,128)(2,1)S(1)}, bf16[512,256]{1,0:T(8,128)(2,1)S(1)}, u32[]{:S(2)}, u32[]{:S(2)}) collective-permute-start(bf16[512,256]{1,0:T(8,128)(2,1)S(1)} %collective-permute-done.16.refs_6_), channel_id=1, source_target_pairs={{0,6},{1,7},{2,0},{3,1},{4,2},{5,3},{6,4},{7,5},{8,14},{9,15},{10,... | collective-permute-start | bytes 786440 | tf_op jit(solution)/shard_map/ppermute | solution.py:208
  72.8 13.3 %collective-permute-start.21 = (bf16[512,256]{1,0:T(8,128)(2,1)S(1)}, bf16[512,256]{1,0:T(8,128)(2,1)S(1)}, u32[]{:S(2)}, u32[]{:S(2)}) collective-permute-start(bf16[512,256]{1,0:T(8,128)(2,1)S(1)} %collective-permute-done.20.refs_4_), channel_id=1, source_target_pairs={{0,8},{1,9},{2,10},{3,11},{4,12},{5,13},{6,14},{7,15},{8,0},{9,1},... | collective-permute-start | bytes 786440 | tf_op jit(solution)/shard_map/ppermute | solution.py:210
  74.2 14.3 %collective-permute-start.18 = (bf16[128,512]{1,0:T(8,128)(2,1)S(1)}, bf16[128,512]{1,0:T(8,128)(2,1)S(1)}, u32[]{:S(2)}, u32[]{:S(2)}) collective-permute-start(bf16[128,512]{1,0:T(8,128)(2,1)S(1)} %fusion.9), channel_id=1, source_target_pairs={{0,2},{1,3},{2,0},{3,1},{4,6},{5,7},{6,4},{7,5},{8,10},{9,11},{10,... | collective-permute-start | bytes 393224 | tf_op jit(solution)/shard_map/ppermute | solution.py:321
  74.5 14.0 %collective-permute-start.22 = (bf16[512,256]{1,0:T(8,128)(2,1)S(1)}, bf16[512,256]{1,0:T(8,128)(2,1)S(1)}, u32[]{:S(2)}, u32[]{:S(2)}) collective-permute-start(bf16[512,256]{1,0:T(8,128)(2,1)S(1)} %collective-permute-done.16.refs_6_), channel_id=1, source_target_pairs={{0,2},{1,3},{2,4},{3,5},{4,6},{5,7},{6,0},{7,1},{8,10},{9,11},{10,... | collective-permute-start | bytes 786440 | tf_op jit(solution)/shard_map/ppermute | solution.py:209
  80.5 8.6 %collective-permute-start.26 = (bf16[512,256]{1,0:T(8,128)(2,1)S(1)}, bf16[512,256]{1,0:T(8,128)(2,1)S(1)}, u32[]{:S(2)}, u32[]{:S(2)}) collective-permute-start(bf16[512,256]{1,0:T(8,128)(2,1)S(1)} %fusion.refs_2_), channel_id=1, source_target_pairs={{0,2},{1,3},{2,4},{3,5},{4,6},{5,7},{6,0},{7,1},{8,10},{9,11},{10,... | collective-permute-start | bytes 786440 | tf_op jit(solution)/shard_map/ppermute | solution.py:206
  86.1 3.1 %collective-permute-start.27 = (bf16[512,256]{1,0:T(8,128)(2,1)S(1)}, bf16[512,256]{1,0:T(8,128)(2,1)S(1)}, u32[]{:S(2)}, u32[]{:S(2)}) collective-permute-start(bf16[512,256]{1,0:T(8,128)(2,1)S(1)} %fusion.refs_2_), channel_id=1, source_target_pairs={{0,1},{1,0},{2,3},{3,2},{4,5},{5,4},{6,7},{7,6},{8,9},{9,8},{10,11... | collective-permute-start | bytes 786440 | tf_op jit(solution)/shard_map/ppermute | solution.py:300
  86.1 4.0 %collective-permute-start.29 = (bf16[512,256]{1,0:T(8,128)(2,1)S(1)}, bf16[512,256]{1,0:T(8,128)(2,1)S(1)}, u32[]{:S(2)}, u32[]{:S(2)}) collective-permute-start(bf16[512,256]{1,0:T(8,128)(2,1)S(1)} %collective-permute-done.20.refs_4_), channel_id=1, source_target_pairs={{0,1},{1,0},{2,3},{3,2},{4,5},{5,4},{6,7},{7,6},{8,9},{9,8},{10,11... | collective-permute-start | bytes 786440 | tf_op jit(solution)/shard_map/ppermute | solution.py:300
  88.5 1.5 %collective-permute-start.28 = (bf16[512,256]{1,0:T(8,128)(2,1)S(1)}, bf16[512,256]{1,0:T(8,128)(2,1)S(1)}, u32[]{:S(2)}, u32[]{:S(2)}) collective-permute-start(bf16[512,256]{1,0:T(8,128)(2,1)S(1)} %collective-permute-done.25.refs_3_), channel_id=1, source_target_pairs={{0,1},{1,0},{2,3},{3,2},{4,5},{5,4},{6,7},{7,6},{8,9},{9,8},{10,11... | collective-permute-start | bytes 786440 | tf_op jit(solution)/shard_map/ppermute | solution.py:300
  88.5 5.8 %collective-permute-start.23 = (bf16[64,512]{1,0:T(8,128)(2,1)S(1)}, bf16[64,512]{1,0:T(8,128)(2,1)S(1)}, u32[]{:S(2)}, u32[]{:S(2)}) collective-permute-start(bf16[64,512]{1,0:T(8,128)(2,1)S(1)} %fusion.12), channel_id=1, source_target_pairs={{0,6},{1,7},{2,4},{3,5},{4,2},{5,3},{6,0},{7,1},{8,14},{9,15},{10,... | collective-permute-start | bytes 196616 | tf_op jit(solution)/shard_map/ppermute | solution.py:321
  89.1 5.6 %collective-permute-start.31 = (bf16[512,256]{1,0:T(8,128)(2,1)S(1)}, bf16[512,256]{1,0:T(8,128)(2,1)S(1)}, u32[]{:S(2)}, u32[]{:S(2)}) collective-permute-start(bf16[512,256]{1,0:T(8,128)(2,1)S(1)} %collective-permute-done.16.refs_6_), channel_id=1, source_target_pairs={{0,1},{1,0},{2,3},{3,2},{4,5},{5,4},{6,7},{7,6},{8,9},{9,8},{10,11... | collective-permute-start | bytes 786440 | tf_op jit(solution)/shard_map/ppermute | solution.py:300
  89.2 5.1 %collective-permute-start.30 = (bf16[512,256]{1,0:T(8,128)(2,1)S(1)}, bf16[512,256]{1,0:T(8,128)(2,1)S(1)}, u32[]{:S(2)}, u32[]{:S(2)}) collective-permute-start(bf16[512,256]{1,0:T(8,128)(2,1)S(1)} %collective-permute-done.26.refs_5_), channel_id=1, source_target_pairs={{0,1},{1,0},{2,3},{3,2},{4,5},{5,4},{6,7},{7,6},{8,9},{9,8},{10,11... | collective-permute-start | bytes 786440 | tf_op jit(solution)/shard_map/ppermute | solution.py:300
  90.0 4.7 %collective-permute-start.32 = (bf16[512,256]{1,0:T(8,128)(2,1)S(1)}, bf16[512,256]{1,0:T(8,128)(2,1)S(1)}, u32[]{:S(2)}, u32[]{:S(2)}) collective-permute-start(bf16[512,256]{1,0:T(8,128)(2,1)S(1)} %collective-permute-done.19.refs_7_), channel_id=1, source_target_pairs={{0,1},{1,0},{2,3},{3,2},{4,5},{5,4},{6,7},{7,6},{8,9},{9,8},{10,11... | collective-permute-start | bytes 786440 | tf_op jit(solution)/shard_map/ppermute | solution.py:300
  90.1 4.6 %collective-permute-start.33 = (bf16[512,256]{1,0:T(8,128)(2,1)S(1)}, bf16[512,256]{1,0:T(8,128)(2,1)S(1)}, u32[]{:S(2)}, u32[]{:S(2)}) collective-permute-start(bf16[512,256]{1,0:T(8,128)(2,1)S(1)} %collective-permute-done.21.refs_8_), channel_id=1, source_target_pairs={{0,1},{1,0},{2,3},{3,2},{4,5},{5,4},{6,7},{7,6},{8,9},{9,8},{10,11... | collective-permute-start | bytes 786440 | tf_op jit(solution)/shard_map/ppermute | solution.py:300
  94.3 1.5 %collective-permute-start.34 = (bf16[512,256]{1,0:T(8,128)(2,1)S(1)}, bf16[512,256]{1,0:T(8,128)(2,1)S(1)}, u32[]{:S(2)}, u32[]{:S(2)}) collective-permute-start(bf16[512,256]{1,0:T(8,128)(2,1)S(1)} %collective-permute-done.22.refs_9_), channel_id=1, source_target_pairs={{0,1},{1,0},{2,3},{3,2},{4,5},{5,4},{6,7},{7,6},{8,9},{9,8},{10,11... | collective-permute-start | bytes 786440 | tf_op jit(solution)/shard_map/ppermute | solution.py:300
  94.4 5.5 %collective-permute-start.24 = (bf16[64,512]{1,0:T(8,128)(2,1)S(1)}, bf16[64,512]{1,0:T(8,128)(2,1)S(1)}, u32[]{:S(2)}, u32[]{:S(2)}) collective-permute-start(bf16[64,512]{1,0:T(8,128)(2,1)S(1)} %fusion.11), channel_id=1, source_target_pairs={{0,8},{1,9},{2,10},{3,11},{4,12},{5,13},{6,14},{7,15},{8,0},{9,1},... | collective-permute-start | bytes 196616 | tf_op jit(solution)/shard_map/ppermute | solution.py:339
  99.9 6.9 %collective-permute-start.35 = (bf16[64,512]{1,0:T(8,128)(2,1)S(1)}, bf16[64,512]{1,0:T(8,128)(2,1)S(1)}, u32[]{:S(2)}, u32[]{:S(2)}) collective-permute-start(bf16[64,512]{1,0:T(8,128)(2,1)S(1)} %convert_element_type.160), channel_id=1, source_target_pairs={{0,64},{16,80},{32,96},{48,112},{64,0},{80,16},{96,32},{112,48},{1... | collective-permute-start | bytes 196616 | tf_op jit(solution)/shard_map/ppermute | solution.py:339
  101.8 9.5 %collective-permute-start.37 = (bf16[512,256]{1,0:T(8,128)(2,1)S(1)}, bf16[512,256]{1,0:T(8,128)(2,1)S(1)}, u32[]{:S(2)}, u32[]{:S(2)}) collective-permute-start(bf16[512,256]{1,0:T(8,128)(2,1)S(1)} %get-tuple-element.75), channel_id=1, source_target_pairs={{0,16},{16,32},{32,48},{48,0},{64,80},{80,96},{96,112},{112,64},{1... | collective-permute-start | bytes 786440 | tf_op jit(solution)/shard_map/ppermute | solution.py:219
  101.8 9.5 %collective-permute-start.38 = (bf16[512,256]{1,0:T(8,128)(2,1)S(1)}, bf16[512,256]{1,0:T(8,128)(2,1)S(1)}, u32[]{:S(2)}, u32[]{:S(2)}) collective-permute-start(bf16[512,256]{1,0:T(8,128)(2,1)S(1)} %get-tuple-element.77), channel_id=1, source_target_pairs={{0,48},{16,0},{32,16},{48,32},{64,112},{80,64},{96,80},{112,96},{1... | collective-permute-start | bytes 786440 | tf_op jit(solution)/shard_map/ppermute | solution.py:220
  105.1 8.1 %collective-permute-start.39 = (bf16[512,256]{1,0:T(8,128)(2,1)S(1)}, bf16[512,256]{1,0:T(8,128)(2,1)S(1)}, u32[]{:S(2)}, u32[]{:S(2)}) collective-permute-start(bf16[512,256]{1,0:T(8,128)(2,1)S(1)} %get-tuple-element.76), channel_id=1, source_target_pairs={{0,64},{16,80},{32,96},{48,112},{64,0},{80,16},{96,32},{112,48},{1... | collective-permute-start | bytes 786440 | tf_op jit(solution)/shard_map/ppermute | solution.py:221
  106.8 4.6 %collective-permute-start.36 = (bf16[64,512]{1,0:T(8,128)(2,1)S(1)}, bf16[64,512]{1,0:T(8,128)(2,1)S(1)}, u32[]{:S(2)}, u32[]{:S(2)}) collective-permute-start(bf16[64,512]{1,0:T(8,128)(2,1)S(1)} %fusion.10), channel_id=1, source_target_pairs={{0,16},{16,0},{32,48},{48,32},{64,80},{80,64},{96,112},{112,96},{1... | collective-permute-start | bytes 196616 | tf_op jit(solution)/shard_map/ppermute | solution.py:339
  113.2 5.6 %collective-permute-start.40 = (bf16[64,512]{1,0:T(8,128)(2,1)S(1)}, bf16[64,512]{1,0:T(8,128)(2,1)S(1)}, u32[]{:S(2)}, u32[]{:S(2)}) collective-permute-start(bf16[64,512]{1,0:T(8,128)(2,1)S(1)} %convert_element_type.164), channel_id=1, source_target_pairs={{0,48},{16,32},{32,16},{48,0},{64,112},{80,96},{96,80},{112,64},{1... | collective-permute-start | bytes 196616 | tf_op jit(solution)/shard_map/ppermute | solution.py:339
  113.5 16.7 %collective-permute-start.44 = (bf16[512,256]{1,0:T(8,128)(2,1)S(1)}, bf16[512,256]{1,0:T(8,128)(2,1)S(1)}, u32[]{:S(2)}, u32[]{:S(2)}) collective-permute-start(bf16[512,256]{1,0:T(8,128)(2,1)S(1)} %get-tuple-element.80), channel_id=1, source_target_pairs={{0,16},{16,32},{32,48},{48,0},{64,80},{80,96},{96,112},{112,64},{1... | collective-permute-start | bytes 786440 | tf_op jit(solution)/shard_map/ppermute | solution.py:222
  113.6 16.7 %collective-permute-start.45 = (bf16[512,256]{1,0:T(8,128)(2,1)S(1)}, bf16[512,256]{1,0:T(8,128)(2,1)S(1)}, u32[]{:S(2)}, u32[]{:S(2)}) collective-permute-start(bf16[512,256]{1,0:T(8,128)(2,1)S(1)} %get-tuple-element.82), channel_id=1, source_target_pairs={{0,48},{16,0},{32,16},{48,32},{64,112},{80,64},{96,80},{112,96},{1... | collective-permute-start | bytes 786440 | tf_op jit(solution)/shard_map/ppermute | solution.py:223
  118.8 5.6 %collective-permute-start.41 = (bf16[64,512]{1,0:T(8,128)(2,1)S(1)}, bf16[64,512]{1,0:T(8,128)(2,1)S(1)}, u32[]{:S(2)}, u32[]{:S(2)}) collective-permute-start(bf16[64,512]{1,0:T(8,128)(2,1)S(1)} %add_convert_fusion.5), channel_id=1, source_target_pairs={{0,6},{1,7},{2,4},{3,5},{4,2},{5,3},{6,0},{7,1},{8,14},{9,15},{10,... | collective-permute-start | bytes 196616 | tf_op jit(solution)/shard_map/ppermute | solution.py:324
  120.1 10.1 %collective-permute-start.46 = (bf16[512,256]{1,0:T(8,128)(2,1)S(1)}, bf16[512,256]{1,0:T(8,128)(2,1)S(1)}, u32[]{:S(2)}, u32[]{:S(2)}) collective-permute-start(bf16[512,256]{1,0:T(8,128)(2,1)S(1)} %add_convert_fusion.1), channel_id=1, source_target_pairs={{0,32},{16,48},{32,0},{48,16},{64,96},{80,112},{96,64},{112,80},{1... | collective-permute-start | bytes 786440 | tf_op jit(solution)/shard_map/ppermute | solution.py:226
  124.6 5.0 %collective-permute-start.42 = (bf16[128,512]{1,0:T(8,128)(2,1)S(1)}, bf16[128,512]{1,0:T(8,128)(2,1)S(1)}, u32[]{:S(2)}, u32[]{:S(2)}) collective-permute-start(bf16[128,512]{1,0:T(8,128)(2,1)S(1)} %fusion.8), channel_id=1, source_target_pairs={{0,2},{1,3},{2,0},{3,1},{4,6},{5,7},{6,4},{7,5},{8,10},{9,11},{10,... | collective-permute-start | bytes 393224 | tf_op jit(solution)/shard_map/ppermute | solution.py:324
  124.8 8.0 %collective-permute-start.47 = (bf16[512,256]{1,0:T(8,128)(2,1)S(1)}, bf16[512,256]{1,0:T(8,128)(2,1)S(1)}, u32[]{:S(2)}, u32[]{:S(2)}) collective-permute-start(bf16[512,256]{1,0:T(8,128)(2,1)S(1)} %add_convert_fusion), channel_id=1, source_target_pairs={{0,64},{16,80},{32,96},{48,112},{64,0},{80,16},{96,32},{112,48},{1... | collective-permute-start | bytes 786440 | tf_op jit(solution)/shard_map/ppermute | solution.py:227
  130.1 3.5 %collective-permute-start.43 = (bf16[256,512]{1,0:T(8,128)(2,1)S(1)}, bf16[256,512]{1,0:T(8,128)(2,1)S(1)}, u32[]{:S(2)}, u32[]{:S(2)}) collective-permute-start(bf16[256,512]{1,0:T(8,128)(2,1)S(1)} %fusion.5), channel_id=1, source_target_pairs={{0,1},{1,0},{2,3},{3,2},{4,5},{5,4},{6,7},{7,6},{8,9},{9,8},{10,11... | collective-permute-start | bytes 786440 | tf_op jit(solution)/shard_map/ppermute | solution.py:324
  (3 other events, 117.4 us)
